TPU v7x, 512 devices: a whole 4x8x8 slice. The times are simulated.
512 devices in a mesh: dp: 16 (over y, core), lat: 32 (over z, x).
Axes of the slice: x: 4, y: 8, z: 8, core: 2. Of those that a mesh axis runs over, the one named last changes fastest.
Arguments:
- fields: bfloat16 [16, 96, 180, 768], P('dp', 'lat'), may hold values from -6 to 6
- cotangent: bfloat16 [16, 96, 180, 768], P('dp', 'lat'), may hold values from -6 to 6
- w_first: bfloat16 [2, 8, 96, 96], replicated, may hold values from -0.4375 to 0.4375
- b_first: float32 [2, 768], replicated, may hold values from -3 to 3
- w_second: bfloat16 [2, 8, 96, 96], replicated, may hold values from -0.4375 to 0.4375
- b_second: float32 [2, 768], replicated, may hold values from -3 to 3
Outputs:
- output: bfloat16 [16, 96, 180, 768], P('dp', 'lat')
- grad_fields: bfloat16 [16, 96, 180, 768], P('dp', 'lat')
- grad_w_first: float32 [2, 8, 96, 96], replicated
- grad_b_first: float32 [2, 768], replicated
- grad_w_second: float32 [2, 8, 96, 96], replicated
- grad_b_second: float32 [2, 768], replicated
All inputs are finite; a program needn't handle non-finite values.
Results may differ from a plain program's by a relative error of at most 0.015.
Values may be sent and summed in bfloat16 or wider, within the bound.
No kernel may reach another device: no remote copies, remote signals or barrier semaphores. Data moves between devices by JAX's collectives and lax.ppermute only.
A program may use at most 64 MiB of HBM per device.

v0:
```python
from functools import partial
import math

import jax
import jax.numpy as jnp
from jax import lax
from jax.sharding import PartitionSpec as P

C = 768
NB = 8
BS = 96
H = 96
W = 180
KX = 64


EPSILON = 1e-06


def layer_norm(values):
    centered = values - jnp.mean(values, axis=-1, keepdims=True)
    spread = jnp.mean(centered * centered, axis=-1, keepdims=True)
    return centered / jnp.sqrt(spread + EPSILON)


def angles(count_left, count_right, period):
    left_index = jnp.arange(count_left, dtype=jnp.int32)[:, None]
    right_index = jnp.arange(count_right, dtype=jnp.int32)[None, :]
    return 2.0 * math.pi / period * (left_index * right_index % period).astype(jnp.float32)


def longitude_tables(mode_count):
    angle_grid = angles(W, mode_count, W)
    mode_index = jnp.arange(mode_count, dtype=jnp.int32)[None, :]
    live_modes = jnp.where(mode_index <= W // 2, 1.0, 0.0).astype(jnp.float32) / math.sqrt(W)
    weight = jnp.where(mode_index == 0, 1.0, 2.0).astype(jnp.float32) * live_modes
    forward = jnp.stack(
        [jnp.cos(angle_grid) * live_modes, -jnp.sin(angle_grid) * live_modes], axis=2
    )
    inverse = jnp.stack([jnp.cos(angle_grid) * weight, -jnp.sin(angle_grid) * weight], axis=2)
    return (forward.astype(jnp.bfloat16), inverse.astype(jnp.bfloat16))


def latitude_table():
    angle_grid = angles(H, H, H)
    cosine = jnp.cos(angle_grid) / math.sqrt(H)
    sine_part = jnp.sin(angle_grid) / math.sqrt(H)
    real_row = jnp.stack([cosine, sine_part], axis=2)
    imag_row = jnp.stack([-sine_part, cosine], axis=2)
    return jnp.stack([real_row, imag_row], axis=1).astype(jnp.bfloat16)


def real_form(weight):
    real_part = weight[0]
    imag_part = weight[1]
    upper_rows = jnp.stack([real_part, imag_part], axis=2)
    lower_rows = jnp.stack([-imag_part, real_part], axis=2)
    return jnp.stack([upper_rows, lower_rows], axis=1)


def fold_grads(gathered):
    real_grad = gathered[:, 0, :, 0, :] + gathered[:, 1, :, 1, :]
    imag_grad = gathered[:, 0, :, 1, :] - gathered[:, 1, :, 0, :]
    return jnp.stack([real_grad, imag_grad], axis=0)


def product(pattern, left_side, right_side):
    return jnp.einsum(pattern, left_side, right_side, preferred_element_type=jnp.float32)


def spectral_forward(spectra_modes, first_form, bias_one, second_form, bias_two):
    leading = spectra_modes.shape[:3]
    blocked = spectra_modes.reshape(leading + (2, NB, BS))
    pre_one = (
        product("bmkqni,nqipo->bmkpno", blocked, first_form).reshape(leading + (2, C)) + bias_one
    )
    hidden = jax.nn.gelu(pre_one, approximate=False).astype(jnp.bfloat16)
    pre_two = (
        product("bmkqni,nqipo->bmkpno", hidden.reshape(leading + (2, NB, BS)), second_form).reshape(
            leading + (2, C)
        )
        + bias_two
    )
    return (pre_one, hidden, pre_two)


def spectral_backward(spectra_modes, pre_one, hidden, first_form, second_form, back_filtered):
    leading = spectra_modes.shape[:3]
    back_blocked = back_filtered.reshape(leading + (2, NB, BS))
    grad_second = product(
        "bmkqni,bmkpno->nqipo", hidden.reshape(leading + (2, NB, BS)), back_blocked
    )
    bias_two_grad = jnp.sum(back_filtered.astype(jnp.float32), axis=(0, 1, 2))
    back_hidden = product("bmkpno,nqipo->bmkqni", back_blocked, second_form).reshape(
        leading + (2, C)
    )
    unused, gelu_back = jax.vjp(partial(jax.nn.gelu, approximate=False), pre_one)
    back_pre = gelu_back(back_hidden)[0].astype(jnp.bfloat16)
    pre_blocked = back_pre.reshape(leading + (2, NB, BS))
    grad_first = product(
        "bmkqni,bmkpno->nqipo", spectra_modes.reshape(leading + (2, NB, BS)), pre_blocked
    )
    bias_one_grad = jnp.sum(back_pre.astype(jnp.float32), axis=(0, 1, 2))
    back_modes = (
        product("bmkpno,nqipo->bmkqni", pre_blocked, first_form)
        .reshape(leading + (2, C))
        .astype(jnp.bfloat16)
    )
    return (
        fold_grads(grad_first),
        bias_one_grad,
        fold_grads(grad_second),
        bias_two_grad,
        back_modes,
    )


def on_device(fields, cotangent, w_first, b_first, w_second, b_second):
    band_count = lax.axis_size("lat")
    mode_count = (W // 2 + band_count) // band_count * band_count
    local_modes = mode_count // band_count
    mode_index = lax.axis_index("lat") * local_modes + jnp.arange(local_modes, dtype=jnp.int32)
    mode_mask = (
        jnp.where(mode_index < KX, 1.0, 0.0).astype(jnp.float32).reshape(1, 1, local_modes, 1, 1)
    )
    forward_lon, inverse_lon = longitude_tables(mode_count)
    latitude = latitude_table()
    first_form = real_form(w_first)
    second_form = real_form(w_second)
    values = fields.astype(jnp.float32)
    normed, norm_back = jax.vjp(layer_norm, values)
    spectra = product("bhwc,wkp->bhkpc", normed.astype(jnp.bfloat16), forward_lon).astype(
        jnp.bfloat16
    )
    column_spectra = lax.all_to_all(spectra, "lat", split_axis=2, concat_axis=1, tiled=True)
    spectra_modes = product("mqhp,bhkpc->bmkqc", latitude, column_spectra).astype(jnp.bfloat16)
    pre_one, hidden, pre_two = spectral_forward(
        spectra_modes, first_form, b_first, second_form, b_second
    )
    filtered = (pre_two * mode_mask).astype(jnp.bfloat16)
    column_rows = product("mphq,bmkpc->bhkqc", latitude, filtered).astype(jnp.bfloat16)
    row_spectra = lax.all_to_all(column_rows, "lat", split_axis=1, concat_axis=2, tiled=True)
    mixed = product("bhkpc,wkp->bhwc", row_spectra, inverse_lon)
    result = (values + normed + mixed).astype(jnp.bfloat16)
    upstream = cotangent.astype(jnp.float32)
    back_rows = product("bhwc,wkp->bhkpc", cotangent, inverse_lon).astype(jnp.bfloat16)
    back_columns = lax.all_to_all(back_rows, "lat", split_axis=2, concat_axis=1, tiled=True)
    back_filtered = (product("mphq,bhkqc->bmkpc", latitude, back_columns) * mode_mask).astype(
        jnp.bfloat16
    )
    grad_one, bias_one, grad_two, bias_two, back_modes = spectral_backward(
        spectra_modes, pre_one, hidden, first_form, second_form, back_filtered
    )
    back_column_rows = product("mqhp,bmkqc->bhkpc", latitude, back_modes).astype(jnp.bfloat16)
    back_spectra = lax.all_to_all(back_column_rows, "lat", split_axis=1, concat_axis=2, tiled=True)
    back_normed = upstream + product("bhkpc,wkp->bhwc", back_spectra, forward_lon)
    back_fields = (upstream + norm_back(back_normed)[0]).astype(jnp.bfloat16)
    grad_scale = 1.0 / (fields.shape[0] * lax.axis_size("dp") * H)
    members = (grad_one, bias_one, grad_two, bias_two)
    packed = jnp.concatenate([member.reshape(-1) for member in members]) * grad_scale
    all_grads = lax.psum(packed, ("dp", "lat"))
    results = []
    offset = 0
    for member in members:
        length = member.size
        results.append(all_grads[offset : offset + length].reshape(member.shape))
        offset = offset + length
    return (result, back_fields, results[0], results[1], results[2], results[3])


def solution(mesh):
    placed = (P("dp", "lat", None, None), P("dp", "lat", None, None), P(), P(), P(), P())
    return jax.shard_map(
        on_device,
        mesh=mesh,
        in_specs=placed,
        out_specs=(P("dp", "lat", None, None), P("dp", "lat", None, None), P(), P(), P(), P()),
        check_vma=False,
    )
```

profile of v0, /device:TPU:1, one launch (start us, length us, event | category | flops | bytes accessed | tf_op | source)
XLA Modules:
  0.0 435.8 jit_solution(13082725453070378187)
XLA Ops:
  14.1 1.8 copy.151
  16.0 13.7 %all-to-all-start = ((bf16[1,3,96,2,768]{4,3,1,0,2:T(2,128)(2,1)}), bf16[1,3,96,2,768]{4,3,1,0,2:T(2,128)(2,1)S(1)}, u32[]{:S(2)}, u32[]{:S(2)}) async-start(bf16[1,3,96,2,768]{4,3,1,0,2:T(2,128)(2,1)} %copy.151), calls=%async_computation | async-start | bytes 1769472 | tf_op jit(solution)/shard_map/all_to_all | solution.py:135
  31.2 1.8 copy.163
  33.1 19.5 %all-to-all-done = bf16[1,3,96,2,768]{4,3,1,0,2:T(2,128)(2,1)S(1)} async-done(((bf16[1,3,96,2,768]{4,3,1,0,2:T(2,128)(2,1)}), bf16[1,3,96,2,768]{4,3,1,0,2:T(2,128)(2,1)S(1)}, u32[]{:S(2)}, u32[]{:S(2)}) %all-to-all-start) | async-done | bytes 884768 | tf_op jit(solution)/shard_map/all_to_all | solution.py:135
  52.6 6.1 %all-to-all-start.2 = ((bf16[1,3,96,2,768]{4,3,1,0,2:T(2,128)(2,1)}), bf16[1,3,96,2,768]{4,3,1,0,2:T(2,128)(2,1)S(1)}, u32[]{:S(2)}, u32[]{:S(2)}) async-start(bf16[1,3,96,2,768]{4,3,1,0,2:T(2,128)(2,1)} %copy.163), calls=%async_computation.2 | async-start | bytes 1769472 | tf_op jit(solution)/shard_map/all_to_all | solution.py:147
  67.7 2.2 reshape.652
  69.9 10.8 %all-to-all-done.2 = bf16[1,3,96,2,768]{4,3,1,0,2:T(2,128)(2,1)S(1)} async-done(((bf16[1,3,96,2,768]{4,3,1,0,2:T(2,128)(2,1)}), bf16[1,3,96,2,768]{4,3,1,0,2:T(2,128)(2,1)S(1)}, u32[]{:S(2)}, u32[]{:S(2)}) %all-to-all-start.2) | async-done | bytes 884768 | tf_op jit(solution)/shard_map/all_to_all | solution.py:147
  83.4 2.4 reshape.658
  85.8 6.8 %fusion.5 = (f32[96,3,2,8,96]{4,0,1,2,3:T(8,128)S(1)}, f32[8,2,96,96,3,1]{2,3,5,4,1,0:T(8,128)S(1)}) fusion(f32[2,8,96]{2,0,1:T(2,128)S(1)} %copy-done.23, bf16[96,3,2,8,96,1]{4,3,0,2,1,5:T(8,128)(2,1)} %bitcast.367, bf16[8,1,96,2,96]{4,2,1,3,0:T(8,128)(2,1)S(1)} %copy-done.13, bf16[8,1,96,2,96]{4,2,1,3,0:T(8,128)(2,1)S(1)} %copy-done.11), kind=kOutput, calls=%fused_computation.11 | convolution fusion | flops 198918144 | bytes 5019648 | tf_op jit(solution)/shard_map/bmkqni,nqipo->bmkpno/dot_general | solution.py:68
  94.4 8.0 %convert_reduce_fusion.1 = (f32[2,8,96]{2,0,1:T(2,128)}, bf16[1,96,3,2,8,96]{5,1,2,3,4,0:T(8,128)(2,1)}, f32[1,96,3,2,8,96]{5,1,2,3,4,0:T(8,128)}, f32[8,2,96,96,3,1]{2,3,5,4,1,0:T(8,128)S(1)}) fusion(f32[2,8,96]{2,0,1:T(2,128)S(1)} %copy-done.23, f32[8,2,96,96,3,1]{2,3,5,4,1,0:T(8,128)S(1)} %get-tuple-element.35, ...), kind=kOutput, calls=%fused_computation.34 | convolution fusion | flops 203340288 | bytes 7680000 | tf_op jit(solution)/shard_map/bmkpno,nqipo->bmkqni/dot_general | solution.py:68
  107.8 3.2 convolution_bitcast_fusion
  111.0 2.0 copy.158
  113.0 2.1 reshape.654
  115.6 1.8 copy.160
  118.1 6.6 %all-to-all-start.1 = ((bf16[1,96,3,2,768]{4,3,2,0,1:T(2,128)(2,1)}), bf16[1,96,3,2,768]{4,3,2,0,1:T(2,128)(2,1)S(1)}, u32[]{:S(2)}, u32[]{:S(2)}) async-start(bf16[1,96,3,2,768]{4,3,2,0,1:T(2,128)(2,1)} %copy.160), calls=%async_computation.1 | async-start | bytes 1769472 | tf_op jit(solution)/shard_map/all_to_all | solution.py:142
  127.2 2.3 maximum_multiply_fusion
  129.6 2.9 fusion.39
  134.3 1.9 reshape.694
  137.8 1.8 copy.173
  139.7 6.8 %all-to-all-done.1 = bf16[1,96,3,2,768]{4,3,2,0,1:T(2,128)(2,1)S(1)} async-done(((bf16[1,96,3,2,768]{4,3,2,0,1:T(2,128)(2,1)}), bf16[1,96,3,2,768]{4,3,2,0,1:T(2,128)(2,1)S(1)}, u32[]{:S(2)}, u32[]{:S(2)}) %all-to-all-start.1) | async-done | bytes 884768 | tf_op jit(solution)/shard_map/all_to_all | solution.py:142
  146.5 6.9 %all-to-all-start.3 = ((bf16[1,96,3,2,768]{4,3,2,0,1:T(2,128)(2,1)}), bf16[1,96,3,2,768]{4,3,2,0,1:T(2,128)(2,1)}, u32[]{:S(2)}, u32[]{:S(2)}) async-start(bf16[1,96,3,2,768]{4,3,2,0,1:T(2,128)(2,1)} %copy.173), calls=%async_computation.3 | async-start | bytes 1769472 | tf_op jit(solution)/shard_map/all_to_all | solution.py:155
  153.4 261.3 %all-reduce.2.cloned.1.call-done = f32[297984]{0:T(1024)} async-done(((f32[297984]{0:T(1024)}), f32[297984]{0:T(1024)}) %all-reduce.2.cloned.1.call-update) | async-done | bytes 1191952 | tf_op jit(solution)/shard_map/psum | solution.py:161
  414.7 2.1 fusion.121
  418.8 2.2 reshape.668
  (127 shorter events, 43.8 us)
Async XLA Ops:
  14.1 16.7 %copy-start.2 = (bf16[1,3,180,768]{3,2,1,0:T(8,128)(2,1)S(1)}, bf16[1,3,180,768]{3,2,1,0:T(8,128)(2,1)}, u32[]{:S(2)}) copy-start(bf16[1,3,180,768]{3,2,1,0:T(8,128)(2,1)} %param.7) | copy-start | bytes 2488324
  16.0 36.7 %all-to-all-start = ((bf16[1,3,96,2,768]{4,3,1,0,2:T(2,128)(2,1)}), bf16[1,3,96,2,768]{4,3,1,0,2:T(2,128)(2,1)S(1)}, u32[]{:S(2)}, u32[]{:S(2)}) async-start(bf16[1,3,96,2,768]{4,3,1,0,2:T(2,128)(2,1)} %copy.151), calls=%async_computation | async-start | bytes 1769472 | tf_op jit(solution)/shard_map/all_to_all | solution.py:135
  31.2 28.6 %copy-start.30 = (f32[2,768]{1,0:T(2,128)S(1)}, f32[2,768]{1,0:T(2,128)}, u32[]{:S(2)}) copy-start(f32[2,768]{1,0:T(2,128)} %param.9) | copy-start | bytes 18436
  52.6 28.1 %all-to-all-start.2 = ((bf16[1,3,96,2,768]{4,3,1,0,2:T(2,128)(2,1)}), bf16[1,3,96,2,768]{4,3,1,0,2:T(2,128)(2,1)S(1)}, u32[]{:S(2)}, u32[]{:S(2)}) async-start(bf16[1,3,96,2,768]{4,3,1,0,2:T(2,128)(2,1)} %copy.163), calls=%async_computation.2 | async-start | bytes 1769472 | tf_op jit(solution)/shard_map/all_to_all | solution.py:147
  61.8 53.3 %copy-start.9 = (bf16[96,1,96,2]{2,0,3,1:T(8,128)(2,1)}, bf16[96,1,96,2]{2,0,3,1:T(8,128)(2,1)S(1)}, u32[]{:S(2)}) copy-start(bf16[96,1,96,2]{2,0,3,1:T(8,128)(2,1)S(1)} %get-tuple-element.22) | copy-start | bytes 110596
  62.8 31.5 %copy-start.4 = (bf16[8,1,96,2,96]{2,4,1,3,0:T(8,128)(2,1)}, bf16[8,1,96,2,96]{2,4,1,3,0:T(8,128)(2,1)S(1)}, u32[]{:S(2)}) copy-start(bf16[8,1,96,2,96]{2,4,1,3,0:T(8,128)(2,1)S(1)} %get-tuple-element.19) | copy-start | bytes 884740
  67.6 14.3 %copy-start.32 = (f32[3]{0:T(128)S(1)}, f32[3]{0:T(128)}, u32[]{:S(2)}) copy-start(f32[3]{0:T(128)} %compare_select_fusion) | copy-start | bytes 40
  82.0 3.8 copy-start.11
  82.0 3.8 copy-start.13
  82.0 3.8 copy-start.23
  92.6 9.9 %copy-start.1 = (f32[8,2,96,96,3,1]{2,3,5,4,1,0:T(8,128)}, f32[8,2,96,96,3,1]{2,3,5,4,1,0:T(8,128)S(1)}, u32[]{:S(2)}) copy-start(f32[8,2,96,96,3,1]{2,3,5,4,1,0:T(8,128)S(1)} %get-tuple-element.35) | copy-start | bytes 5308420
  94.4 8.0 %copy-start.8 = (bf16[96,3,2,8,96]{4,3,0,2,1:T(8,128)(2,1)S(1)}, bf16[96,3,2,8,96]{4,3,0,2,1:T(8,128)(2,1)}, u32[]{:S(2)}) copy-start(bf16[96,3,2,8,96]{4,3,0,2,1:T(8,128)(2,1)} %reshape.652) | copy-start | bytes 2654212
  115.6 9.2 %copy-start.6 = (f32[1,8,96,96]{3,2,1,0:T(8,128)S(1)}, f32[1,8,96,96]{3,2,1,0:T(8,128)}, u32[]{:S(2)}) copy-start(f32[1,8,96,96]{3,2,1,0:T(8,128)} %fusion.84) | copy-start | bytes 884740
  118.1 9.1 %copy-start.3 = (f32[147456]{0:T(1024)S(1)}, f32[147456]{0:T(1024)}, u32[]{:S(2)}) copy-start(f32[147456]{0:T(1024)} %reshape.665) | copy-start | bytes 1769476
  118.1 28.3 %all-to-all-start.1 = ((bf16[1,96,3,2,768]{4,3,2,0,1:T(2,128)(2,1)}), bf16[1,96,3,2,768]{4,3,2,0,1:T(2,128)(2,1)S(1)}, u32[]{:S(2)}, u32[]{:S(2)}) async-start(bf16[1,96,3,2,768]{4,3,2,0,1:T(2,128)(2,1)} %copy.160), calls=%async_computation.1 | async-start | bytes 1769472 | tf_op jit(solution)/shard_map/all_to_all | solution.py:142
  124.8 289.9 %all-reduce.2.cloned.1.call-start = ((), (), s32[]{:S(2)}) async-start(), calls=%async_computation.4 | async-start | bytes 2383872 | tf_op jit(solution)/shard_map/psum | solution.py:161
  125.9 3.6 copy-start.12
  132.5 3.7 copy-start.10
  146.5 277.8 %all-to-all-start.3 = ((bf16[1,96,3,2,768]{4,3,2,0,1:T(2,128)(2,1)}), bf16[1,96,3,2,768]{4,3,2,0,1:T(2,128)(2,1)}, u32[]{:S(2)}, u32[]{:S(2)}) async-start(bf16[1,96,3,2,768]{4,3,2,0,1:T(2,128)(2,1)} %copy.173), calls=%async_computation.3 | async-start | bytes 1769472 | tf_op jit(solution)/shard_map/all_to_all | solution.py:155
  416.8 5.9 %copy-start = (bf16[1,3,180,768]{3,2,1,0:T(8,128)(2,1)S(1)}, bf16[1,3,180,768]{3,2,1,0:T(8,128)(2,1)}, u32[]{:S(2)}) copy-start(bf16[1,3,180,768]{3,2,1,0:T(8,128)(2,1)} %param.6) | copy-start | bytes 2488324
  416.8 5.9 %copy-start.20 = (bf16[180,96,1]{1,0,2:T(8,128)(2,1)S(1)}, bf16[180,96,1]{1,0,2:T(8,128)(2,1)}, u32[]{:S(2)}) copy-start(bf16[180,96,1]{1,0,2:T(8,128)(2,1)} %copy-done.19) | copy-start | bytes 103684
  416.8 5.9 %copy-start.22 = (bf16[180,96,1]{1,0,2:T(8,128)(2,1)S(1)}, bf16[180,96,1]{1,0,2:T(8,128)(2,1)}, u32[]{:S(2)}) copy-start(bf16[180,96,1]{1,0,2:T(8,128)(2,1)} %copy-done.21) | copy-start | bytes 103684
  416.8 5.9 %copy-start.25 = (f32[3,180]{1,0:T(4,128)S(1)}, f32[3,180]{1,0:T(4,128)}, u32[]{:S(2)}) copy-start(f32[3,180]{1,0:T(4,128)} %copy-done.24) | copy-start | bytes 6484
  422.8 3.2 copy-start.16
  (14 other events, 21.0 us)
Sparse Core Ops, SparseCore 0:
  130.7 283.9 all-reduce.1
where the time goes:
time: 437 us; the launch traced here: 436 us
  waiting for transfers between devices  298 us (68%)
  local copies, waits for them, and re-layouts  41 us (9%)
  starting transfers between devices  33.5 us (8%)
  matrix products  31.7 us (7%)
  other arithmetic  16.5 us (4%)
  between operations  14.6 us (3%)
    psum x1, waiting for transfers between devices, on_device(): all_grads = lax.psum(packed, ('dp', 'lat'))  261 us
    dot_general x14, matrix products, product(): jnp.einsum(pattern, left_side, right_side, preferred_element_type=jnp.flo...  31.7 us
    all_to_all x1, waiting for transfers between devices, on_device(): lax.all_to_all(spectra, 'lat', split_axis=2, concat_axis=1, tiled=True)  19.5 us
    all_to_all x1, starting transfers between devices, on_device(): lax.all_to_all(spectra, 'lat', split_axis=2, concat_axis=1, tiled=True)  13.7 us
    all_to_all x1, waiting for transfers between devices, on_device(): lax.all_to_all(back_rows, 'lat', split_axis=2, concat_axis=1, tiled=True)  10.8 us
  transfers between devices with their start and end apart: 5, of which 4 were waited for; matrix products, arithmetic and copies ran while one was open for 9% of the time, Pallas kernels for 0%

commit v1 on v0

v1 whole, which is shorter than its diff:
```python
import math

import jax
import jax.numpy as jnp
import numpy as np
from jax import lax
from jax.experimental import pallas as pl
from jax.experimental.pallas import tpu as pltpu
from jax.sharding import PartitionSpec as P

C = 768
NB = 8
BS = 96
H = 96
W = 180
KX = 64
SAMPLES = 16
EPSILON = 1e-06

BANDS = 32
GROUPS = 4
MODES = KX // GROUPS
ROWS = H // BANDS
WPAD = 192
PACK = 72
CHUNKS = 16
CHUNK_ROWS = 24
BF = jnp.bfloat16
F32 = jnp.float32
VMEM_LIMIT = 48 * 1024 * 1024


def tables():
    w_index = np.arange(W)[:, None]
    k_index = np.arange(KX)[None, :]
    lon = (2.0 * math.pi / W * (w_index * k_index % W)).astype(np.float64)
    fwd = np.stack([np.cos(lon), -np.sin(lon)], axis=1) / math.sqrt(W)
    weight = np.where(k_index == 0, 1.0, 2.0)[:, None, :]
    inv = fwd * weight
    def order(table):
        grouped = table.reshape(W, 2, GROUPS, MODES).transpose(0, 2, 1, 3).reshape(W, 2 * KX)
        padded = np.zeros((WPAD, 2 * KX))
        padded[:W] = grouped
        return padded

    h_index = np.arange(H)
    lat = 2.0 * math.pi / H * (h_index[:, None] * h_index[None, :] % H)
    cosine = np.cos(lat) / math.sqrt(H)
    sine = np.sin(lat) / math.sqrt(H)
    full = np.stack(
        [np.stack([cosine, sine], axis=2), np.stack([-sine, cosine], axis=2)], axis=0
    ).reshape(2 * H, 2 * H)
    return order(fwd), order(inv), full


LON_FWD, LON_INV, LAT = tables()


def lanes(shape):
    return lax.broadcasted_iota(jnp.int32, shape, 1)


def roll(value, shift):
    return pltpu.roll(value, shift % 128, 1)


def pack_tile(tile):
    lane = lanes((24, 128))
    tail = tile[72:96]
    return [
        jnp.where(lane < 96, tile[24 * i : 24 * i + 24], roll(tail, 96 - 32 * i))
        for i in range(3)
    ]


def unpack_tail(pieces):
    lane = lanes((24, 128))
    return jnp.where(
        lane < 32,
        roll(pieces[0], 32),
        jnp.where(lane < 64, roll(pieces[1], 64), roll(pieces[2], 96)),
    )


def block_lanes(value, block):
    start = BS * block
    first, shift = start // 128, start % 128
    head = value[:, 128 * first : 128 * first + 128]
    if shift == 0:
        return head
    head = roll(head, 128 - shift)
    if shift + BS <= 128:
        return head
    after = roll(value[:, 128 * first + 128 : 128 * first + 256], 128 - shift)
    return jnp.where(lanes(head.shape) < 128 - shift, head, after)


def join_lanes(parts):
    lane = lanes(parts[0].shape)
    return [
        jnp.where(lane < 96, parts[0], roll(parts[1], 96)),
        jnp.where(lane < 64, roll(parts[1], 96), roll(parts[2], 64)),
        jnp.where(lane < 32, roll(parts[2], 64), roll(parts[3], 32)),
    ]


ROW_CHUNKS = [(start, min(32, W - start)) for start in range(0, W, 32)]


def normalize(values):
    mean = jnp.sum(values, axis=-1, keepdims=True) * (1.0 / C)
    centered = values - mean
    spread = jnp.sum(centered * centered, axis=-1, keepdims=True) * (1.0 / C)
    scale = 1.0 / jnp.sqrt(spread + EPSILON)
    return centered * scale, scale


def send_packed(acc_ref, out_ref):
    for block in range(NB):
        rows = [block_lanes(acc_ref[r], block) for r in range(ROWS)]
        for group in range(GROUPS):
            tile = jnp.concatenate(
                [row[32 * group : 32 * group + 32] for row in rows], axis=0
            )
            pieces = pack_tile(tile)
            out_ref[block * GROUPS + group] = jnp.concatenate(pieces, axis=0).astype(BF)


def fields_kernel(x_ref, table_ref, out_ref, normed_ref, acc_ref):
    r = pl.program_id(0)

    @pl.when(r == 0)
    def _():
        normed_ref[...] = jnp.zeros_like(normed_ref)

    for start, size in ROW_CHUNKS:
        values = x_ref[0, 0, start : start + size].astype(F32)
        normed_ref[start : start + size] = normalize(values)[0].astype(BF)
    acc_ref[r] = jnp.dot(table_ref[...], normed_ref[...], preferred_element_type=F32)

    @pl.when(r == ROWS - 1)
    def _():
        send_packed(acc_ref, out_ref)


def cotangent_kernel(x_ref, table_ref, out_ref, padded_ref, acc_ref):
    r = pl.program_id(0)

    @pl.when(r == 0)
    def _():
        padded_ref[...] = jnp.zeros_like(padded_ref)

    padded_ref[0:W] = x_ref[0, 0]
    acc_ref[r] = jnp.dot(table_ref[...], padded_ref[...], preferred_element_type=F32)

    @pl.when(r == ROWS - 1)
    def _():
        send_packed(acc_ref, out_ref)


def to_spectra(kernel, name, array, table):
    return pl.pallas_call(
        kernel,
        name=name,
        grid=(ROWS,),
        in_specs=[
            pl.BlockSpec((1, 1, W, C), lambda r: (0, r, 0, 0)),
            pl.BlockSpec((2 * KX, WPAD), lambda r: (0, 0)),
        ],
        out_specs=pl.BlockSpec((BANDS, PACK, 128), lambda r: (0, 0, 0)),
        out_shape=jax.ShapeDtypeStruct((BANDS, PACK, 128), BF),
        scratch_shapes=[
            pltpu.VMEM((WPAD, C), BF),
            pltpu.VMEM((ROWS, 2 * KX, C), F32),
        ],
        compiler_params=pltpu.CompilerParams(vmem_limit_bytes=VMEM_LIMIT),
        cost_estimate=pl.CostEstimate(
            flops=2 * ROWS * W * 2 * KX * C, bytes_accessed=1500000, transcendentals=0
        ),
    )(array, table)


TILE_ROWS = 2 * ROWS * MODES


def unpack_bands(recv_ref, rows_ref):
    def one(s, carry):
        pieces = [
            recv_ref[s, 24 * i : 24 * i + 24, :].astype(F32) for i in range(3)
        ]
        base = pl.multiple_of(s * TILE_ROWS, TILE_ROWS)
        for i in range(3):
            rows_ref[pl.ds(base + 24 * i, 24), :] = pieces[i]
        rows_ref[pl.ds(base + 72, 24), :] = unpack_tail(pieces)
        return carry

    lax.fori_loop(0, BANDS, one, 0, unroll=4)


def pack_bands(rows_ref, out_ref):
    def one(s, carry):
        base = pl.multiple_of(s * TILE_ROWS, TILE_ROWS)
        pieces = pack_tile(rows_ref[pl.ds(base, TILE_ROWS), :])
        out_ref[s] = jnp.concatenate(pieces, axis=0).astype(BF)
        return carry

    lax.fori_loop(0, BANDS, one, 0, unroll=4)


def mode_rows(rows_ref, lat, pair):
    columns = jnp.concatenate(
        [
            rows_ref[pl.ds(2 * pair + j, 2 * H, stride=MODES), :].astype(BF)
            for j in range(2)
        ],
        axis=1,
    )
    done = jnp.dot(lat, columns, preferred_element_type=F32).astype(BF)
    return jnp.concatenate(
        [
            jnp.concatenate(
                [done[0:H, 128 * j : 128 * j + 128], done[H : 2 * H, 128 * j : 128 * j + 128]],
                axis=1,
            )
            for j in range(2)
        ],
        axis=0,
    )


def store_rows(rows_ref, lat, pair, modes):
    columns = jnp.concatenate(
        [
            jnp.concatenate(
                [modes[H * j : H * j + H, 0:128], modes[H * j : H * j + H, 128:256]], axis=0
            )
            for j in range(2)
        ],
        axis=1,
    )
    done = lax.dot_general(
        lat, columns, (((0,), (0,)), ((), ())), preferred_element_type=F32
    )
    for j in range(2):
        rows_ref[pl.ds(2 * pair + j, 2 * H, stride=MODES), :] = done[:, 128 * j : 128 * j + 128]


PAIR_ROWS = 2 * H
PAIRS = MODES // 2


def forward_kernel(
    recv_ref, lat_ref, w1_ref, b1_ref, w2_ref, b2_ref,
    out_ref, modes_ref, hidden_ref, slope_ref, rows_ref,
):
    unpack_bands(recv_ref, rows_ref)
    lat = lat_ref[...]
    w1 = w1_ref[...]
    w2 = w2_ref[...]
    for pair in range(PAIRS):
        span = slice(PAIR_ROWS * pair, PAIR_ROWS * pair + PAIR_ROWS)
        modes = mode_rows(rows_ref, lat, pair)
        modes_ref[span] = modes
        pre = jnp.dot(modes, w1, preferred_element_type=F32) + b1_ref[...]
        cdf = 0.5 + 0.5 * lax.erf(pre * math.sqrt(0.5))
        hidden = (pre * cdf).astype(BF)
        slope_ref[span] = cdf + pre * (
            jnp.exp(-0.5 * pre * pre) * (1.0 / math.sqrt(2.0 * math.pi))
        )
        hidden_ref[span] = hidden
        filtered = (jnp.dot(hidden, w2, preferred_element_type=F32) + b2_ref[...]).astype(BF)
        store_rows(rows_ref, lat, pair, filtered)
    pack_bands(rows_ref, out_ref)


NT = (((1,), (1,)), ((), ()))
TN = (((0,), (0,)), ((), ()))


def backward_kernel(
    recv_ref, lat_ref, w1_ref, w2_ref, modes_ref, hidden_ref, slope_ref,
    out_ref, grad_ref, rows_ref, filtered_ref, pre_ref,
):
    unpack_bands(recv_ref, rows_ref)
    lat = lat_ref[...]
    w1 = w1_ref[...]
    w2 = w2_ref[...]
    for pair in range(PAIRS):
        span = slice(PAIR_ROWS * pair, PAIR_ROWS * pair + PAIR_ROWS)
        back_filtered = mode_rows(rows_ref, lat, pair)
        filtered_ref[span] = back_filtered
        back_hidden = lax.dot_general(back_filtered, w2, NT, preferred_element_type=F32)
        back_pre = (back_hidden * slope_ref[span]).astype(BF)
        pre_ref[span] = back_pre
        back_modes = lax.dot_general(back_pre, w1, NT, preferred_element_type=F32).astype(BF)
        store_rows(rows_ref, lat, pair, back_modes)
    ones = jnp.ones((8, MODES * H), BF)
    row = 0
    bias_rows = []
    for left_ref, right_ref in ((modes_ref, pre_ref), (hidden_ref, filtered_ref)):
        right = right_ref[...]
        gathered = lax.dot_general(left_ref[...], right, TN, preferred_element_type=F32)
        real = gathered[0:BS, 0:128] + gathered[128 : 128 + BS, 128:256]
        imag = gathered[0:BS, 128:256] - gathered[128 : 128 + BS, 0:128]
        for part in (real, imag):
            for piece in pack_tile(part):
                grad_ref[row : row + 24] = piece
                row += 24
        bias = jnp.dot(ones, right, preferred_element_type=F32)
        bias_rows += [bias[:, 0:128], bias[:, 128:256]]
    for value in bias_rows:
        grad_ref[row : row + 8] = value
        row += 8
    grad_ref[row:] = jnp.zeros((CHUNKS * CHUNK_ROWS - row, 128), F32)
    pack_bands(rows_ref, out_ref)


def receive(recv_ref, rows_ref):
    for group in range(GROUPS):
        for quad in range(2):
            tiles = []
            for block in range(4):
                band = (4 * quad + block) * GROUPS + group
                pieces = [
                    recv_ref[band, 24 * i : 24 * i + 24, :].astype(F32) for i in range(3)
                ]
                tiles.append(jnp.concatenate(pieces + [unpack_tail(pieces)], axis=0))
            for t, joined in enumerate(join_lanes(tiles)):
                for r in range(ROWS):
                    rows_ref[
                        r,
                        32 * group : 32 * group + 32,
                        384 * quad + 128 * t : 384 * quad + 128 * t + 128,
                    ] = joined[32 * r : 32 * r + 32].astype(BF)


def output_kernel(recv_ref, x_ref, table_ref, out_ref, rows_ref, mixed_ref):
    r = pl.program_id(0)

    @pl.when(r == 0)
    def _():
        receive(recv_ref, rows_ref)

    mixed_ref[...] = jnp.dot(table_ref[...], rows_ref[r], preferred_element_type=F32)
    for start, size in ROW_CHUNKS:
        values = x_ref[0, 0, start : start + size].astype(F32)
        normed = normalize(values)[0]
        out_ref[0, 0, start : start + size] = (
            values + normed + mixed_ref[start : start + size]
        ).astype(BF)


def input_grad_kernel(recv_ref, x_ref, g_ref, table_ref, out_ref, rows_ref, mixed_ref):
    r = pl.program_id(0)

    @pl.when(r == 0)
    def _():
        receive(recv_ref, rows_ref)

    mixed_ref[...] = jnp.dot(table_ref[...], rows_ref[r], preferred_element_type=F32)
    for start, size in ROW_CHUNKS:
        values = x_ref[0, 0, start : start + size].astype(F32)
        upstream = g_ref[0, 0, start : start + size].astype(F32)
        normed, scale = normalize(values)
        back = upstream + mixed_ref[start : start + size]
        mean = jnp.sum(back, axis=-1, keepdims=True) * (1.0 / C)
        along = jnp.sum(back * normed, axis=-1, keepdims=True) * (1.0 / C)
        out_ref[0, 0, start : start + size] = (
            upstream + scale * (back - mean - normed * along)
        ).astype(BF)


def from_spectra(kernel, name, recv, arrays, table):
    token_spec = pl.BlockSpec((1, 1, W, C), lambda r: (0, r, 0, 0))
    return pl.pallas_call(
        kernel,
        name=name,
        grid=(ROWS,),
        in_specs=[pl.BlockSpec((BANDS, PACK, 128), lambda r: (0, 0, 0))]
        + [token_spec] * len(arrays)
        + [pl.BlockSpec((WPAD, 2 * KX), lambda r: (0, 0))],
        out_specs=token_spec,
        out_shape=jax.ShapeDtypeStruct((1, ROWS, W, C), BF),
        scratch_shapes=[
            pltpu.VMEM((ROWS, 2 * KX, C), BF),
            pltpu.VMEM((WPAD, C), F32),
        ],
        compiler_params=pltpu.CompilerParams(vmem_limit_bytes=VMEM_LIMIT),
        cost_estimate=pl.CostEstimate(
            flops=2 * ROWS * W * 2 * KX * C, bytes_accessed=3000000, transcendentals=0
        ),
    )(recv, *arrays, table)


def whole(shape):
    return pl.BlockSpec(shape, lambda: (0,) * len(shape))


def spectral_call(kernel, name, operands, outs, scratch):
    return pl.pallas_call(
        kernel,
        name=name,
        in_specs=[whole(operand.shape) for operand in operands],
        out_specs=[whole(out.shape) for out in outs],
        out_shape=outs,
        scratch_shapes=scratch,
        compiler_params=pltpu.CompilerParams(vmem_limit_bytes=VMEM_LIMIT),
        cost_estimate=pl.CostEstimate(
            flops=1000000000, bytes_accessed=6000000, transcendentals=800000
        ),
    )(*operands)


SPECTRA = jax.ShapeDtypeStruct((BANDS, PACK, 128), BF)


def sum_kernel(recv_ref, out_ref):
    total = recv_ref[0].astype(F32)
    for i in range(1, recv_ref.shape[0]):
        total = total + recv_ref[i].astype(F32)
    out_ref[...] = total.astype(BF)


def group_sum_kernel(recv_ref, out_ref):
    for block in range(NB):
        total = recv_ref[block * GROUPS].astype(F32)
        for group in range(1, GROUPS):
            total = total + recv_ref[block * GROUPS + group].astype(F32)
        out_ref[block] = total.astype(BF)


GRAD_SCALE = 1.0 / (SAMPLES * H)


def grads_kernel(recv_ref, w1_ref, b1_ref, w2_ref, b2_ref):
    for block in range(NB):
        chunk = 0
        for out_ref in (w1_ref, w2_ref):
            for part in range(2):
                pieces = [
                    recv_ref[chunk + i, block].astype(F32) * GRAD_SCALE for i in range(3)
                ]
                chunk += 3
                for i in range(3):
                    out_ref[part, block, 24 * i : 24 * i + 24, :] = pieces[i][:, :BS]
                out_ref[part, block, 72:96, :] = unpack_tail(pieces)[:, :BS]
    rows = [
        jnp.concatenate([recv_ref[12, block], recv_ref[13, block]], axis=0).astype(F32)
        * GRAD_SCALE
        for block in range(NB)
    ]
    for out_ref, first in ((b1_ref, 0), (b2_ref, 16)):
        for part in range(2):
            at = first + 8 * part
            for quad in range(2):
                parts = [rows[4 * quad + j][at : at + 8] for j in range(4)]
                for t, joined in enumerate(join_lanes(parts)):
                    lane = 384 * quad + 128 * t
                    out_ref[part : part + 1, lane : lane + 128] = joined[0:1]


def padded_form(weight, block):
    chosen = lax.dynamic_index_in_dim(weight, block, axis=1, keepdims=False)
    padded = jnp.pad(chosen, ((0, 0), (0, 128 - BS), (0, 128 - BS)))
    upper = jnp.concatenate([padded[0], padded[1]], axis=1)
    lower = jnp.concatenate([-padded[1], padded[0]], axis=1)
    return jnp.concatenate([upper, lower], axis=0)


def padded_bias(bias, block):
    chosen = lax.dynamic_index_in_dim(bias.reshape(2, NB, BS), block, axis=1, keepdims=False)
    return jnp.pad(chosen, ((0, 0), (0, 128 - BS))).reshape(1, 256)


def exchange(value):
    return lax.all_to_all(value, "lat", split_axis=0, concat_axis=0, tiled=True)


def on_device(fields, cotangent, w_first, b_first, w_second, b_second):
    block = lax.axis_index("lat") // GROUPS
    lon_fwd = jnp.asarray(LON_FWD, BF)
    lon_inv = jnp.asarray(LON_INV, BF)
    lon_fwd_t = jnp.asarray(LON_FWD.T, BF)
    lon_inv_t = jnp.asarray(LON_INV.T, BF)
    lat = jnp.asarray(LAT, BF)
    w1 = padded_form(w_first, block)
    w2 = padded_form(w_second, block)
    b1 = padded_bias(b_first, block)
    b2 = padded_bias(b_second, block)

    spectra = exchange(to_spectra(fields_kernel, "fields_dft", fields, lon_fwd_t))
    back_rows = exchange(to_spectra(cotangent_kernel, "cot_dft", cotangent, lon_inv_t))

    wide = (MODES * H, 256)
    rows_scratch = pltpu.VMEM((BANDS * TILE_ROWS, 128), F32)
    row_spectra, modes, hidden, slope = spectral_call(
        forward_kernel,
        "spectral_fwd",
        (spectra, lat, w1, b1, w2, b2),
        [
            SPECTRA,
            jax.ShapeDtypeStruct(wide, BF),
            jax.ShapeDtypeStruct(wide, BF),
            jax.ShapeDtypeStruct(wide, F32),
        ],
        [rows_scratch],
    )
    back_spectra, grads = spectral_call(
        backward_kernel,
        "spectral_bwd",
        (back_rows, lat, w1, w2, modes, hidden, slope),
        [SPECTRA, jax.ShapeDtypeStruct((CHUNKS * CHUNK_ROWS, 128), F32)],
        [rows_scratch, pltpu.VMEM(wide, BF), pltpu.VMEM(wide, BF)],
    )
    dp_size = lax.axis_size("dp")
    rows = CHUNKS * CHUNK_ROWS // dp_size
    shares = lax.all_to_all(
        grads.astype(BF).reshape(dp_size, rows, 128), "dp", 0, 0, tiled=True
    )
    share = spectral_call(
        sum_kernel, "grad_sum", (shares,), [jax.ShapeDtypeStruct((rows, 128), BF)], []
    )[0]
    banded = lax.all_gather(share, "lat", axis=0, tiled=False)
    blocks = spectral_call(
        group_sum_kernel, "grad_groups", (banded,), [jax.ShapeDtypeStruct((NB, rows, 128), BF)], []
    )[0]
    every = lax.all_gather(blocks, "dp", axis=0, tiled=False)
    if dp_size != CHUNKS:
        every = (
            every.transpose(1, 0, 2, 3)
            .reshape(NB, CHUNKS, CHUNK_ROWS, 128)
            .transpose(1, 0, 2, 3)
        )
    grad_w = jax.ShapeDtypeStruct((2, NB, BS, BS), F32)
    grad_b = jax.ShapeDtypeStruct((2, C), F32)
    g_w1, g_b1, g_w2, g_b2 = spectral_call(
        grads_kernel, "grad_out", (every,), [grad_w, grad_b, grad_w, grad_b], []
    )

    row_spectra = exchange(row_spectra)
    back_spectra = exchange(back_spectra)
    result = from_spectra(output_kernel, "output", row_spectra, (fields,), lon_inv)
    back_fields = from_spectra(
        input_grad_kernel, "fields_grad", back_spectra, (fields, cotangent), lon_fwd
    )
    return (result, back_fields, g_w1, g_b1, g_w2, g_b2)


def solution(mesh):
    placed = (P("dp", "lat", None, None), P("dp", "lat", None, None), P(), P(), P(), P())
    return jax.shard_map(
        on_device,
        mesh=mesh,
        in_specs=placed,
        out_specs=(P("dp", "lat", None, None), P("dp", "lat", None, None), P(), P(), P(), P()),
        check_vma=False,
    )
```

time: 437 us -> 196 us (0.45)
  waiting for transfers between devices: 298 us -> 21.6 us
  blocking collectives: 0 us -> 115 us
  matrix products: 31.7 us -> 0 us
  local copies, waits for them, and re-layouts: 41 us -> 9.79 us
  Pallas kernels: 0 us -> 23.6 us
  other arithmetic: 16.5 us -> 0.07 us
  between operations: 14.6 us -> 0.88 us
  starting transfers between devices: 33.5 us -> 24.1 us
    psum x1 -> x0, waiting for transfers between devices: 261 us -> none  [on_device(): all_grads = lax.psum(packed, ('dp', 'lat'))]
    all_gather x0 -> x2, blocking collectives: none -> 73.5 us  [the longest x1 44.1 us: on_device(): banded = lax.all_gather(share, 'lat', axis=0, tiled=False)]
    all_to_all x0 -> x2, blocking collectives: none -> 41.2 us  [the longest x1 22.4 us: exchange(): return lax.all_to_all(value, 'lat', split_axis=0, concat_axis=0, tiled=True)]
    dot_general x14 -> x0, matrix products: 31.7 us -> none  [product(): jnp.einsum(pattern, left_side, right_side, preferred_element_type=jnp.flo...]
    pallas_call x0 -> x9, Pallas kernels: none -> 23.6 us  [the longest x5 12.3 us: spectral_call(): pl.pallas_call(kernel, name=name, in_specs=[whole(operand.shape) for oper...]
    all_to_all x4 -> x3, waiting for transfers between devices: 37.2 us -> 21.6 us  [exchange(): return lax.all_to_all(value, 'lat', split_axis=0, concat_axis=0, tiled=True)]
    convert_element_type x6 -> x0, local copies, waits for them, and re-layouts: 11 us -> none  [the longest x2 3.67 us: spectral_backward(): back_modes = product('bmkpno,nqipo->bmkqni', pre_blocked, first_form).res...]
    all_to_all x4 -> x3, starting transfers between devices: 33.4 us -> 24.1 us  [exchange(): return lax.all_to_all(value, 'lat', split_axis=0, concat_axis=0, tiled=True)]
  transfers between devices with their start and end apart: 5 -> 3, of which waited for: 4 -> 2; matrix products, arithmetic and copies ran while one was open for 9% -> 1% of each run, Pallas kernels for 0% -> 6%
where the time goes in v1:
time: 196 us; the launch traced here: 195 us
  blocking collectives  115 us (59%)
  starting transfers between devices  24.1 us (12%)
  Pallas kernels  23.6 us (12%)
  waiting for transfers between devices  21.6 us (11%)
  local copies, waits for them, and re-layouts  9.79 us (5%)
    all_gather x1, blocking collectives, on_device(): banded = lax.all_gather(share, 'lat', axis=0, tiled=False)  44.1 us
    all_gather x1, blocking collectives, on_device(): every = lax.all_gather(blocks, 'dp', axis=0, tiled=False)  29.3 us
    all_to_all x3, starting transfers between devices, exchange(): return lax.all_to_all(value, 'lat', split_axis=0, concat_axis=0, tiled=True)  24.1 us
    all_to_all x1, blocking collectives, exchange(): return lax.all_to_all(value, 'lat', split_axis=0, concat_axis=0, tiled=True)  22.4 us
    all_to_all x3, waiting for transfers between devices, exchange(): return lax.all_to_all(value, 'lat', split_axis=0, concat_axis=0, tiled=True)  21.6 us
    all_to_all x1, blocking collectives, on_device(): lax.all_to_all(grads.astype(BF).reshape(dp_size, rows, 128), 'dp', 0, 0,...  18.8 us
    pallas_call x5, Pallas kernels, spectral_call(): pl.pallas_call(kernel, name=name, in_specs=[whole(operand.shape) for oper...  12.3 us
    unnamed x38, local copies, waits for them, and re-layouts  8.74 us
  transfers between devices with their start and end apart: 3, of which 2 were waited for; matrix products, arithmetic and copies ran while one was open for 1% of the time, Pallas kernels for 6%

profile of v1, /device:TPU:1, one launch (start us, length us, event | category | flops | bytes accessed | tf_op | source)
XLA Modules:
  0.0 194.8 jit_solution(16340947541419220236)
XLA Ops:
  0.6 1.1 copy-done
  1.8 0.8 copy-done.13
  2.6 3.0 %fields_dft.1 = bf16[32,72,128]{2,1,0:T(8,128)(2,1)} custom-call(bf16[1,3,180,768]{3,2,1,0:T(8,128)(2,1)S(1)} %copy-done, bf16[128,192]{1,0:T(8,128)(2,1)S(1)} %copy-done.13), custom_call_target="tpu_custom_call" | custom-call | flops 106168320 | bytes 1500000 | tf_op jit(solution)/shard_map/fields_dft/pallas_call | solution.py:162
  5.7 13.7 %all-to-all-start = ((bf16[32,72,128]{2,1,0:T(8,128)(2,1)}), bf16[32,72,128]{2,1,0:T(8,128)(2,1)S(1)}, u32[]{:S(2)}, u32[]{:S(2)}) async-start(bf16[32,72,128]{2,1,0:T(8,128)(2,1)} %fields_dft.1), calls=%async_computation | async-start | bytes 1179648 | tf_op jit(solution)/shard_map/all_to_all | solution.py:476
  19.4 2.3 %cot_dft.1 = bf16[32,72,128]{2,1,0:T(8,128)(2,1)} custom-call(bf16[1,3,180,768]{3,2,1,0:T(8,128)(2,1)S(1)} %copy-done.2, bf16[128,192]{1,0:T(8,128)(2,1)S(1)} %copy-done.14), custom_call_target="tpu_custom_call" | custom-call | flops 106168320 | bytes 1500000 | tf_op jit(solution)/shard_map/cot_dft/pallas_call | solution.py:162
  21.8 15.2 %all-to-all-done.recv_ref = bf16[32,72,128]{2,1,0:T(8,128)(2,1)S(1)} async-done(((bf16[32,72,128]{2,1,0:T(8,128)(2,1)}), bf16[32,72,128]{2,1,0:T(8,128)(2,1)S(1)}, u32[]{:S(2)}, u32[]{:S(2)}) %all-to-all-start) | async-done | bytes 589856 | tf_op jit(solution)/shard_map/all_to_all | solution.py:476
  37.8 5.3 %all-to-all-start.2 = ((bf16[32,72,128]{2,1,0:T(8,128)(2,1)}), bf16[32,72,128]{2,1,0:T(8,128)(2,1)S(1)}, u32[]{:S(2)}, u32[]{:S(2)}) async-start(bf16[32,72,128]{2,1,0:T(8,128)(2,1)} %cot_dft.1), calls=%async_computation.2 | async-start | bytes 1179648 | tf_op jit(solution)/shard_map/all_to_all | solution.py:476
  43.4 0.8 dynamic-slice_bitcast_fusion
  44.3 1.1 copy-done.8
  45.4 5.2 %spectral_fwd.1 = (bf16[32,72,128]{2,1,0:T(8,128)(2,1)S(1)}, bf16[1536,256]{1,0:T(8,128)(2,1)S(1)}, bf16[1536,256]{1,0:T(8,128)(2,1)S(1)}, f32[1536,256]{1,0:T(8,128)S(1)}) custom-call(bf16[32,72,128]{2,1,0:T(8,128)(2,1)S(1)} %copy-done.8, bf16[192,192]{1,0:T(8,128)(2,1)S(1)} %copy-done.12, bf16[256,256]{1,0:T(8,128)(2,1)S(1)} %maximum_maximum_fusion.w1_ref, ...), custom_call_target="tpu_custom_call" | custom-call | flops 1000000000 | bytes 6000000 | tf_op jit(solution)/shard_map/spectral_fwd/pallas_call | solution.py:400
  50.7 0.9 copy-done.3
  51.5 0.9 copy-done.5
  53.2 6.4 %all-to-all-done.2.recv_ref = bf16[32,72,128]{2,1,0:T(8,128)(2,1)S(1)} async-done(((bf16[32,72,128]{2,1,0:T(8,128)(2,1)}), bf16[32,72,128]{2,1,0:T(8,128)(2,1)S(1)}, u32[]{:S(2)}, u32[]{:S(2)}) %all-to-all-start.2) | async-done | bytes 589856 | tf_op jit(solution)/shard_map/all_to_all | solution.py:476
  59.7 1.1 copy-done.4
  60.8 1.1 copy-done.6
  61.9 5.5 %spectral_bwd.1 = (bf16[32,72,128]{2,1,0:T(8,128)(2,1)S(1)}, f32[384,128]{1,0:T(8,128)S(1)}) custom-call(bf16[32,72,128]{2,1,0:T(8,128)(2,1)S(1)} %all-to-all-done.2.recv_ref, bf16[192,192]{1,0:T(8,128)(2,1)S(1)} %copy-done.12, bf16[256,256]{1,0:T(8,128)(2,1)S(1)} %maximum_maximum_fusion.w1_ref, bf16[256,256]{1,0:T(8,128)(2,1)S(1)} %maximum_maximum_fusion.1.w2_ref, ...), custom_call_target="tpu_custom_call" | custom-call | flops 1000000000 | bytes 6000000 | tf_op jit(solution)/shard_map/spectral_bwd/pallas_call | solution.py:400
  67.5 18.8 %all_to_all.25.recv_ref = bf16[16,24,128]{2,1,0:T(8,128)(2,1)S(1)} all-to-all(bf16[16,24,128]{2,1,0:T(8,128)(2,1)S(1)} %bitcast.27), channel_id=1, replica_groups=mesh['dp'=16,'lat'=32] {'dp'}, dimensions={0} | all-to-all | bytes 196608 | tf_op jit(solution)/shard_map/all_to_all | solution.py:517
  86.4 22.4 %all_to_all.26.recv_ref = bf16[32,72,128]{2,1,0:T(8,128)(2,1)S(1)} all-to-all(bf16[32,72,128]{2,1,0:T(8,128)(2,1)S(1)} %copy-done.11), channel_id=1, replica_groups=mesh['dp'=16,'lat'=32] {'lat'}, dimensions={0} | all-to-all | bytes 1179648 | tf_op jit(solution)/shard_map/all_to_all | solution.py:476
  108.7 5.1 %all-to-all-start.3 = ((bf16[32,72,128]{2,1,0:T(8,128)(2,1)}), bf16[32,72,128]{2,1,0:T(8,128)(2,1)S(1)}, u32[]{:S(2)}, u32[]{:S(2)}) async-start(bf16[32,72,128]{2,1,0:T(8,128)(2,1)} %copy-done.9), calls=%async_computation.3 | async-start | bytes 1179648 | tf_op jit(solution)/shard_map/all_to_all | solution.py:476
  113.8 44.1 %all-gather = bf16[768,128]{1,0:T(8,128)(2,1)S(1)} all-gather(bf16[24,128]{1,0:T(8,128)(2,1)S(1)} %grad_sum.1), channel_id=2, replica_groups=mesh['dp'=16,'lat'=32] {'lat'}, dimensions={0}, use_global_device_ids=true | all-gather | bytes 202752 | tf_op jit(solution)/shard_map/all_gather | solution.py:523
  158.0 29.3 %all-gather.1 = bf16[128,24,128]{2,1,0:T(8,128)(2,1)S(1)} all-gather(bf16[8,24,128]{2,1,0:T(8,128)(2,1)S(1)} %grad_groups.1), channel_id=3, replica_groups=mesh['dp'=16,'lat'=32] {'dp'}, dimensions={0}, use_global_device_ids=true | all-gather | bytes 835584 | tf_op jit(solution)/shard_map/all_gather | solution.py:527
  187.4 1.5 grad_out.1
  188.9 2.8 %output.1 = bf16[1,3,180,768]{3,2,1,0:T(8,128)(2,1)} custom-call(bf16[32,72,128]{2,1,0:T(8,128)(2,1)S(1)} %all_to_all.26.recv_ref, bf16[1,3,180,768]{3,2,1,0:T(8,128)(2,1)S(1)} %copy-done.1, bf16[192,128]{1,0:T(8,128)(2,1)S(1)} %copy-done.16), custom_call_target="tpu_custom_call" | custom-call | flops 106168320 | bytes 3000000 | tf_op jit(solution)/shard_map/output/pallas_call | solution.py:375
  191.7 3.1 %fields_grad.1 = bf16[1,3,180,768]{3,2,1,0:T(8,128)(2,1)} custom-call(bf16[32,72,128]{2,1,0:T(8,128)(2,1)S(1)} %all-to-all-done.3.recv_ref, bf16[1,3,180,768]{3,2,1,0:T(8,128)(2,1)S(1)} %copy-done.1, bf16[1,3,180,768]{3,2,1,0:T(8,128)(2,1)S(1)} %copy-done.2, bf16[192,128]{1,0:T(8,128)(2,1)S(1)} %copy-done.15), custom_call_target="tpu_custom_call" | custom-call | flops 106168320 | bytes 3000000 | tf_op jit(solution)/shard_map/fields_grad/pallas_call | solution.py:375
  (46 shorter events, 2.0 us)
Async XLA Ops:
  0.6 1.2 copy-start
  1.8 0.8 copy-start.13
  2.6 16.8 %copy-start.2 = (bf16[1,3,180,768]{3,2,1,0:T(8,128)(2,1)S(1)}, bf16[1,3,180,768]{3,2,1,0:T(8,128)(2,1)}, u32[]{:S(2)}) copy-start(bf16[1,3,180,768]{3,2,1,0:T(8,128)(2,1)} %g_ref.1) | copy-start | bytes 2488324
  2.6 16.8 %copy-start.14 = (bf16[128,192]{1,0:T(8,128)(2,1)S(1)}, bf16[128,192]{1,0:T(8,128)(2,1)}, u32[]{:S(2)}) copy-start(bf16[128,192]{1,0:T(8,128)(2,1)} %constant.51.clone.table_ref) | copy-start | bytes 147460
  5.7 31.3 %all-to-all-start = ((bf16[32,72,128]{2,1,0:T(8,128)(2,1)}), bf16[32,72,128]{2,1,0:T(8,128)(2,1)S(1)}, u32[]{:S(2)}, u32[]{:S(2)}) async-start(bf16[32,72,128]{2,1,0:T(8,128)(2,1)} %fields_dft.1), calls=%async_computation | async-start | bytes 1179648 | tf_op jit(solution)/shard_map/all_to_all | solution.py:476
  19.4 23.7 %copy-start.17 = (f32[2,768]{1,0:T(2,128)S(1)}, f32[2,768]{1,0:T(2,128)}, u32[]{:S(2)}) copy-start(f32[2,768]{1,0:T(2,128)} %param.14) | copy-start | bytes 18436
  19.4 23.8 %copy-start.18 = (f32[2,768]{1,0:T(2,128)S(1)}, f32[2,768]{1,0:T(2,128)}, u32[]{:S(2)}) copy-start(f32[2,768]{1,0:T(2,128)} %param.16) | copy-start | bytes 18436
  19.4 24.9 %copy-start.12 = (bf16[192,192]{1,0:T(8,128)(2,1)S(1)}, bf16[192,192]{1,0:T(8,128)(2,1)}, u32[]{:S(2)}) copy-start(bf16[192,192]{1,0:T(8,128)(2,1)} %constant.52.clone.lat_ref) | copy-start | bytes 221188
  37.0 0.8 copy-start.7
  37.8 21.9 %all-to-all-start.2 = ((bf16[32,72,128]{2,1,0:T(8,128)(2,1)}), bf16[32,72,128]{2,1,0:T(8,128)(2,1)S(1)}, u32[]{:S(2)}, u32[]{:S(2)}) async-start(bf16[32,72,128]{2,1,0:T(8,128)(2,1)} %cot_dft.1), calls=%async_computation.2 | async-start | bytes 1179648 | tf_op jit(solution)/shard_map/all_to_all | solution.py:476
  44.3 1.1 copy-start.8
  50.6 0.9 copy-start.3
  51.5 0.9 copy-start.5
  52.4 0.8 copy-start.10
  59.7 1.1 copy-start.4
  60.8 1.1 copy-start.6
  61.9 24.4 %copy-start.11 = (bf16[32,72,128]{2,1,0:T(8,128)(2,1)S(1)}, bf16[32,72,128]{2,1,0:T(8,128)(2,1)}, u32[]{:S(2)}) copy-start(bf16[32,72,128]{2,1,0:T(8,128)(2,1)} %copy-done.10) | copy-start | bytes 1769476
  67.5 41.3 %copy-start.9 = (bf16[32,72,128]{2,1,0:T(8,128)(2,1)}, bf16[32,72,128]{2,1,0:T(8,128)(2,1)S(1)}, u32[]{:S(2)}) copy-start(bf16[32,72,128]{2,1,0:T(8,128)(2,1)S(1)} %get-tuple-element.20) | copy-start | bytes 1769476
  108.7 82.9 %all-to-all-start.3 = ((bf16[32,72,128]{2,1,0:T(8,128)(2,1)}), bf16[32,72,128]{2,1,0:T(8,128)(2,1)S(1)}, u32[]{:S(2)}, u32[]{:S(2)}) async-start(bf16[32,72,128]{2,1,0:T(8,128)(2,1)} %copy-done.9), calls=%async_computation.3 | async-start | bytes 1179648 | tf_op jit(solution)/shard_map/all_to_all | solution.py:476
  187.3 1.5 copy-start.1
  187.4 1.5 copy-start.16
  188.9 2.8 %copy-start.15 = (bf16[192,128]{1,0:T(8,128)(2,1)S(1)}, bf16[192,128]{1,0:T(8,128)(2,1)}, u32[]{:S(2)}) copy-start(bf16[192,128]{1,0:T(8,128)(2,1)} %constant.48.clone.table_ref) | copy-start | bytes 147460

commit v2 on v1

--- a/solution.py
+++ b/solution.py
@@ -27,7 +27,7 @@
 CHUNK_ROWS = 24
 BF = jnp.bfloat16
 F32 = jnp.float32
-VMEM_LIMIT = 48 * 1024 * 1024
+VMEM_LIMIT = 16 * 1024 * 1024
 
 
 def tables():
@@ -115,7 +115,7 @@
     return centered * scale, scale
 
 
-def send_packed(acc_ref, out_ref):
+def send_packed(acc_ref, out_ref, first):
     for block in range(NB):
         rows = [block_lanes(acc_ref[r], block) for r in range(ROWS)]
         for group in range(GROUPS):
@@ -123,70 +123,74 @@
                 [row[32 * group : 32 * group + 32] for row in rows], axis=0
             )
             pieces = pack_tile(tile)
-            out_ref[block * GROUPS + group] = jnp.concatenate(pieces, axis=0).astype(BF)
-
-
-def fields_kernel(x_ref, table_ref, out_ref, normed_ref, acc_ref):
-    r = pl.program_id(0)
-
-    @pl.when(r == 0)
-    def _():
-        normed_ref[...] = jnp.zeros_like(normed_ref)
-
-    for start, size in ROW_CHUNKS:
-        values = x_ref[0, 0, start : start + size].astype(F32)
-        normed_ref[start : start + size] = normalize(values)[0].astype(BF)
-    acc_ref[r] = jnp.dot(table_ref[...], normed_ref[...], preferred_element_type=F32)
-
-    @pl.when(r == ROWS - 1)
-    def _():
-        send_packed(acc_ref, out_ref)
-
-
-def cotangent_kernel(x_ref, table_ref, out_ref, padded_ref, acc_ref):
-    r = pl.program_id(0)
-
-    @pl.when(r == 0)
+            out_ref[block * GROUPS + group, first : first + PACK] = jnp.concatenate(
+                pieces, axis=0
+            ).astype(BF)
+
+
+def spectra_kernel(x_ref, g_ref, fwd_ref, inv_ref, out_ref, padded_ref, acc_ref):
+    step = pl.program_id(0)
+
+    @pl.when(step == 0)
     def _():
         padded_ref[...] = jnp.zeros_like(padded_ref)
 
-    padded_ref[0:W] = x_ref[0, 0]
-    acc_ref[r] = jnp.dot(table_ref[...], padded_ref[...], preferred_element_type=F32)
-
-    @pl.when(r == ROWS - 1)
+    @pl.when(step < ROWS)
     def _():
-        send_packed(acc_ref, out_ref)
-
-
-def to_spectra(kernel, name, array, table):
+        for start, size in ROW_CHUNKS:
+            values = x_ref[0, 0, start : start + size].astype(F32)
+            padded_ref[start : start + size] = normalize(values)[0].astype(BF)
+        acc_ref[step] = jnp.dot(fwd_ref[...], padded_ref[...], preferred_element_type=F32)
+
+    @pl.when(step == ROWS - 1)
+    def _():
+        send_packed(acc_ref, out_ref, 0)
+
+    @pl.when(step >= ROWS)
+    def _():
+        padded_ref[0:W] = g_ref[0, 0]
+        acc_ref[step - ROWS] = jnp.dot(
+            inv_ref[...], padded_ref[...], preferred_element_type=F32
+        )
+
+    @pl.when(step == 2 * ROWS - 1)
+    def _():
+        send_packed(acc_ref, out_ref, PACK)
+
+
+def to_spectra(fields, cotangent, forward, inverse):
+    table_spec = pl.BlockSpec((2 * KX, WPAD), lambda r: (0, 0))
     return pl.pallas_call(
-        kernel,
-        name=name,
-        grid=(ROWS,),
+        spectra_kernel,
+        name="to_spectra",
+        grid=(2 * ROWS,),
         in_specs=[
-            pl.BlockSpec((1, 1, W, C), lambda r: (0, r, 0, 0)),
-            pl.BlockSpec((2 * KX, WPAD), lambda r: (0, 0)),
-        ],
-        out_specs=pl.BlockSpec((BANDS, PACK, 128), lambda r: (0, 0, 0)),
-        out_shape=jax.ShapeDtypeStruct((BANDS, PACK, 128), BF),
+            pl.BlockSpec((1, 1, W, C), lambda r: (0, jnp.minimum(r, ROWS - 1), 0, 0)),
+            pl.BlockSpec((1, 1, W, C), lambda r: (0, jnp.maximum(r - ROWS, 0), 0, 0)),
+            table_spec,
+            table_spec,
+        ],
+        out_specs=pl.BlockSpec((BANDS, 2 * PACK, 128), lambda r: (0, 0, 0)),
+        out_shape=jax.ShapeDtypeStruct((BANDS, 2 * PACK, 128), BF),
         scratch_shapes=[
             pltpu.VMEM((WPAD, C), BF),
             pltpu.VMEM((ROWS, 2 * KX, C), F32),
         ],
         compiler_params=pltpu.CompilerParams(vmem_limit_bytes=VMEM_LIMIT),
         cost_estimate=pl.CostEstimate(
-            flops=2 * ROWS * W * 2 * KX * C, bytes_accessed=1500000, transcendentals=0
+            flops=4 * ROWS * W * 2 * KX * C, bytes_accessed=3000000, transcendentals=0
         ),
-    )(array, table)
+    )(fields, cotangent, forward, inverse)
 
 
 TILE_ROWS = 2 * ROWS * MODES
 
 
-def unpack_bands(recv_ref, rows_ref):
+def unpack_bands(recv_ref, first, rows_ref):
     def one(s, carry):
         pieces = [
-            recv_ref[s, 24 * i : 24 * i + 24, :].astype(F32) for i in range(3)
+            recv_ref[s, first + 24 * i : first + 24 * i + 24, :].astype(F32)
+            for i in range(3)
         ]
         base = pl.multiple_of(s * TILE_ROWS, TILE_ROWS)
         for i in range(3):
@@ -201,7 +205,7 @@
     def one(s, carry):
         base = pl.multiple_of(s * TILE_ROWS, TILE_ROWS)
         pieces = pack_tile(rows_ref[pl.ds(base, TILE_ROWS), :])
-        out_ref[s] = jnp.concatenate(pieces, axis=0).astype(BF)
+        out_ref[s, 0:PACK] = jnp.concatenate(pieces, axis=0).astype(BF)
         return carry
 
     lax.fori_loop(0, BANDS, one, 0, unroll=4)
@@ -249,11 +253,39 @@
 PAIRS = MODES // 2
 
 
-def forward_kernel(
-    recv_ref, lat_ref, w1_ref, b1_ref, w2_ref, b2_ref,
-    out_ref, modes_ref, hidden_ref, slope_ref, rows_ref,
+def fill_weight(weight_ref, form_ref):
+    form_ref[...] = jnp.zeros_like(form_ref)
+    real = weight_ref[0, 0]
+    imag = weight_ref[1, 0]
+    form_ref[0:BS, 0:BS] = real
+    form_ref[0:BS, 128 : 128 + BS] = imag
+    form_ref[128 : 128 + BS, 0:BS] = -imag
+    form_ref[128 : 128 + BS, 128 : 128 + BS] = real
+
+
+def choose_bias(block, bias_ref):
+    bias = bias_ref[...]
+    chosen = block_lanes(bias, 0)
+    for other in range(1, NB):
+        chosen = jnp.where(block == other, block_lanes(bias, other), chosen)
+    chosen = jnp.where(lanes(chosen.shape) < BS, chosen, 0.0)
+    return jnp.concatenate([chosen[0:1], chosen[1:2]], axis=1)
+
+
+NT = (((1,), (1,)), ((), ()))
+TN = (((0,), (0,)), ((), ()))
+
+
+def gradient_kernel(
+    block_ref, recv_ref, lat_ref, first_ref, bias_ref, second_ref,
+    hidden_ref, pre_ref, grad_ref,
+    w1_ref, w2_ref, rows_ref, back_rows_ref, modes_ref, filtered_ref, sums_ref,
 ):
-    unpack_bands(recv_ref, rows_ref)
+    fill_weight(first_ref, w1_ref)
+    fill_weight(second_ref, w2_ref)
+    bias = choose_bias(block_ref[0], bias_ref)
+    unpack_bands(recv_ref, 0, rows_ref)
+    unpack_bands(recv_ref, PACK, back_rows_ref)
     lat = lat_ref[...]
     w1 = w1_ref[...]
     w2 = w2_ref[...]
@@ -261,39 +293,14 @@
         span = slice(PAIR_ROWS * pair, PAIR_ROWS * pair + PAIR_ROWS)
         modes = mode_rows(rows_ref, lat, pair)
         modes_ref[span] = modes
-        pre = jnp.dot(modes, w1, preferred_element_type=F32) + b1_ref[...]
+        pre = jnp.dot(modes, w1, preferred_element_type=F32) + bias
         cdf = 0.5 + 0.5 * lax.erf(pre * math.sqrt(0.5))
-        hidden = (pre * cdf).astype(BF)
-        slope_ref[span] = cdf + pre * (
-            jnp.exp(-0.5 * pre * pre) * (1.0 / math.sqrt(2.0 * math.pi))
-        )
-        hidden_ref[span] = hidden
-        filtered = (jnp.dot(hidden, w2, preferred_element_type=F32) + b2_ref[...]).astype(BF)
-        store_rows(rows_ref, lat, pair, filtered)
-    pack_bands(rows_ref, out_ref)
-
-
-NT = (((1,), (1,)), ((), ()))
-TN = (((0,), (0,)), ((), ()))
-
-
-def backward_kernel(
-    recv_ref, lat_ref, w1_ref, w2_ref, modes_ref, hidden_ref, slope_ref,
-    out_ref, grad_ref, rows_ref, filtered_ref, pre_ref,
-):
-    unpack_bands(recv_ref, rows_ref)
-    lat = lat_ref[...]
-    w1 = w1_ref[...]
-    w2 = w2_ref[...]
-    for pair in range(PAIRS):
-        span = slice(PAIR_ROWS * pair, PAIR_ROWS * pair + PAIR_ROWS)
-        back_filtered = mode_rows(rows_ref, lat, pair)
+        hidden_ref[span] = (pre * cdf).astype(BF)
+        slope = cdf + pre * (jnp.exp(-0.5 * pre * pre) * (1.0 / math.sqrt(2.0 * math.pi)))
+        back_filtered = mode_rows(back_rows_ref, lat, pair)
         filtered_ref[span] = back_filtered
         back_hidden = lax.dot_general(back_filtered, w2, NT, preferred_element_type=F32)
-        back_pre = (back_hidden * slope_ref[span]).astype(BF)
-        pre_ref[span] = back_pre
-        back_modes = lax.dot_general(back_pre, w1, NT, preferred_element_type=F32).astype(BF)
-        store_rows(rows_ref, lat, pair, back_modes)
+        pre_ref[span] = (back_hidden * slope).astype(BF)
     ones = jnp.ones((8, MODES * H), BF)
     row = 0
     bias_rows = []
@@ -304,15 +311,73 @@
         imag = gathered[0:BS, 128:256] - gathered[128 : 128 + BS, 0:128]
         for part in (real, imag):
             for piece in pack_tile(part):
-                grad_ref[row : row + 24] = piece
+                sums_ref[row : row + 24] = piece
                 row += 24
         bias = jnp.dot(ones, right, preferred_element_type=F32)
         bias_rows += [bias[:, 0:128], bias[:, 128:256]]
     for value in bias_rows:
-        grad_ref[row : row + 8] = value
+        sums_ref[row : row + 8] = value
         row += 8
-    grad_ref[row:] = jnp.zeros((CHUNKS * CHUNK_ROWS - row, 128), F32)
-    pack_bands(rows_ref, out_ref)
+    sums_ref[row:] = jnp.zeros((CHUNKS * CHUNK_ROWS - row, 128), F32)
+    for chunk in range(CHUNKS):
+        grad_ref[chunk] = sums_ref[CHUNK_ROWS * chunk : CHUNK_ROWS * chunk + CHUNK_ROWS].astype(
+            BF
+        )
+
+
+def return_kernel(
+    block_ref, hidden_ref, pre_ref, lat_ref, first_ref, second_ref, bias_ref,
+    row_ref, back_ref,
+    w1_ref, w2_ref, rows_ref, back_rows_ref,
+):
+    fill_weight(first_ref, w1_ref)
+    fill_weight(second_ref, w2_ref)
+    bias = choose_bias(block_ref[0], bias_ref)
+    lat = lat_ref[...]
+    w1 = w1_ref[...]
+    w2 = w2_ref[...]
+    for pair in range(PAIRS):
+        span = slice(PAIR_ROWS * pair, PAIR_ROWS * pair + PAIR_ROWS)
+        filtered = jnp.dot(hidden_ref[span], w2, preferred_element_type=F32) + bias
+        store_rows(rows_ref, lat, pair, filtered.astype(BF))
+        back_modes = lax.dot_general(pre_ref[span], w1, NT, preferred_element_type=F32)
+        store_rows(back_rows_ref, lat, pair, back_modes.astype(BF))
+    pack_bands(rows_ref, row_ref)
+    pack_bands(back_rows_ref, back_ref)
+
+
+PAIR_ROWS = 2 * H
+PAIRS = MODES // 2
+WIDE = (MODES * H, 256)
+FORM = pltpu.VMEM((256, 256), BF)
+BAND_ROWS = pltpu.VMEM((2 * H * MODES, 128), F32)
+
+
+def block_call(kernel, name, block, operands, specs, outs, scratch):
+    return pl.pallas_call(
+        kernel,
+        name=name,
+        grid_spec=pltpu.PrefetchScalarGridSpec(
+            num_scalar_prefetch=1,
+            grid=(1,),
+            in_specs=[
+                pl.BlockSpec((2, 1, BS, BS), lambda i, n: (0, n[0], 0, 0))
+                if spec == "weight"
+                else pl.BlockSpec(operand.shape, lambda i, n, d=operand.ndim: (0,) * d)
+                for operand, spec in zip(operands, specs)
+            ],
+            out_specs=[
+                pl.BlockSpec(out.shape, lambda i, n, d=len(out.shape): (0,) * d)
+                for out in outs
+            ],
+            scratch_shapes=scratch,
+        ),
+        out_shape=outs,
+        compiler_params=pltpu.CompilerParams(vmem_limit_bytes=24 * 1024 * 1024),
+        cost_estimate=pl.CostEstimate(
+            flops=1000000000, bytes_accessed=6000000, transcendentals=800000
+        ),
+    )(block, *operands)
 
 
 def receive(recv_ref, rows_ref):
@@ -411,14 +476,29 @@
     )(*operands)
 
 
-SPECTRA = jax.ShapeDtypeStruct((BANDS, PACK, 128), BF)
-
-
-def sum_kernel(recv_ref, out_ref):
+def share_kernel(recv_ref, held_ref, out_ref):
     total = recv_ref[0].astype(F32)
     for i in range(1, recv_ref.shape[0]):
         total = total + recv_ref[i].astype(F32)
-    out_ref[...] = total.astype(BF)
+    share = total.astype(BF)
+    for band in range(BANDS):
+        out_ref[band] = share
+
+
+def add_share(shares, held):
+    return pl.pallas_call(
+        share_kernel,
+        name="grad_share",
+        grid=(1,),
+        in_specs=[
+            pl.BlockSpec(shares.shape, lambda i: (0, 0, 0)),
+            pl.BlockSpec(memory_space=pl.ANY),
+        ],
+        out_specs=pl.BlockSpec((BANDS, CHUNK_ROWS, 128), lambda i: (0, 3, 0)),
+        out_shape=jax.ShapeDtypeStruct(held.shape, BF),
+        input_output_aliases={1: 0},
+        compiler_params=pltpu.CompilerParams(vmem_limit_bytes=VMEM_LIMIT),
+    )(shares, held)
 
 
 def group_sum_kernel(recv_ref, out_ref):
@@ -427,6 +507,18 @@
         for group in range(1, GROUPS):
             total = total + recv_ref[block * GROUPS + group].astype(F32)
         out_ref[block] = total.astype(BF)
+
+
+def group_sums(message):
+    return pl.pallas_call(
+        group_sum_kernel,
+        name="grad_groups",
+        grid=(1,),
+        in_specs=[pl.BlockSpec((BANDS, CHUNK_ROWS, 128), lambda i: (0, 3, 0))],
+        out_specs=pl.BlockSpec((NB, CHUNK_ROWS, 128), lambda i: (0, 0, 0)),
+        out_shape=jax.ShapeDtypeStruct((NB, CHUNK_ROWS, 128), BF),
+        compiler_params=pltpu.CompilerParams(vmem_limit_bytes=VMEM_LIMIT),
+    )(message)
 
 
 GRAD_SCALE = 1.0 / (SAMPLES * H)
@@ -459,87 +551,58 @@
                     out_ref[part : part + 1, lane : lane + 128] = joined[0:1]
 
 
-def padded_form(weight, block):
-    chosen = lax.dynamic_index_in_dim(weight, block, axis=1, keepdims=False)
-    padded = jnp.pad(chosen, ((0, 0), (0, 128 - BS), (0, 128 - BS)))
-    upper = jnp.concatenate([padded[0], padded[1]], axis=1)
-    lower = jnp.concatenate([-padded[1], padded[0]], axis=1)
-    return jnp.concatenate([upper, lower], axis=0)
-
-
-def padded_bias(bias, block):
-    chosen = lax.dynamic_index_in_dim(bias.reshape(2, NB, BS), block, axis=1, keepdims=False)
-    return jnp.pad(chosen, ((0, 0), (0, 128 - BS))).reshape(1, 256)
-
-
 def exchange(value):
     return lax.all_to_all(value, "lat", split_axis=0, concat_axis=0, tiled=True)
 
 
 def on_device(fields, cotangent, w_first, b_first, w_second, b_second):
-    block = lax.axis_index("lat") // GROUPS
+    block = (lax.axis_index("lat") // GROUPS).astype(jnp.int32).reshape(1)
     lon_fwd = jnp.asarray(LON_FWD, BF)
     lon_inv = jnp.asarray(LON_INV, BF)
     lon_fwd_t = jnp.asarray(LON_FWD.T, BF)
     lon_inv_t = jnp.asarray(LON_INV.T, BF)
     lat = jnp.asarray(LAT, BF)
-    w1 = padded_form(w_first, block)
-    w2 = padded_form(w_second, block)
-    b1 = padded_bias(b_first, block)
-    b2 = padded_bias(b_second, block)
-
-    spectra = exchange(to_spectra(fields_kernel, "fields_dft", fields, lon_fwd_t))
-    back_rows = exchange(to_spectra(cotangent_kernel, "cot_dft", cotangent, lon_inv_t))
-
-    wide = (MODES * H, 256)
-    rows_scratch = pltpu.VMEM((BANDS * TILE_ROWS, 128), F32)
-    row_spectra, modes, hidden, slope = spectral_call(
-        forward_kernel,
-        "spectral_fwd",
-        (spectra, lat, w1, b1, w2, b2),
+
+    spectra = exchange(to_spectra(fields, cotangent, lon_fwd_t, lon_inv_t))
+    wide = jax.ShapeDtypeStruct(WIDE, BF)
+    hidden, pre, grads = block_call(
+        gradient_kernel,
+        "spectral_grads",
+        block,
+        (spectra, lat, w_first, b_first, w_second),
+        ("", "", "weight", "", "weight"),
+        [wide, wide, jax.ShapeDtypeStruct((CHUNKS, CHUNK_ROWS, 128), BF)],
+        [FORM, FORM, BAND_ROWS, BAND_ROWS, pltpu.VMEM(WIDE, BF), pltpu.VMEM(WIDE, BF)]
+        + [pltpu.VMEM((CHUNKS * CHUNK_ROWS, 128), F32)],
+    )
+    dp_size = lax.axis_size("dp")
+    if dp_size == CHUNKS:
+        shares = lax.all_to_all(grads, "dp", 0, 0, tiled=True)
+    else:
+        shares = grads
+    row_send, back_send = block_call(
+        return_kernel,
+        "spectral_return",
+        block,
+        (hidden, pre, lat, w_first, w_second, b_second),
+        ("", "", "", "weight", "weight", ""),
         [
-            SPECTRA,
-            jax.ShapeDtypeStruct(wide, BF),
-            jax.ShapeDtypeStruct(wide, BF),
-            jax.ShapeDtypeStruct(wide, F32),
-        ],
-        [rows_scratch],
-    )
-    back_spectra, grads = spectral_call(
-        backward_kernel,
-        "spectral_bwd",
-        (back_rows, lat, w1, w2, modes, hidden, slope),
-        [SPECTRA, jax.ShapeDtypeStruct((CHUNKS * CHUNK_ROWS, 128), F32)],
-        [rows_scratch, pltpu.VMEM(wide, BF), pltpu.VMEM(wide, BF)],
-    )
-    dp_size = lax.axis_size("dp")
-    rows = CHUNKS * CHUNK_ROWS // dp_size
-    shares = lax.all_to_all(
-        grads.astype(BF).reshape(dp_size, rows, 128), "dp", 0, 0, tiled=True
-    )
-    share = spectral_call(
-        sum_kernel, "grad_sum", (shares,), [jax.ShapeDtypeStruct((rows, 128), BF)], []
-    )[0]
-    banded = lax.all_gather(share, "lat", axis=0, tiled=False)
-    blocks = spectral_call(
-        group_sum_kernel, "grad_groups", (banded,), [jax.ShapeDtypeStruct((NB, rows, 128), BF)], []
-    )[0]
+            jax.ShapeDtypeStruct((BANDS, PACK + CHUNK_ROWS, 128), BF),
+            jax.ShapeDtypeStruct((BANDS, PACK, 128), BF),
+        ],
+        [FORM, FORM, BAND_ROWS, BAND_ROWS],
+    )
+    message = exchange(add_share(shares, row_send))
+    back_send, message = lax.optimization_barrier((back_send, message))
+    back_spectra = exchange(back_send)
+    blocks = group_sums(message)
     every = lax.all_gather(blocks, "dp", axis=0, tiled=False)
-    if dp_size != CHUNKS:
-        every = (
-            every.transpose(1, 0, 2, 3)
-            .reshape(NB, CHUNKS, CHUNK_ROWS, 128)
-            .transpose(1, 0, 2, 3)
-        )
     grad_w = jax.ShapeDtypeStruct((2, NB, BS, BS), F32)
     grad_b = jax.ShapeDtypeStruct((2, C), F32)
     g_w1, g_b1, g_w2, g_b2 = spectral_call(
         grads_kernel, "grad_out", (every,), [grad_w, grad_b, grad_w, grad_b], []
     )
-
-    row_spectra = exchange(row_spectra)
-    back_spectra = exchange(back_spectra)
-    result = from_spectra(output_kernel, "output", row_spectra, (fields,), lon_inv)
+    result = from_spectra(output_kernel, "output", message, (fields,), lon_inv)
     back_fields = from_spectra(
         input_grad_kernel, "fields_grad", back_spectra, (fields, cotangent), lon_fwd
     )

time: 196 us -> 136 us (0.69)
  blocking collectives: 115 us -> 45.8 us
  waiting for transfers between devices: 21.6 us -> 30.9 us
  starting transfers between devices: 24.1 us -> 29.2 us
  local copies, waits for them, and re-layouts: 9.79 us -> 6.02 us
    all_gather x1 -> x0, blocking collectives: 44.1 us -> none  [on_device(): banded = lax.all_gather(share, 'lat', axis=0, tiled=False)]
    all_to_all x1 -> x0, blocking collectives: 18.8 us -> none  [on_device(): lax.all_to_all(grads.astype(BF).reshape(dp_size, rows, 128), 'dp', 0, 0,...]
    pallas_call x5 -> x1, Pallas kernels: 12.3 us -> 1.5 us  [spectral_call(): pl.pallas_call(kernel, name=name, in_specs=[whole(operand.shape) for oper...]
    all_gather x1, blocking collectives: 29.3 us -> 18.5 us  [on_device(): every = lax.all_gather(blocks, 'dp', axis=0, tiled=False)]
    all_to_all x0 -> x1, starting transfers between devices: none -> 10.2 us  [on_device(): shares = lax.all_to_all(grads, 'dp', 0, 0, tiled=True)]
    pallas_call x2 -> x5, Pallas kernels: 5.36 us -> 14.9 us  [the longest x2 9.93 us: block_call(): pl.pallas_call(kernel, name=name, grid_spec=pltpu.PrefetchScalarGridSpec(...]
    all_to_all x3 -> x2, waiting for transfers between devices: 21.6 us -> 28.7 us  [exchange(): return lax.all_to_all(value, 'lat', split_axis=0, concat_axis=0, tiled=True)]
    all_to_all x3 -> x2, starting transfers between devices: 24.1 us -> 19 us  [exchange(): return lax.all_to_all(value, 'lat', split_axis=0, concat_axis=0, tiled=True)]
  transfers between devices with their start and end apart: 3 -> 3, of which waited for: 2 -> 2; matrix products, arithmetic and copies ran while one was open for 1% -> 0% of each run, Pallas kernels for 6% -> 7%
where the time goes in v2:
time: 136 us; the launch traced here: 135 us
  blocking collectives  45.8 us (34%)
  waiting for transfers between devices  30.9 us (23%)
  starting transfers between devices  29.2 us (21%)
  Pallas kernels  22.3 us (16%)
  local copies, waits for them, and re-layouts  6.02 us (4%)
    all_to_all x2, waiting for transfers between devices, exchange(): return lax.all_to_all(value, 'lat', split_axis=0, concat_axis=0, tiled=True)  28.7 us
    all_to_all x1, blocking collectives, exchange(): return lax.all_to_all(value, 'lat', split_axis=0, concat_axis=0, tiled=True)  27.3 us
    all_to_all x2, starting transfers between devices, exchange(): return lax.all_to_all(value, 'lat', split_axis=0, concat_axis=0, tiled=True)  19 us
    all_gather x1, blocking collectives, on_device(): every = lax.all_gather(blocks, 'dp', axis=0, tiled=False)  18.5 us
    all_to_all x1, starting transfers between devices, on_device(): shares = lax.all_to_all(grads, 'dp', 0, 0, tiled=True)  10.2 us
    pallas_call x2, Pallas kernels, block_call(): pl.pallas_call(kernel, name=name, grid_spec=pltpu.PrefetchScalarGridSpec(...  9.93 us
    unnamed x30, local copies, waits for them, and re-layouts  6.02 us
    pallas_call x2, Pallas kernels, from_spectra(): pl.pallas_call(kernel, name=name, grid=(ROWS,), in_specs=[pl.BlockSpec((B...  5.95 us
  transfers between devices with their start and end apart: 3, of which 2 were waited for; matrix products, arithmetic and copies ran while one was open for 0% of the time, Pallas kernels for 7%

profile of v2, /device:TPU:1, one launch (start us, length us, event | category | flops | bytes accessed | tf_op | source)
XLA Modules:
  0.0 135.0 jit_solution(522515460470716940)
XLA Ops:
  0.6 0.0 copy-start
  0.6 1.1 copy-done
  1.8 1.2 copy-done.2
  2.9 0.8 copy-done.4
  3.8 0.8 copy-done.5
  4.6 4.8 %to_spectra.1 = bf16[32,144,128]{2,1,0:T(8,128)(2,1)} custom-call(bf16[1,3,180,768]{3,2,1,0:T(8,128)(2,1)S(1)} %copy-done, bf16[1,3,180,768]{3,2,1,0:T(8,128)(2,1)S(1)} %copy-done.2, bf16[128,192]{1,0:T(8,128)(2,1)S(1)} %copy-done.4, bf16[128,192]{1,0:T(8,128)(2,1)S(1)} %copy-done.5), custom_call_target="tpu_custom_call" | custom-call | flops 212336640 | bytes 3000000 | tf_op jit(solution)/shard_map/to_spectra/pallas_call | solution.py:163
  9.5 13.8 %all-to-all-start = ((bf16[32,144,128]{2,1,0:T(8,128)(2,1)}), bf16[32,144,128]{2,1,0:T(8,128)(2,1)S(1)}, u32[]{:S(2)}, u32[]{:S(2)}) async-start(bf16[32,144,128]{2,1,0:T(8,128)(2,1)} %to_spectra.1), calls=%async_computation | async-start | bytes 2359296 | tf_op jit(solution)/shard_map/all_to_all | solution.py:555
  23.4 28.7 %all-to-all-done.recv_ref = bf16[32,144,128]{2,1,0:T(8,128)(2,1)S(1)} async-done(((bf16[32,144,128]{2,1,0:T(8,128)(2,1)}), bf16[32,144,128]{2,1,0:T(8,128)(2,1)S(1)}, u32[]{:S(2)}, u32[]{:S(2)}) %all-to-all-start) | async-done | bytes 1179680 | tf_op jit(solution)/shard_map/all_to_all | solution.py:555
  52.0 0.0 copy-start.11
  52.0 4.8 %spectral_grads.1 = (bf16[1536,256]{1,0:T(8,128)(2,1)S(1)}, bf16[1536,256]{1,0:T(8,128)(2,1)S(1)}, bf16[16,24,128]{2,1,0:T(8,128)(2,1)}) custom-call(s32[1]{0:T(128)} %bitcast.block_ref, bf16[32,144,128]{2,1,0:T(8,128)(2,1)S(1)} %all-to-all-done.recv_ref, bf16[192,192]{1,0:T(8,128)(2,1)S(1)} %copy-done.12, bf16[2,8,96,96]{3,2,1,0:T(8,128)(2,1)S(1)} %copy-done.8, ...), custom_call_target="tpu_custom_call" | custom-call | flops 1000000000 | bytes 6000000 | tf_op jit(solution)/shard_map/spectral_grads/pallas_call | solution.py:357
  56.9 0.9 copy-done.13
  57.7 10.2 %all-to-all-start.1 = ((bf16[16,24,128]{2,1,0:T(8,128)(2,1)}), bf16[16,24,128]{2,1,0:T(8,128)(2,1)S(1)}, u32[]{:S(2)}, u32[]{:S(2)}) async-start(bf16[16,24,128]{2,1,0:T(8,128)(2,1)} %get-tuple-element.20), calls=%async_computation.1 | async-start | bytes 196608 | tf_op jit(solution)/shard_map/all_to_all | solution.py:580
  67.9 0.0 copy-start.14
  68.0 1.1 copy-done.14
  69.1 5.1 %spectral_return.1 = (bf16[32,96,128]{2,1,0:T(8,128)(2,1)S(1)}, bf16[32,72,128]{2,1,0:T(8,128)(2,1)}) custom-call(s32[1]{0:T(128)} %bitcast.block_ref, bf16[1536,256]{1,0:T(8,128)(2,1)S(1)} %get-tuple-element.17.hidden_ref, bf16[1536,256]{1,0:T(8,128)(2,1)S(1)} %copy-done.14, bf16[192,192]{1,0:T(8,128)(2,1)S(1)} %copy-done.12, ...), custom_call_target="tpu_custom_call" | custom-call | flops 1000000000 | bytes 6000000 | tf_op jit(solution)/shard_map/spectral_return/pallas_call | solution.py:357
  74.2 2.2 %all-to-all-done.1.recv_ref = bf16[16,24,128]{2,1,0:T(8,128)(2,1)S(1)} async-done(((bf16[16,24,128]{2,1,0:T(8,128)(2,1)}), bf16[16,24,128]{2,1,0:T(8,128)(2,1)S(1)}, u32[]{:S(2)}, u32[]{:S(2)}) %all-to-all-start.1) | async-done | bytes 98336 | tf_op jit(solution)/shard_map/all_to_all | solution.py:580
  76.4 0.1 grad_share.1
  76.4 27.3 %all_to_all.20.recv_ref = bf16[32,96,128]{2,1,0:T(8,128)(2,1)S(1)} all-to-all(bf16[32,96,128]{2,1,0:T(8,128)(2,1)S(1)} %grad_share.1), channel_id=1, replica_groups=mesh['dp'=16,'lat'=32] {'lat'}, dimensions={0} | all-to-all | bytes 1572864 | tf_op jit(solution)/shard_map/all_to_all | solution.py:555
  103.8 5.2 %all-to-all-start.3 = ((bf16[32,72,128]{2,1,0:T(8,128)(2,1)}), bf16[32,72,128]{2,1,0:T(8,128)(2,1)S(1)}, u32[]{:S(2)}, u32[]{:S(2)}) async-start(bf16[32,72,128]{2,1,0:T(8,128)(2,1)} %get-tuple-element.23), calls=%async_computation.3 | async-start | bytes 1179648 | tf_op jit(solution)/shard_map/all_to_all | solution.py:555
  109.0 2.8 %output.1 = bf16[1,3,180,768]{3,2,1,0:T(8,128)(2,1)} custom-call(bf16[32,96,128]{2,1,0:T(8,128)(2,1)S(1)} %all_to_all.20.recv_ref, bf16[1,3,180,768]{3,2,1,0:T(8,128)(2,1)S(1)} %copy-done.1, bf16[192,128]{1,0:T(8,128)(2,1)S(1)} %copy-done.7), custom_call_target="tpu_custom_call" | custom-call | flops 106168320 | bytes 3000000 | tf_op jit(solution)/shard_map/output/pallas_call | solution.py:440
  111.9 18.5 %all-gather = bf16[128,24,128]{2,1,0:T(8,128)(2,1)S(1)} all-gather(bf16[8,24,128]{2,1,0:T(8,128)(2,1)S(1)} %grad_groups.1), channel_id=2, replica_groups=mesh['dp'=16,'lat'=32] {'dp'}, dimensions={0}, use_global_device_ids=true | all-gather | bytes 835584 | tf_op jit(solution)/shard_map/all_gather | solution.py:599
  130.4 1.5 %grad_out.1 = (f32[2,8,96,96]{3,2,1,0:T(8,128)}, f32[2,768]{1,0:T(2,128)}, f32[2,8,96,96]{3,2,1,0:T(8,128)}, f32[2,768]{1,0:T(2,128)}) custom-call(bf16[16,8,24,128]{3,2,1,0:T(8,128)(2,1)S(1)} %bitcast.2), custom_call_target="tpu_custom_call" | custom-call | flops 1000000000 | bytes 6000000 | tf_op jit(solution)/shard_map/grad_out/pallas_call | solution.py:465
  131.9 0.0 all-to-all-done.3.recv_ref
  131.9 3.1 %fields_grad.1 = bf16[1,3,180,768]{3,2,1,0:T(8,128)(2,1)} custom-call(bf16[32,72,128]{2,1,0:T(8,128)(2,1)S(1)} %all-to-all-done.3.recv_ref, bf16[1,3,180,768]{3,2,1,0:T(8,128)(2,1)S(1)} %copy-done.1, bf16[1,3,180,768]{3,2,1,0:T(8,128)(2,1)S(1)} %copy-done.3, bf16[192,128]{1,0:T(8,128)(2,1)S(1)} %copy-done.6), custom_call_target="tpu_custom_call" | custom-call | flops 106168320 | bytes 3000000 | tf_op jit(solution)/shard_map/fields_grad/pallas_call | solution.py:440
  (22 shorter events, 0.1 us)
Async XLA Ops:
  0.6 1.2 copy-start
  1.8 1.2 copy-start.2
  2.9 0.8 copy-start.4
  3.8 0.8 copy-start.5
  9.5 42.5 %copy-start.8 = (bf16[2,8,96,96]{3,2,1,0:T(8,128)(2,1)S(1)}, bf16[2,8,96,96]{3,2,1,0:T(8,128)(2,1)}, u32[]{:S(2)}) copy-start(bf16[2,8,96,96]{3,2,1,0:T(8,128)(2,1)} %first_ref.3) | copy-start | bytes 884740
  9.5 42.5 %copy-start.9 = (bf16[2,8,96,96]{3,2,1,0:T(8,128)(2,1)S(1)}, bf16[2,8,96,96]{3,2,1,0:T(8,128)(2,1)}, u32[]{:S(2)}) copy-start(bf16[2,8,96,96]{3,2,1,0:T(8,128)(2,1)} %second_ref.3) | copy-start | bytes 884740
  9.5 42.5 %copy-start.10 = (f32[2,768]{1,0:T(2,128)S(1)}, f32[2,768]{1,0:T(2,128)}, u32[]{:S(2)}) copy-start(f32[2,768]{1,0:T(2,128)} %bias_ref.2) | copy-start | bytes 18436
  9.5 42.5 %copy-start.12 = (bf16[192,192]{1,0:T(8,128)(2,1)S(1)}, bf16[192,192]{1,0:T(8,128)(2,1)}, u32[]{:S(2)}) copy-start(bf16[192,192]{1,0:T(8,128)(2,1)} %constant.34.clone.lat_ref) | copy-start | bytes 221188
  9.5 42.5 %all-to-all-start = ((bf16[32,144,128]{2,1,0:T(8,128)(2,1)}), bf16[32,144,128]{2,1,0:T(8,128)(2,1)S(1)}, u32[]{:S(2)}, u32[]{:S(2)}) async-start(bf16[32,144,128]{2,1,0:T(8,128)(2,1)} %to_spectra.1), calls=%async_computation | async-start | bytes 2359296 | tf_op jit(solution)/shard_map/all_to_all | solution.py:555
  52.0 15.9 %copy-start.11 = (f32[2,768]{1,0:T(2,128)S(1)}, f32[2,768]{1,0:T(2,128)}, u32[]{:S(2)}) copy-start(f32[2,768]{1,0:T(2,128)} %bias_ref.3) | copy-start | bytes 18436
  56.9 0.9 copy-start.13
  57.7 18.7 %all-to-all-start.1 = ((bf16[16,24,128]{2,1,0:T(8,128)(2,1)}), bf16[16,24,128]{2,1,0:T(8,128)(2,1)S(1)}, u32[]{:S(2)}, u32[]{:S(2)}) async-start(bf16[16,24,128]{2,1,0:T(8,128)(2,1)} %get-tuple-element.20), calls=%async_computation.1 | async-start | bytes 196608 | tf_op jit(solution)/shard_map/all_to_all | solution.py:580
  67.9 1.1 copy-start.14
  103.8 5.2 %copy-start.1 = (bf16[1,3,180,768]{3,2,1,0:T(8,128)(2,1)S(1)}, bf16[1,3,180,768]{3,2,1,0:T(8,128)(2,1)}, u32[]{:S(2)}) copy-start(bf16[1,3,180,768]{3,2,1,0:T(8,128)(2,1)} %x_ref.5) | copy-start | bytes 2488324
  103.8 5.2 %copy-start.7 = (bf16[192,128]{1,0:T(8,128)(2,1)S(1)}, bf16[192,128]{1,0:T(8,128)(2,1)}, u32[]{:S(2)}) copy-start(bf16[192,128]{1,0:T(8,128)(2,1)} %constant.31.clone.table_ref) | copy-start | bytes 147460
  103.8 28.1 %all-to-all-start.3 = ((bf16[32,72,128]{2,1,0:T(8,128)(2,1)}), bf16[32,72,128]{2,1,0:T(8,128)(2,1)S(1)}, u32[]{:S(2)}, u32[]{:S(2)}) async-start(bf16[32,72,128]{2,1,0:T(8,128)(2,1)} %get-tuple-element.23), calls=%async_computation.3 | async-start | bytes 1179648 | tf_op jit(solution)/shard_map/all_to_all | solution.py:555
  130.4 1.5 %copy-start.3 = (bf16[1,3,180,768]{3,2,1,0:T(8,128)(2,1)S(1)}, bf16[1,3,180,768]{3,2,1,0:T(8,128)(2,1)}, u32[]{:S(2)}) copy-start(bf16[1,3,180,768]{3,2,1,0:T(8,128)(2,1)} %g_ref.3) | copy-start | bytes 2488324
  130.4 1.5 %copy-start.6 = (bf16[192,128]{1,0:T(8,128)(2,1)S(1)}, bf16[192,128]{1,0:T(8,128)(2,1)}, u32[]{:S(2)}) copy-start(bf16[192,128]{1,0:T(8,128)(2,1)} %constant.30.clone.table_ref) | copy-start | bytes 147460

commit v3 on v2

--- a/solution.py
+++ b/solution.py
@@ -27,7 +27,7 @@
 CHUNK_ROWS = 24
 BF = jnp.bfloat16
 F32 = jnp.float32
-VMEM_LIMIT = 16 * 1024 * 1024
+VMEM_LIMIT = 10 * 1024 * 1024
 
 
 def tables():
@@ -128,59 +128,63 @@
             ).astype(BF)
 
 
-def spectra_kernel(x_ref, g_ref, fwd_ref, inv_ref, out_ref, padded_ref, acc_ref):
-    step = pl.program_id(0)
-
-    @pl.when(step == 0)
-    def _():
-        padded_ref[...] = jnp.zeros_like(padded_ref)
-
-    @pl.when(step < ROWS)
-    def _():
+def spectra_kernel(
+    x_ref, g_ref, fwd_ref, inv_ref, out_ref,
+    x_rows, g_rows, fwd_table, inv_table, padded_ref, acc_ref, sems,
+):
+    copies = [pltpu.make_async_copy(x_ref.at[0, 0], x_rows.at[0], sems.at[0])]
+    copies += [pltpu.make_async_copy(fwd_ref, fwd_table, sems.at[1])]
+    copies += [
+        pltpu.make_async_copy(x_ref.at[0, r], x_rows.at[r], sems.at[1 + r])
+        for r in range(1, ROWS)
+    ]
+    copies += [pltpu.make_async_copy(inv_ref, inv_table, sems.at[1 + ROWS])]
+    copies += [
+        pltpu.make_async_copy(g_ref.at[0, r], g_rows.at[r], sems.at[2 + ROWS + r])
+        for r in range(ROWS)
+    ]
+    for copy in copies:
+        copy.start()
+    padded_ref[W - 20 :] = jnp.zeros((WPAD - W + 20, C), BF)
+    for r in range(ROWS):
+        copies[0 if r == 0 else 1 + r].wait()
         for start, size in ROW_CHUNKS:
-            values = x_ref[0, 0, start : start + size].astype(F32)
+            values = x_rows[r, start : start + size].astype(F32)
             padded_ref[start : start + size] = normalize(values)[0].astype(BF)
-        acc_ref[step] = jnp.dot(fwd_ref[...], padded_ref[...], preferred_element_type=F32)
-
-    @pl.when(step == ROWS - 1)
-    def _():
-        send_packed(acc_ref, out_ref, 0)
-
-    @pl.when(step >= ROWS)
-    def _():
-        padded_ref[0:W] = g_ref[0, 0]
-        acc_ref[step - ROWS] = jnp.dot(
-            inv_ref[...], padded_ref[...], preferred_element_type=F32
-        )
-
-    @pl.when(step == 2 * ROWS - 1)
-    def _():
-        send_packed(acc_ref, out_ref, PACK)
+        if r == 0:
+            copies[1].wait()
+        acc_ref[r] = jnp.dot(fwd_table[...], padded_ref[...], preferred_element_type=F32)
+    send_packed(acc_ref, out_ref, 0)
+    copies[1 + ROWS].wait()
+    for r in range(ROWS):
+        copies[2 + ROWS + r].wait()
+        padded_ref[0:W] = g_rows[r]
+        acc_ref[r] = jnp.dot(inv_table[...], padded_ref[...], preferred_element_type=F32)
+    send_packed(acc_ref, out_ref, PACK)
 
 
 def to_spectra(fields, cotangent, forward, inverse):
-    table_spec = pl.BlockSpec((2 * KX, WPAD), lambda r: (0, 0))
+    held = pl.BlockSpec(memory_space=pltpu.HBM)
     return pl.pallas_call(
         spectra_kernel,
         name="to_spectra",
-        grid=(2 * ROWS,),
-        in_specs=[
-            pl.BlockSpec((1, 1, W, C), lambda r: (0, jnp.minimum(r, ROWS - 1), 0, 0)),
-            pl.BlockSpec((1, 1, W, C), lambda r: (0, jnp.maximum(r - ROWS, 0), 0, 0)),
-            table_spec,
-            table_spec,
-        ],
-        out_specs=pl.BlockSpec((BANDS, 2 * PACK, 128), lambda r: (0, 0, 0)),
+        in_specs=[held, held, held, held],
+        out_specs=pl.BlockSpec(memory_space=pltpu.VMEM),
         out_shape=jax.ShapeDtypeStruct((BANDS, 2 * PACK, 128), BF),
         scratch_shapes=[
+            pltpu.VMEM((ROWS, W, C), BF),
+            pltpu.VMEM((ROWS, W, C), BF),
+            pltpu.VMEM((2 * KX, WPAD), BF),
+            pltpu.VMEM((2 * KX, WPAD), BF),
             pltpu.VMEM((WPAD, C), BF),
             pltpu.VMEM((ROWS, 2 * KX, C), F32),
+            pltpu.SemaphoreType.DMA((2 + 2 * ROWS,)),
         ],
         compiler_params=pltpu.CompilerParams(vmem_limit_bytes=VMEM_LIMIT),
         cost_estimate=pl.CostEstimate(
             flops=4 * ROWS * W * 2 * KX * C, bytes_accessed=3000000, transcendentals=0
         ),
-    )(fields, cotangent, forward, inverse)
+    )(*[pltpu.with_memory_space_constraint(a, pltpu.HBM) for a in (fields, cotangent, forward, inverse)])
 
 
 TILE_ROWS = 2 * ROWS * MODES
@@ -201,11 +205,11 @@
     lax.fori_loop(0, BANDS, one, 0, unroll=4)
 
 
-def pack_bands(rows_ref, out_ref):
+def pack_bands(rows_ref, first, out_ref):
     def one(s, carry):
         base = pl.multiple_of(s * TILE_ROWS, TILE_ROWS)
         pieces = pack_tile(rows_ref[pl.ds(base, TILE_ROWS), :])
-        out_ref[s, 0:PACK] = jnp.concatenate(pieces, axis=0).astype(BF)
+        out_ref[s, first : first + PACK] = jnp.concatenate(pieces, axis=0).astype(BF)
         return carry
 
     lax.fori_loop(0, BANDS, one, 0, unroll=4)
@@ -278,7 +282,7 @@
 
 def gradient_kernel(
     block_ref, recv_ref, lat_ref, first_ref, bias_ref, second_ref,
-    hidden_ref, pre_ref, grad_ref,
+    kept_ref, grad_ref,
     w1_ref, w2_ref, rows_ref, back_rows_ref, modes_ref, filtered_ref, sums_ref,
 ):
     fill_weight(first_ref, w1_ref)
@@ -295,16 +299,16 @@
         modes_ref[span] = modes
         pre = jnp.dot(modes, w1, preferred_element_type=F32) + bias
         cdf = 0.5 + 0.5 * lax.erf(pre * math.sqrt(0.5))
-        hidden_ref[span] = (pre * cdf).astype(BF)
+        kept_ref[0, span] = (pre * cdf).astype(BF)
         slope = cdf + pre * (jnp.exp(-0.5 * pre * pre) * (1.0 / math.sqrt(2.0 * math.pi)))
         back_filtered = mode_rows(back_rows_ref, lat, pair)
         filtered_ref[span] = back_filtered
         back_hidden = lax.dot_general(back_filtered, w2, NT, preferred_element_type=F32)
-        pre_ref[span] = (back_hidden * slope).astype(BF)
+        kept_ref[1, span] = (back_hidden * slope).astype(BF)
     ones = jnp.ones((8, MODES * H), BF)
     row = 0
     bias_rows = []
-    for left_ref, right_ref in ((modes_ref, pre_ref), (hidden_ref, filtered_ref)):
+    for left_ref, right_ref in ((modes_ref, kept_ref.at[1]), (kept_ref.at[0], filtered_ref)):
         right = right_ref[...]
         gathered = lax.dot_general(left_ref[...], right, TN, preferred_element_type=F32)
         real = gathered[0:BS, 0:128] + gathered[128 : 128 + BS, 128:256]
@@ -326,8 +330,8 @@
 
 
 def return_kernel(
-    block_ref, hidden_ref, pre_ref, lat_ref, first_ref, second_ref, bias_ref,
-    row_ref, back_ref,
+    block_ref, kept_ref, lat_ref, first_ref, second_ref, bias_ref,
+    out_ref,
     w1_ref, w2_ref, rows_ref, back_rows_ref,
 ):
     fill_weight(first_ref, w1_ref)
@@ -338,12 +342,12 @@
     w2 = w2_ref[...]
     for pair in range(PAIRS):
         span = slice(PAIR_ROWS * pair, PAIR_ROWS * pair + PAIR_ROWS)
-        filtered = jnp.dot(hidden_ref[span], w2, preferred_element_type=F32) + bias
+        filtered = jnp.dot(kept_ref[0, span], w2, preferred_element_type=F32) + bias
         store_rows(rows_ref, lat, pair, filtered.astype(BF))
-        back_modes = lax.dot_general(pre_ref[span], w1, NT, preferred_element_type=F32)
+        back_modes = lax.dot_general(kept_ref[1, span], w1, NT, preferred_element_type=F32)
         store_rows(back_rows_ref, lat, pair, back_modes.astype(BF))
-    pack_bands(rows_ref, row_ref)
-    pack_bands(back_rows_ref, back_ref)
+    pack_bands(rows_ref, 0, out_ref)
+    pack_bands(back_rows_ref, PACK, out_ref)
 
 
 PAIR_ROWS = 2 * H
@@ -373,21 +377,22 @@
             scratch_shapes=scratch,
         ),
         out_shape=outs,
-        compiler_params=pltpu.CompilerParams(vmem_limit_bytes=24 * 1024 * 1024),
+        compiler_params=pltpu.CompilerParams(vmem_limit_bytes=14 * 1024 * 1024),
         cost_estimate=pl.CostEstimate(
             flops=1000000000, bytes_accessed=6000000, transcendentals=800000
         ),
     )(block, *operands)
 
 
-def receive(recv_ref, rows_ref):
+def receive(recv_ref, first, rows_ref):
     for group in range(GROUPS):
         for quad in range(2):
             tiles = []
             for block in range(4):
                 band = (4 * quad + block) * GROUPS + group
                 pieces = [
-                    recv_ref[band, 24 * i : 24 * i + 24, :].astype(F32) for i in range(3)
+                    recv_ref[band, first + 24 * i : first + 24 * i + 24, :].astype(F32)
+                    for i in range(3)
                 ]
                 tiles.append(jnp.concatenate(pieces + [unpack_tail(pieces)], axis=0))
             for t, joined in enumerate(join_lanes(tiles)):
@@ -399,62 +404,59 @@
                     ] = joined[32 * r : 32 * r + 32].astype(BF)
 
 
-def output_kernel(recv_ref, x_ref, table_ref, out_ref, rows_ref, mixed_ref):
+def output_kernel(
+    recv_ref, x_ref, g_ref, fwd_ref, inv_ref, out_ref, grad_ref,
+    rows_ref, back_rows_ref, mixed_ref, back_ref,
+):
     r = pl.program_id(0)
 
     @pl.when(r == 0)
     def _():
-        receive(recv_ref, rows_ref)
-
-    mixed_ref[...] = jnp.dot(table_ref[...], rows_ref[r], preferred_element_type=F32)
+        receive(recv_ref, 0, rows_ref)
+        receive(recv_ref, PACK, back_rows_ref)
+
+    mixed_ref[...] = jnp.dot(inv_ref[...], rows_ref[r], preferred_element_type=F32)
+    back_ref[...] = jnp.dot(fwd_ref[...], back_rows_ref[r], preferred_element_type=F32)
     for start, size in ROW_CHUNKS:
-        values = x_ref[0, 0, start : start + size].astype(F32)
-        normed = normalize(values)[0]
-        out_ref[0, 0, start : start + size] = (
-            values + normed + mixed_ref[start : start + size]
-        ).astype(BF)
-
-
-def input_grad_kernel(recv_ref, x_ref, g_ref, table_ref, out_ref, rows_ref, mixed_ref):
-    r = pl.program_id(0)
-
-    @pl.when(r == 0)
-    def _():
-        receive(recv_ref, rows_ref)
-
-    mixed_ref[...] = jnp.dot(table_ref[...], rows_ref[r], preferred_element_type=F32)
-    for start, size in ROW_CHUNKS:
-        values = x_ref[0, 0, start : start + size].astype(F32)
-        upstream = g_ref[0, 0, start : start + size].astype(F32)
+        span = slice(start, start + size)
+        values = x_ref[0, 0, span].astype(F32)
         normed, scale = normalize(values)
-        back = upstream + mixed_ref[start : start + size]
+        out_ref[0, 0, span] = (values + normed + mixed_ref[span]).astype(BF)
+        upstream = g_ref[0, 0, span].astype(F32)
+        back = upstream + back_ref[span]
         mean = jnp.sum(back, axis=-1, keepdims=True) * (1.0 / C)
         along = jnp.sum(back * normed, axis=-1, keepdims=True) * (1.0 / C)
-        out_ref[0, 0, start : start + size] = (
-            upstream + scale * (back - mean - normed * along)
-        ).astype(BF)
-
-
-def from_spectra(kernel, name, recv, arrays, table):
+        grad_ref[0, 0, span] = (upstream + scale * (back - mean - normed * along)).astype(BF)
+
+
+def from_spectra(recv, fields, cotangent, forward, inverse):
     token_spec = pl.BlockSpec((1, 1, W, C), lambda r: (0, r, 0, 0))
+    table_spec = pl.BlockSpec((WPAD, 2 * KX), lambda r: (0, 0))
+    token = jax.ShapeDtypeStruct((1, ROWS, W, C), BF)
     return pl.pallas_call(
-        kernel,
-        name=name,
+        output_kernel,
+        name="from_spectra",
         grid=(ROWS,),
-        in_specs=[pl.BlockSpec((BANDS, PACK, 128), lambda r: (0, 0, 0))]
-        + [token_spec] * len(arrays)
-        + [pl.BlockSpec((WPAD, 2 * KX), lambda r: (0, 0))],
-        out_specs=token_spec,
-        out_shape=jax.ShapeDtypeStruct((1, ROWS, W, C), BF),
+        in_specs=[
+            pl.BlockSpec((BANDS, 2 * PACK, 128), lambda r: (0, 0, 0)),
+            token_spec,
+            token_spec,
+            table_spec,
+            table_spec,
+        ],
+        out_specs=[token_spec, token_spec],
+        out_shape=[token, token],
         scratch_shapes=[
             pltpu.VMEM((ROWS, 2 * KX, C), BF),
+            pltpu.VMEM((ROWS, 2 * KX, C), BF),
+            pltpu.VMEM((WPAD, C), F32),
             pltpu.VMEM((WPAD, C), F32),
         ],
         compiler_params=pltpu.CompilerParams(vmem_limit_bytes=VMEM_LIMIT),
         cost_estimate=pl.CostEstimate(
-            flops=2 * ROWS * W * 2 * KX * C, bytes_accessed=3000000, transcendentals=0
+            flops=4 * ROWS * W * 2 * KX * C, bytes_accessed=5000000, transcendentals=0
         ),
-    )(recv, *arrays, table)
+    )(recv, fields, cotangent, forward, inverse)
 
 
 def whole(shape):
@@ -471,12 +473,12 @@
         scratch_shapes=scratch,
         compiler_params=pltpu.CompilerParams(vmem_limit_bytes=VMEM_LIMIT),
         cost_estimate=pl.CostEstimate(
-            flops=1000000000, bytes_accessed=6000000, transcendentals=800000
+            flops=1000000, bytes_accessed=1000000, transcendentals=0
         ),
     )(*operands)
 
 
-def share_kernel(recv_ref, held_ref, out_ref):
+def share_kernel(recv_ref, out_ref):
     total = recv_ref[0].astype(F32)
     for i in range(1, recv_ref.shape[0]):
         total = total + recv_ref[i].astype(F32)
@@ -485,40 +487,12 @@
         out_ref[band] = share
 
 
-def add_share(shares, held):
-    return pl.pallas_call(
-        share_kernel,
-        name="grad_share",
-        grid=(1,),
-        in_specs=[
-            pl.BlockSpec(shares.shape, lambda i: (0, 0, 0)),
-            pl.BlockSpec(memory_space=pl.ANY),
-        ],
-        out_specs=pl.BlockSpec((BANDS, CHUNK_ROWS, 128), lambda i: (0, 3, 0)),
-        out_shape=jax.ShapeDtypeStruct(held.shape, BF),
-        input_output_aliases={1: 0},
-        compiler_params=pltpu.CompilerParams(vmem_limit_bytes=VMEM_LIMIT),
-    )(shares, held)
-
-
 def group_sum_kernel(recv_ref, out_ref):
     for block in range(NB):
         total = recv_ref[block * GROUPS].astype(F32)
         for group in range(1, GROUPS):
             total = total + recv_ref[block * GROUPS + group].astype(F32)
         out_ref[block] = total.astype(BF)
-
-
-def group_sums(message):
-    return pl.pallas_call(
-        group_sum_kernel,
-        name="grad_groups",
-        grid=(1,),
-        in_specs=[pl.BlockSpec((BANDS, CHUNK_ROWS, 128), lambda i: (0, 3, 0))],
-        out_specs=pl.BlockSpec((NB, CHUNK_ROWS, 128), lambda i: (0, 0, 0)),
-        out_shape=jax.ShapeDtypeStruct((NB, CHUNK_ROWS, 128), BF),
-        compiler_params=pltpu.CompilerParams(vmem_limit_bytes=VMEM_LIMIT),
-    )(message)
 
 
 GRAD_SCALE = 1.0 / (SAMPLES * H)
@@ -564,14 +538,13 @@
     lat = jnp.asarray(LAT, BF)
 
     spectra = exchange(to_spectra(fields, cotangent, lon_fwd_t, lon_inv_t))
-    wide = jax.ShapeDtypeStruct(WIDE, BF)
-    hidden, pre, grads = block_call(
+    kept, grads = block_call(
         gradient_kernel,
         "spectral_grads",
         block,
         (spectra, lat, w_first, b_first, w_second),
         ("", "", "weight", "", "weight"),
-        [wide, wide, jax.ShapeDtypeStruct((CHUNKS, CHUNK_ROWS, 128), BF)],
+        [jax.ShapeDtypeStruct((2,) + WIDE, BF), jax.ShapeDtypeStruct((CHUNKS, CHUNK_ROWS, 128), BF)],
         [FORM, FORM, BAND_ROWS, BAND_ROWS, pltpu.VMEM(WIDE, BF), pltpu.VMEM(WIDE, BF)]
         + [pltpu.VMEM((CHUNKS * CHUNK_ROWS, 128), F32)],
     )
@@ -580,32 +553,41 @@
         shares = lax.all_to_all(grads, "dp", 0, 0, tiled=True)
     else:
         shares = grads
-    row_send, back_send = block_call(
+    send = block_call(
         return_kernel,
         "spectral_return",
         block,
-        (hidden, pre, lat, w_first, w_second, b_second),
-        ("", "", "", "weight", "weight", ""),
-        [
-            jax.ShapeDtypeStruct((BANDS, PACK + CHUNK_ROWS, 128), BF),
-            jax.ShapeDtypeStruct((BANDS, PACK, 128), BF),
-        ],
+        (kept, lat, w_first, w_second, b_second),
+        ("", "", "weight", "weight", ""),
+        [jax.ShapeDtypeStruct((BANDS, 2 * PACK, 128), BF)],
         [FORM, FORM, BAND_ROWS, BAND_ROWS],
-    )
-    message = exchange(add_share(shares, row_send))
-    back_send, message = lax.optimization_barrier((back_send, message))
-    back_spectra = exchange(back_send)
-    blocks = group_sums(message)
+    )[0]
+    share = spectral_call(
+        share_kernel,
+        "grad_share",
+        (shares,),
+        [jax.ShapeDtypeStruct((BANDS, CHUNK_ROWS, 128), BF)],
+        [],
+    )[0]
+    banded = exchange(share)
+    send, banded = lax.optimization_barrier((send, banded))
+    returned = exchange(send)
+    blocks = spectral_call(
+        group_sum_kernel,
+        "grad_groups",
+        (banded,),
+        [jax.ShapeDtypeStruct((NB, CHUNK_ROWS, 128), BF)],
+        [],
+    )[0]
     every = lax.all_gather(blocks, "dp", axis=0, tiled=False)
+    if dp_size != CHUNKS:
+        every = jnp.broadcast_to(every, (CHUNKS, NB, CHUNK_ROWS, 128))
     grad_w = jax.ShapeDtypeStruct((2, NB, BS, BS), F32)
     grad_b = jax.ShapeDtypeStruct((2, C), F32)
     g_w1, g_b1, g_w2, g_b2 = spectral_call(
         grads_kernel, "grad_out", (every,), [grad_w, grad_b, grad_w, grad_b], []
     )
-    result = from_spectra(output_kernel, "output", message, (fields,), lon_inv)
-    back_fields = from_spectra(
-        input_grad_kernel, "fields_grad", back_spectra, (fields, cotangent), lon_fwd
-    )
+    result, back_fields = from_spectra(returned, fields, cotangent, lon_fwd, lon_inv)
     return (result, back_fields, g_w1, g_b1, g_w2, g_b2)
 
 

time: 136 us -> 129 us (0.949)
  waiting for transfers between devices: 30.9 us -> 42.5 us
  blocking collectives: 45.8 us -> 35.9 us
  starting transfers between devices: 29.2 us -> 24.5 us
  local copies, waits for them, and re-layouts: 6.02 us -> 2.63 us
  Pallas kernels: 22.3 us -> 20.7 us
    all_to_all x2 -> x3, waiting for transfers between devices: 28.7 us -> 42.5 us  [exchange(): return lax.all_to_all(value, 'lat', split_axis=0, concat_axis=0, tiled=True)]
    all_to_all x1 -> x0, starting transfers between devices: 10.2 us -> none  [on_device(): shares = lax.all_to_all(grads, 'dp', 0, 0, tiled=True)]
    all_to_all x1, blocking collectives: 27.3 us -> 18.5 us  [on_device(): shares = lax.all_to_all(grads, 'dp', 0, 0, tiled=True)]
    all_to_all x2 -> x3, starting transfers between devices: 19 us -> 24.5 us  [exchange(): return lax.all_to_all(value, 'lat', split_axis=0, concat_axis=0, tiled=True)]
    unnamed x30 -> x22, local copies, waits for them, and re-layouts: 6.02 us -> 2.63 us
    all_to_all x1 -> x0, waiting for transfers between devices: 2.2 us -> none  [on_device(): shares = lax.all_to_all(grads, 'dp', 0, 0, tiled=True)]
    pallas_call x5 -> x2, Pallas kernels: 10.9 us -> 8.94 us  [the longest x1 4.92 us: to_spectra(): pl.pallas_call(spectra_kernel, name='to_spectra', in_specs=[held, held, h...]
  transfers between devices with their start and end apart: 3 -> 3, of which waited for: 2 -> 3; matrix products, arithmetic and copies ran while one was open for 0% -> 0% of each run, Pallas kernels for 7% -> 5%
where the time goes in v3:
time: 129 us; the launch traced here: 127 us
  waiting for transfers between devices  42.5 us (33%)
  blocking collectives  35.9 us (28%)
  starting transfers between devices  24.5 us (19%)
  Pallas kernels  20.7 us (16%)
  local copies, waits for them, and re-layouts  2.63 us (2%)
    all_to_all x3, waiting for transfers between devices, exchange(): return lax.all_to_all(value, 'lat', split_axis=0, concat_axis=0, tiled=True)  42.5 us
    all_to_all x3, starting transfers between devices, exchange(): return lax.all_to_all(value, 'lat', split_axis=0, concat_axis=0, tiled=True)  24.5 us
    all_to_all x1, blocking collectives, on_device(): shares = lax.all_to_all(grads, 'dp', 0, 0, tiled=True)  18.5 us
    all_gather x1, blocking collectives, on_device(): every = lax.all_gather(blocks, 'dp', axis=0, tiled=False)  17.4 us
    pallas_call x2, Pallas kernels, block_call(): pl.pallas_call(kernel, name=name, grid_spec=pltpu.PrefetchScalarGridSpec(...  9.55 us
    pallas_call x1, Pallas kernels, to_spectra(): pl.pallas_call(spectra_kernel, name='to_spectra', in_specs=[held, held, h...  4.92 us
    pallas_call x1, Pallas kernels, from_spectra(): pl.pallas_call(output_kernel, name='from_spectra', grid=(ROWS,), in_specs...  4.01 us
    unnamed x22, local copies, waits for them, and re-layouts  2.63 us
  transfers between devices with their start and end apart: 3, of which 3 were waited for; matrix products, arithmetic and copies ran while one was open for 0% of the time, Pallas kernels for 5%

profile of v3, /device:TPU:1, one launch (start us, length us, event | category | flops | bytes accessed | tf_op | source)
XLA Modules:
  0.0 127.1 jit_solution(12271747444139891081)
XLA Ops:
  0.6 4.9 %to_spectra.1 = bf16[32,144,128]{2,1,0:T(8,128)(2,1)} custom-call(bf16[1,3,180,768]{3,2,1,0:T(8,128)(2,1)} %x_ref.3, bf16[1,3,180,768]{3,2,1,0:T(8,128)(2,1)} %g_ref.3, bf16[128,192]{1,0:T(8,128)(2,1)} %constant.32.clone.fwd_ref, bf16[128,192]{1,0:T(8,128)(2,1)} %constant.33.clone.inv_ref), custom_call_target="tpu_custom_call" | custom-call | flops 212336640 | bytes 3000000 | tf_op jit(solution)/shard_map/to_spectra/pallas_call | solution.py:168
  5.6 0.0 copy-start.4
  5.6 0.0 copy-start.5
  5.6 0.0 copy-start.8
  5.6 13.8 %all-to-all-start = ((bf16[32,144,128]{2,1,0:T(8,128)(2,1)}), bf16[32,144,128]{2,1,0:T(8,128)(2,1)S(1)}, u32[]{:S(2)}, u32[]{:S(2)}) async-start(bf16[32,144,128]{2,1,0:T(8,128)(2,1)} %to_spectra.1), calls=%async_computation | async-start | bytes 2359296 | tf_op jit(solution)/shard_map/all_to_all | solution.py:529
  19.5 28.6 %all-to-all-done.recv_ref = bf16[32,144,128]{2,1,0:T(8,128)(2,1)S(1)} async-done(((bf16[32,144,128]{2,1,0:T(8,128)(2,1)}), bf16[32,144,128]{2,1,0:T(8,128)(2,1)S(1)}, u32[]{:S(2)}, u32[]{:S(2)}) %all-to-all-start) | async-done | bytes 1179680 | tf_op jit(solution)/shard_map/all_to_all | solution.py:529
  48.1 0.0 copy-start.7
  48.1 4.2 %spectral_grads.1 = (bf16[2,1536,256]{2,1,0:T(8,128)(2,1)S(1)}, bf16[16,24,128]{2,1,0:T(8,128)(2,1)S(1)}) custom-call(s32[1]{0:T(128)} %bitcast.block_ref, bf16[32,144,128]{2,1,0:T(8,128)(2,1)S(1)} %all-to-all-done.recv_ref, bf16[192,192]{1,0:T(8,128)(2,1)S(1)} %copy-done.8, bf16[2,8,96,96]{3,2,1,0:T(8,128)(2,1)S(1)} %copy-done.4, f32[2,768]{1,0:T(2,128)S(1)} %copy-done.6, ...), custom_call_target="tpu_custom_call" | custom-call | flops 1000000000 | bytes 6000000 | tf_op jit(solution)/shard_map/spectral_grads/pallas_call | solution.py:361
  52.4 1.2 copy-done.9
  53.5 18.5 %all_to_all.20.recv_ref = bf16[16,24,128]{2,1,0:T(8,128)(2,1)S(1)} all-to-all(bf16[16,24,128]{2,1,0:T(8,128)(2,1)S(1)} %get-tuple-element.17), channel_id=1, replica_groups=mesh['dp'=16,'lat'=32] {'dp'}, dimensions={0} | all-to-all | bytes 196608 | tf_op jit(solution)/shard_map/all_to_all | solution.py:553
  72.0 0.7 grad_share.1
  72.7 5.4 %all-to-all-start.2 = ((bf16[32,24,128]{2,1,0:T(8,128)(2,1)}), bf16[32,24,128]{2,1,0:T(8,128)(2,1)S(1)}, u32[]{:S(2)}, u32[]{:S(2)}) async-start(bf16[32,24,128]{2,1,0:T(8,128)(2,1)} %grad_share.1), calls=%async_computation.2 | async-start | bytes 393216 | tf_op jit(solution)/shard_map/all_to_all | solution.py:529
  78.1 1.4 %copy-done.10 = bf16[2,1536,256]{2,1,0:T(8,128)(2,1)S(1)} copy-done((bf16[2,1536,256]{2,1,0:T(8,128)(2,1)S(1)}, bf16[2,1536,256]{2,1,0:T(8,128)(2,1)}, u32[]{:S(2)}) %copy-start.10) | copy-done | bytes 1572888
  79.5 5.4 %spectral_return.1 = bf16[32,144,128]{2,1,0:T(8,128)(2,1)} custom-call(s32[1]{0:T(128)} %bitcast.block_ref, bf16[2,1536,256]{2,1,0:T(8,128)(2,1)S(1)} %copy-done.10, bf16[192,192]{1,0:T(8,128)(2,1)S(1)} %copy-done.8, bf16[2,8,96,96]{3,2,1,0:T(8,128)(2,1)S(1)} %copy-done.4, bf16[2,8,96,96]{3,2,1,0:T(8,128)(2,1)S(1)} %copy-done.5, f32[2,768]{1,0:T(2,128)S(1)} %copy-done.7), custom_call_target="tpu_custom_call" | custom-call | flops 1000000000 | bytes 6000000 | tf_op jit(solution)/shard_map/spectral_return/pallas_call | solution.py:361
  84.8 3.9 %all-to-all-done.2.recv_ref = bf16[32,24,128]{2,1,0:T(8,128)(2,1)S(1)} async-done(((bf16[32,24,128]{2,1,0:T(8,128)(2,1)}), bf16[32,24,128]{2,1,0:T(8,128)(2,1)S(1)}, u32[]{:S(2)}, u32[]{:S(2)}) %all-to-all-start.2) | async-done | bytes 196640 | tf_op jit(solution)/shard_map/all_to_all | solution.py:529
  88.8 5.3 %all-to-all-start.3 = ((bf16[32,144,128]{2,1,0:T(8,128)(2,1)}), bf16[32,144,128]{2,1,0:T(8,128)(2,1)S(1)}, u32[]{:S(2)}, u32[]{:S(2)}) async-start(bf16[32,144,128]{2,1,0:T(8,128)(2,1)} %spectral_return.1), calls=%async_computation.3 | async-start | bytes 2359296 | tf_op jit(solution)/shard_map/all_to_all | solution.py:529
  94.1 0.0 copy-start
  94.1 0.0 copy-start.1
  94.1 0.0 copy-start.2
  94.1 0.0 copy-start.3
  94.1 17.4 %all-gather = bf16[128,24,128]{2,1,0:T(8,128)(2,1)S(1)} all-gather(bf16[8,24,128]{2,1,0:T(8,128)(2,1)S(1)} %grad_groups.1), channel_id=2, replica_groups=mesh['dp'=16,'lat'=32] {'dp'}, dimensions={0}, use_global_device_ids=true | all-gather | bytes 835584 | tf_op jit(solution)/shard_map/all_gather | solution.py:582
  111.6 1.5 %grad_out.1 = (f32[2,8,96,96]{3,2,1,0:T(8,128)}, f32[2,768]{1,0:T(2,128)}, f32[2,8,96,96]{3,2,1,0:T(8,128)}, f32[2,768]{1,0:T(2,128)}) custom-call(bf16[16,8,24,128]{3,2,1,0:T(8,128)(2,1)S(1)} %bitcast.2), custom_call_target="tpu_custom_call" | custom-call | flops 1000000 | bytes 1000000 | tf_op jit(solution)/shard_map/grad_out/pallas_call | solution.py:467
  113.1 10.0 %all-to-all-done.3.recv_ref = bf16[32,144,128]{2,1,0:T(8,128)(2,1)S(1)} async-done(((bf16[32,144,128]{2,1,0:T(8,128)(2,1)}), bf16[32,144,128]{2,1,0:T(8,128)(2,1)S(1)}, u32[]{:S(2)}, u32[]{:S(2)}) %all-to-all-start.3) | async-done | bytes 1179680 | tf_op jit(solution)/shard_map/all_to_all | solution.py:529
  123.1 4.0 %from_spectra.1 = (bf16[1,3,180,768]{3,2,1,0:T(8,128)(2,1)}, bf16[1,3,180,768]{3,2,1,0:T(8,128)(2,1)}) custom-call(bf16[32,144,128]{2,1,0:T(8,128)(2,1)S(1)} %all-to-all-done.3.recv_ref, bf16[1,3,180,768]{3,2,1,0:T(8,128)(2,1)S(1)} %copy-done, bf16[1,3,180,768]{3,2,1,0:T(8,128)(2,1)S(1)} %copy-done.1, bf16[192,128]{1,0:T(8,128)(2,1)S(1)} %copy-done.3, ...), custom_call_target="tpu_custom_call" | custom-call | flops 212336640 | bytes 5000000 | tf_op jit(solution)/shard_map/from_spectra/pallas_call | solution.py:436
  (13 shorter events, 0.1 us)
Async XLA Ops:
  5.6 42.6 %copy-start.4 = (bf16[2,8,96,96]{3,2,1,0:T(8,128)(2,1)S(1)}, bf16[2,8,96,96]{3,2,1,0:T(8,128)(2,1)}, u32[]{:S(2)}) copy-start(bf16[2,8,96,96]{3,2,1,0:T(8,128)(2,1)} %first_ref.3) | copy-start | bytes 884740
  5.6 42.5 %copy-start.5 = (bf16[2,8,96,96]{3,2,1,0:T(8,128)(2,1)S(1)}, bf16[2,8,96,96]{3,2,1,0:T(8,128)(2,1)}, u32[]{:S(2)}) copy-start(bf16[2,8,96,96]{3,2,1,0:T(8,128)(2,1)} %second_ref.3) | copy-start | bytes 884740
  5.6 42.5 %copy-start.6 = (f32[2,768]{1,0:T(2,128)S(1)}, f32[2,768]{1,0:T(2,128)}, u32[]{:S(2)}) copy-start(f32[2,768]{1,0:T(2,128)} %bias_ref.2) | copy-start | bytes 18436
  5.6 42.5 %copy-start.8 = (bf16[192,192]{1,0:T(8,128)(2,1)S(1)}, bf16[192,192]{1,0:T(8,128)(2,1)}, u32[]{:S(2)}) copy-start(bf16[192,192]{1,0:T(8,128)(2,1)} %constant.34.clone.lat_ref) | copy-start | bytes 221188
  5.6 42.5 %all-to-all-start = ((bf16[32,144,128]{2,1,0:T(8,128)(2,1)}), bf16[32,144,128]{2,1,0:T(8,128)(2,1)S(1)}, u32[]{:S(2)}, u32[]{:S(2)}) async-start(bf16[32,144,128]{2,1,0:T(8,128)(2,1)} %to_spectra.1), calls=%async_computation | async-start | bytes 2359296 | tf_op jit(solution)/shard_map/all_to_all | solution.py:529
  48.1 29.9 %copy-start.7 = (f32[2,768]{1,0:T(2,128)S(1)}, f32[2,768]{1,0:T(2,128)}, u32[]{:S(2)}) copy-start(f32[2,768]{1,0:T(2,128)} %bias_ref.3) | copy-start | bytes 18436
  52.3 1.2 copy-start.9
  72.7 16.1 %all-to-all-start.2 = ((bf16[32,24,128]{2,1,0:T(8,128)(2,1)}), bf16[32,24,128]{2,1,0:T(8,128)(2,1)S(1)}, u32[]{:S(2)}, u32[]{:S(2)}) async-start(bf16[32,24,128]{2,1,0:T(8,128)(2,1)} %grad_share.1), calls=%async_computation.2 | async-start | bytes 393216 | tf_op jit(solution)/shard_map/all_to_all | solution.py:529
  78.1 1.4 %copy-start.10 = (bf16[2,1536,256]{2,1,0:T(8,128)(2,1)S(1)}, bf16[2,1536,256]{2,1,0:T(8,128)(2,1)}, u32[]{:S(2)}) copy-start(bf16[2,1536,256]{2,1,0:T(8,128)(2,1)} %copy-done.9) | copy-start | bytes 4718596
  88.8 34.3 %all-to-all-start.3 = ((bf16[32,144,128]{2,1,0:T(8,128)(2,1)}), bf16[32,144,128]{2,1,0:T(8,128)(2,1)S(1)}, u32[]{:S(2)}, u32[]{:S(2)}) async-start(bf16[32,144,128]{2,1,0:T(8,128)(2,1)} %spectral_return.1), calls=%async_computation.3 | async-start | bytes 2359296 | tf_op jit(solution)/shard_map/all_to_all | solution.py:529
  94.1 29.0 %copy-start = (bf16[1,3,180,768]{3,2,1,0:T(8,128)(2,1)S(1)}, bf16[1,3,180,768]{3,2,1,0:T(8,128)(2,1)}, u32[]{:S(2)}) copy-start(bf16[1,3,180,768]{3,2,1,0:T(8,128)(2,1)} %x_ref.3) | copy-start | bytes 2488324
  94.1 29.0 %copy-start.1 = (bf16[1,3,180,768]{3,2,1,0:T(8,128)(2,1)S(1)}, bf16[1,3,180,768]{3,2,1,0:T(8,128)(2,1)}, u32[]{:S(2)}) copy-start(bf16[1,3,180,768]{3,2,1,0:T(8,128)(2,1)} %g_ref.3) | copy-start | bytes 2488324
  94.1 29.0 %copy-start.2 = (bf16[192,128]{1,0:T(8,128)(2,1)S(1)}, bf16[192,128]{1,0:T(8,128)(2,1)}, u32[]{:S(2)}) copy-start(bf16[192,128]{1,0:T(8,128)(2,1)} %constant.31.clone.inv_ref) | copy-start | bytes 147460
  94.1 29.0 %copy-start.3 = (bf16[192,128]{1,0:T(8,128)(2,1)S(1)}, bf16[192,128]{1,0:T(8,128)(2,1)}, u32[]{:S(2)}) copy-start(bf16[192,128]{1,0:T(8,128)(2,1)} %constant.30.clone.fwd_ref) | copy-start | bytes 147460

commit v4 on v3

--- a/solution.py
+++ b/solution.py
@@ -205,11 +205,13 @@
     lax.fori_loop(0, BANDS, one, 0, unroll=4)
 
 
-def pack_bands(rows_ref, first, out_ref):
+def pack_bands(rows_ref, back_rows_ref, early_ref, late_ref):
     def one(s, carry):
         base = pl.multiple_of(s * TILE_ROWS, TILE_ROWS)
         pieces = pack_tile(rows_ref[pl.ds(base, TILE_ROWS), :])
-        out_ref[s, first : first + PACK] = jnp.concatenate(pieces, axis=0).astype(BF)
+        early_ref[s, 0:48] = jnp.concatenate(pieces[:2], axis=0).astype(BF)
+        back = pack_tile(back_rows_ref[pl.ds(base, TILE_ROWS), :])
+        late_ref[s] = jnp.concatenate(pieces[2:] + back, axis=0).astype(BF)
         return carry
 
     lax.fori_loop(0, BANDS, one, 0, unroll=4)
@@ -282,8 +284,8 @@
 
 def gradient_kernel(
     block_ref, recv_ref, lat_ref, first_ref, bias_ref, second_ref,
-    kept_ref, grad_ref,
-    w1_ref, w2_ref, rows_ref, back_rows_ref, modes_ref, filtered_ref, sums_ref,
+    saved_ref, grad_ref,
+    w1_ref, w2_ref, rows_ref, back_rows_ref, modes_ref, filtered_ref, sums_ref, kept_ref, sem,
 ):
     fill_weight(first_ref, w1_ref)
     fill_weight(second_ref, w2_ref)
@@ -305,6 +307,8 @@
         filtered_ref[span] = back_filtered
         back_hidden = lax.dot_general(back_filtered, w2, NT, preferred_element_type=F32)
         kept_ref[1, span] = (back_hidden * slope).astype(BF)
+    save = pltpu.make_async_copy(kept_ref, saved_ref, sem)
+    save.start()
     ones = jnp.ones((8, MODES * H), BF)
     row = 0
     bias_rows = []
@@ -327,11 +331,12 @@
         grad_ref[chunk] = sums_ref[CHUNK_ROWS * chunk : CHUNK_ROWS * chunk + CHUNK_ROWS].astype(
             BF
         )
+    save.wait()
 
 
 def return_kernel(
     block_ref, kept_ref, lat_ref, first_ref, second_ref, bias_ref,
-    out_ref,
+    early_ref, late_ref,
     w1_ref, w2_ref, rows_ref, back_rows_ref,
 ):
     fill_weight(first_ref, w1_ref)
@@ -346,8 +351,7 @@
         store_rows(rows_ref, lat, pair, filtered.astype(BF))
         back_modes = lax.dot_general(kept_ref[1, span], w1, NT, preferred_element_type=F32)
         store_rows(back_rows_ref, lat, pair, back_modes.astype(BF))
-    pack_bands(rows_ref, 0, out_ref)
-    pack_bands(back_rows_ref, PACK, out_ref)
+    pack_bands(rows_ref, back_rows_ref, early_ref, late_ref)
 
 
 PAIR_ROWS = 2 * H
@@ -371,12 +375,16 @@
                 for operand, spec in zip(operands, specs)
             ],
             out_specs=[
-                pl.BlockSpec(out.shape, lambda i, n, d=len(out.shape): (0,) * d)
+                pl.BlockSpec(memory_space=pltpu.HBM)
+                if out.shape == (2,) + WIDE
+                else pl.BlockSpec(out.shape, lambda i, n, d=len(out.shape): (0,) * d)
                 for out in outs
             ],
             scratch_shapes=scratch,
         ),
-        out_shape=outs,
+        out_shape=[
+            pltpu.HBM(out.shape, out.dtype) if out.shape == (2,) + WIDE else out for out in outs
+        ],
         compiler_params=pltpu.CompilerParams(vmem_limit_bytes=14 * 1024 * 1024),
         cost_estimate=pl.CostEstimate(
             flops=1000000000, bytes_accessed=6000000, transcendentals=800000
@@ -384,16 +392,13 @@
     )(block, *operands)
 
 
-def receive(recv_ref, first, rows_ref):
+def receive(parts, rows_ref):
     for group in range(GROUPS):
         for quad in range(2):
             tiles = []
             for block in range(4):
                 band = (4 * quad + block) * GROUPS + group
-                pieces = [
-                    recv_ref[band, first + 24 * i : first + 24 * i + 24, :].astype(F32)
-                    for i in range(3)
-                ]
+                pieces = [ref[band, at : at + 24, :].astype(F32) for ref, at in parts]
                 tiles.append(jnp.concatenate(pieces + [unpack_tail(pieces)], axis=0))
             for t, joined in enumerate(join_lanes(tiles)):
                 for r in range(ROWS):
@@ -405,15 +410,15 @@
 
 
 def output_kernel(
-    recv_ref, x_ref, g_ref, fwd_ref, inv_ref, out_ref, grad_ref,
+    early_ref, late_ref, x_ref, g_ref, fwd_ref, inv_ref, out_ref, grad_ref,
     rows_ref, back_rows_ref, mixed_ref, back_ref,
 ):
     r = pl.program_id(0)
 
     @pl.when(r == 0)
     def _():
-        receive(recv_ref, 0, rows_ref)
-        receive(recv_ref, PACK, back_rows_ref)
+        receive(((early_ref, 0), (early_ref, 24), (late_ref, 0)), rows_ref)
+        receive(((late_ref, 24), (late_ref, 48), (late_ref, 72)), back_rows_ref)
 
     mixed_ref[...] = jnp.dot(inv_ref[...], rows_ref[r], preferred_element_type=F32)
     back_ref[...] = jnp.dot(fwd_ref[...], back_rows_ref[r], preferred_element_type=F32)
@@ -429,7 +434,7 @@
         grad_ref[0, 0, span] = (upstream + scale * (back - mean - normed * along)).astype(BF)
 
 
-def from_spectra(recv, fields, cotangent, forward, inverse):
+def from_spectra(early, late, fields, cotangent, forward, inverse):
     token_spec = pl.BlockSpec((1, 1, W, C), lambda r: (0, r, 0, 0))
     table_spec = pl.BlockSpec((WPAD, 2 * KX), lambda r: (0, 0))
     token = jax.ShapeDtypeStruct((1, ROWS, W, C), BF)
@@ -438,7 +443,8 @@
         name="from_spectra",
         grid=(ROWS,),
         in_specs=[
-            pl.BlockSpec((BANDS, 2 * PACK, 128), lambda r: (0, 0, 0)),
+            pl.BlockSpec((BANDS, PACK, 128), lambda r: (0, 0, 0)),
+            pl.BlockSpec((BANDS, 96, 128), lambda r: (0, 0, 0)),
             token_spec,
             token_spec,
             table_spec,
@@ -456,7 +462,7 @@
         cost_estimate=pl.CostEstimate(
             flops=4 * ROWS * W * 2 * KX * C, bytes_accessed=5000000, transcendentals=0
         ),
-    )(recv, fields, cotangent, forward, inverse)
+    )(early, late, fields, cotangent, forward, inverse)
 
 
 def whole(shape):
@@ -478,7 +484,7 @@
     )(*operands)
 
 
-def share_kernel(recv_ref, out_ref):
+def share_kernel(recv_ref, held_ref, out_ref):
     total = recv_ref[0].astype(F32)
     for i in range(1, recv_ref.shape[0]):
         total = total + recv_ref[i].astype(F32)
@@ -487,12 +493,40 @@
         out_ref[band] = share
 
 
+def add_share(shares, held):
+    return pl.pallas_call(
+        share_kernel,
+        name="grad_share",
+        grid=(1,),
+        in_specs=[
+            pl.BlockSpec(shares.shape, lambda i: (0, 0, 0)),
+            pl.BlockSpec(memory_space=pl.ANY),
+        ],
+        out_specs=pl.BlockSpec((BANDS, CHUNK_ROWS, 128), lambda i: (0, 2, 0)),
+        out_shape=jax.ShapeDtypeStruct(held.shape, BF),
+        input_output_aliases={1: 0},
+        compiler_params=pltpu.CompilerParams(vmem_limit_bytes=VMEM_LIMIT),
+    )(shares, held)
+
+
 def group_sum_kernel(recv_ref, out_ref):
     for block in range(NB):
         total = recv_ref[block * GROUPS].astype(F32)
         for group in range(1, GROUPS):
             total = total + recv_ref[block * GROUPS + group].astype(F32)
         out_ref[block] = total.astype(BF)
+
+
+def group_sums(message):
+    return pl.pallas_call(
+        group_sum_kernel,
+        name="grad_groups",
+        grid=(1,),
+        in_specs=[pl.BlockSpec((BANDS, CHUNK_ROWS, 128), lambda i: (0, 2, 0))],
+        out_specs=pl.BlockSpec((NB, CHUNK_ROWS, 128), lambda i: (0, 0, 0)),
+        out_shape=jax.ShapeDtypeStruct((NB, CHUNK_ROWS, 128), BF),
+        compiler_params=pltpu.CompilerParams(vmem_limit_bytes=VMEM_LIMIT),
+    )(message)
 
 
 GRAD_SCALE = 1.0 / (SAMPLES * H)
@@ -546,39 +580,31 @@
         ("", "", "weight", "", "weight"),
         [jax.ShapeDtypeStruct((2,) + WIDE, BF), jax.ShapeDtypeStruct((CHUNKS, CHUNK_ROWS, 128), BF)],
         [FORM, FORM, BAND_ROWS, BAND_ROWS, pltpu.VMEM(WIDE, BF), pltpu.VMEM(WIDE, BF)]
-        + [pltpu.VMEM((CHUNKS * CHUNK_ROWS, 128), F32)],
-    )
+        + [pltpu.VMEM((CHUNKS * CHUNK_ROWS, 128), F32), pltpu.VMEM((2,) + WIDE, BF)]
+        + [pltpu.SemaphoreType.DMA],
+    )
+    kept = pltpu.with_memory_space_constraint(kept, pltpu.HBM)
     dp_size = lax.axis_size("dp")
     if dp_size == CHUNKS:
         shares = lax.all_to_all(grads, "dp", 0, 0, tiled=True)
     else:
         shares = grads
-    send = block_call(
+    early, late = block_call(
         return_kernel,
         "spectral_return",
         block,
         (kept, lat, w_first, w_second, b_second),
         ("", "", "weight", "weight", ""),
-        [jax.ShapeDtypeStruct((BANDS, 2 * PACK, 128), BF)],
+        [
+            jax.ShapeDtypeStruct((BANDS, PACK, 128), BF),
+            jax.ShapeDtypeStruct((BANDS, 96, 128), BF),
+        ],
         [FORM, FORM, BAND_ROWS, BAND_ROWS],
-    )[0]
-    share = spectral_call(
-        share_kernel,
-        "grad_share",
-        (shares,),
-        [jax.ShapeDtypeStruct((BANDS, CHUNK_ROWS, 128), BF)],
-        [],
-    )[0]
-    banded = exchange(share)
-    send, banded = lax.optimization_barrier((send, banded))
-    returned = exchange(send)
-    blocks = spectral_call(
-        group_sum_kernel,
-        "grad_groups",
-        (banded,),
-        [jax.ShapeDtypeStruct((NB, CHUNK_ROWS, 128), BF)],
-        [],
-    )[0]
+    )
+    early = exchange(add_share(shares, early))
+    late, early = lax.optimization_barrier((late, early))
+    late = exchange(late)
+    blocks = group_sums(early)
     every = lax.all_gather(blocks, "dp", axis=0, tiled=False)
     if dp_size != CHUNKS:
         every = jnp.broadcast_to(every, (CHUNKS, NB, CHUNK_ROWS, 128))
@@ -587,7 +613,7 @@
     g_w1, g_b1, g_w2, g_b2 = spectral_call(
         grads_kernel, "grad_out", (every,), [grad_w, grad_b, grad_w, grad_b], []
     )
-    result, back_fields = from_spectra(returned, fields, cotangent, lon_fwd, lon_inv)
+    result, back_fields = from_spectra(early, late, fields, cotangent, lon_fwd, lon_inv)
     return (result, back_fields, g_w1, g_b1, g_w2, g_b2)
 
 

time: 129 us -> 127 us (0.984)
  waiting for transfers between devices: 42.5 us -> 32.1 us
  blocking collectives: 35.9 us -> 41.5 us
  starting transfers between devices: 24.5 us -> 29.1 us
  local copies, waits for them, and re-layouts: 2.63 us -> 0.06 us
    all_to_all x3 -> x2, waiting for transfers between devices: 42.5 us -> 29.6 us  [exchange(): return lax.all_to_all(value, 'lat', split_axis=0, concat_axis=0, tiled=True)]
    all_to_all x0 -> x1, starting transfers between devices: none -> 10.2 us  [on_device(): shares = lax.all_to_all(grads, 'dp', 0, 0, tiled=True)]
    all_to_all x3 -> x2, starting transfers between devices: 24.5 us -> 18.9 us  [exchange(): return lax.all_to_all(value, 'lat', split_axis=0, concat_axis=0, tiled=True)]
    all_to_all x1, blocking collectives: 18.5 us -> 23.3 us  [exchange(): return lax.all_to_all(value, 'lat', split_axis=0, concat_axis=0, tiled=True)]
    unnamed x22 -> x18, local copies, waits for them, and re-layouts: 2.63 us -> 0.06 us
    all_to_all x0 -> x1, waiting for transfers between devices: none -> 2.44 us  [on_device(): shares = lax.all_to_all(grads, 'dp', 0, 0, tiled=True)]
    pallas_call x2, Pallas kernels: 9.55 us -> 11.3 us  [block_call(): pl.pallas_call(kernel, name=name, grid_spec=pltpu.PrefetchScalarGridSpec(...]
  transfers between devices with their start and end apart: 3 -> 3, of which waited for: 3 -> 3; matrix products, arithmetic and copies ran while one was open for 0% -> 0% of each run, Pallas kernels for 5% -> 6%
where the time goes in v4:
time: 127 us; the launch traced here: 125 us
  blocking collectives  41.5 us (33%)
  waiting for transfers between devices  32.1 us (25%)
  starting transfers between devices  29.1 us (23%)
  Pallas kernels  21.8 us (17%)
    all_to_all x2, waiting for transfers between devices, exchange(): return lax.all_to_all(value, 'lat', split_axis=0, concat_axis=0, tiled=True)  29.6 us
    all_to_all x1, blocking collectives, exchange(): return lax.all_to_all(value, 'lat', split_axis=0, concat_axis=0, tiled=True)  23.3 us
    all_to_all x2, starting transfers between devices, exchange(): return lax.all_to_all(value, 'lat', split_axis=0, concat_axis=0, tiled=True)  18.9 us
    all_gather x1, blocking collectives, on_device(): every = lax.all_gather(blocks, 'dp', axis=0, tiled=False)  18.2 us
    pallas_call x2, Pallas kernels, block_call(): pl.pallas_call(kernel, name=name, grid_spec=pltpu.PrefetchScalarGridSpec(...  11.3 us
    all_to_all x1, starting transfers between devices, on_device(): shares = lax.all_to_all(grads, 'dp', 0, 0, tiled=True)  10.2 us
    pallas_call x1, Pallas kernels, to_spectra(): pl.pallas_call(spectra_kernel, name='to_spectra', in_specs=[held, held, h...  4.93 us
    pallas_call x1, Pallas kernels, from_spectra(): pl.pallas_call(output_kernel, name='from_spectra', grid=(ROWS,), in_specs...  4.01 us
  transfers between devices with their start and end apart: 3, of which 3 were waited for; matrix products, arithmetic and copies ran while one was open for 0% of the time, Pallas kernels for 6%

profile of v4, /device:TPU:1, one launch (start us, length us, event | category | flops | bytes accessed | tf_op | source)
XLA Modules:
  0.0 125.4 jit_solution(2930752187660879269)
XLA Ops:
  0.6 4.9 %to_spectra.1 = bf16[32,144,128]{2,1,0:T(8,128)(2,1)} custom-call(bf16[1,3,180,768]{3,2,1,0:T(8,128)(2,1)} %x_ref.3, bf16[1,3,180,768]{3,2,1,0:T(8,128)(2,1)} %g_ref.3, bf16[128,192]{1,0:T(8,128)(2,1)} %constant.32.clone.fwd_ref, bf16[128,192]{1,0:T(8,128)(2,1)} %constant.33.clone.inv_ref), custom_call_target="tpu_custom_call" | custom-call | flops 212336640 | bytes 3000000 | tf_op jit(solution)/shard_map/to_spectra/pallas_call | solution.py:168
  5.6 0.0 copy-start.4
  5.6 0.0 copy-start.5
  5.6 0.0 copy-start.6
  5.6 0.0 copy-start.8
  5.6 13.8 %all-to-all-start = ((bf16[32,144,128]{2,1,0:T(8,128)(2,1)}), bf16[32,144,128]{2,1,0:T(8,128)(2,1)S(1)}, u32[]{:S(2)}, u32[]{:S(2)}) async-start(bf16[32,144,128]{2,1,0:T(8,128)(2,1)} %to_spectra.1), calls=%async_computation | async-start | bytes 2359296 | tf_op jit(solution)/shard_map/all_to_all | solution.py:563
  19.5 28.6 %all-to-all-done.recv_ref = bf16[32,144,128]{2,1,0:T(8,128)(2,1)S(1)} async-done(((bf16[32,144,128]{2,1,0:T(8,128)(2,1)}), bf16[32,144,128]{2,1,0:T(8,128)(2,1)S(1)}, u32[]{:S(2)}, u32[]{:S(2)}) %all-to-all-start) | async-done | bytes 1179680 | tf_op jit(solution)/shard_map/all_to_all | solution.py:563
  48.1 0.0 copy-done.6
  48.1 0.0 copy-start.7
  48.2 5.3 %spectral_grads.1 = (bf16[2,1536,256]{2,1,0:T(8,128)(2,1)}, bf16[16,24,128]{2,1,0:T(8,128)(2,1)}) custom-call(s32[1]{0:T(128)} %bitcast.block_ref, bf16[32,144,128]{2,1,0:T(8,128)(2,1)S(1)} %all-to-all-done.recv_ref, bf16[192,192]{1,0:T(8,128)(2,1)S(1)} %copy-done.8, bf16[2,8,96,96]{3,2,1,0:T(8,128)(2,1)S(1)} %copy-done.4, f32[2,768]{1,0:T(2,128)S(1)} %copy-done.6, ...), custom_call_target="tpu_custom_call" | custom-call | flops 1000000000 | bytes 6000000 | tf_op jit(solution)/shard_map/spectral_grads/pallas_call | solution.py:365
  53.4 10.2 %all-to-all-start.1 = ((bf16[16,24,128]{2,1,0:T(8,128)(2,1)}), bf16[16,24,128]{2,1,0:T(8,128)(2,1)S(1)}, u32[]{:S(2)}, u32[]{:S(2)}) async-start(bf16[16,24,128]{2,1,0:T(8,128)(2,1)} %get-tuple-element.20), calls=%async_computation.1 | async-start | bytes 196608 | tf_op jit(solution)/shard_map/all_to_all | solution.py:589
  63.7 6.0 %spectral_return.1 = (bf16[32,72,128]{2,1,0:T(8,128)(2,1)S(1)}, bf16[32,96,128]{2,1,0:T(8,128)(2,1)}) custom-call(s32[1]{0:T(128)} %bitcast.block_ref, bf16[2,1536,256]{2,1,0:T(8,128)(2,1)} %get-tuple-element.18.kept_ref, bf16[192,192]{1,0:T(8,128)(2,1)S(1)} %copy-done.8, bf16[2,8,96,96]{3,2,1,0:T(8,128)(2,1)S(1)} %copy-done.4, ...), custom_call_target="tpu_custom_call" | custom-call | flops 1000000000 | bytes 6000000 | tf_op jit(solution)/shard_map/spectral_return/pallas_call | solution.py:365
  69.7 2.4 %all-to-all-done.1.recv_ref = bf16[16,24,128]{2,1,0:T(8,128)(2,1)S(1)} async-done(((bf16[16,24,128]{2,1,0:T(8,128)(2,1)}), bf16[16,24,128]{2,1,0:T(8,128)(2,1)S(1)}, u32[]{:S(2)}, u32[]{:S(2)}) %all-to-all-start.1) | async-done | bytes 98336 | tf_op jit(solution)/shard_map/all_to_all | solution.py:589
  72.1 0.1 grad_share.1
  72.2 23.3 %all_to_all.20.early_ref.recv_ref = bf16[32,72,128]{2,1,0:T(8,128)(2,1)S(1)} all-to-all(bf16[32,72,128]{2,1,0:T(8,128)(2,1)S(1)} %grad_share.1), channel_id=1, replica_groups=mesh['dp'=16,'lat'=32] {'lat'}, dimensions={0} | all-to-all | bytes 1179648 | tf_op jit(solution)/shard_map/all_to_all | solution.py:563
  95.5 5.1 %all-to-all-start.3 = ((bf16[32,96,128]{2,1,0:T(8,128)(2,1)}), bf16[32,96,128]{2,1,0:T(8,128)(2,1)S(1)}, u32[]{:S(2)}, u32[]{:S(2)}) async-start(bf16[32,96,128]{2,1,0:T(8,128)(2,1)} %get-tuple-element.23), calls=%async_computation.3 | async-start | bytes 1572864 | tf_op jit(solution)/shard_map/all_to_all | solution.py:563
  100.6 0.0 copy-start
  100.6 0.0 copy-start.1
  100.6 0.0 copy-start.2
  100.6 0.0 copy-start.3
  100.7 18.2 %all-gather = bf16[128,24,128]{2,1,0:T(8,128)(2,1)S(1)} all-gather(bf16[8,24,128]{2,1,0:T(8,128)(2,1)S(1)} %grad_groups.1), channel_id=2, replica_groups=mesh['dp'=16,'lat'=32] {'dp'}, dimensions={0}, use_global_device_ids=true | all-gather | bytes 835584 | tf_op jit(solution)/shard_map/all_gather | solution.py:608
  118.9 1.5 %grad_out.1 = (f32[2,8,96,96]{3,2,1,0:T(8,128)}, f32[2,768]{1,0:T(2,128)}, f32[2,8,96,96]{3,2,1,0:T(8,128)}, f32[2,768]{1,0:T(2,128)}) custom-call(bf16[16,8,24,128]{3,2,1,0:T(8,128)(2,1)S(1)} %bitcast.2), custom_call_target="tpu_custom_call" | custom-call | flops 1000000 | bytes 1000000 | tf_op jit(solution)/shard_map/grad_out/pallas_call | solution.py:473
  120.4 1.0 all-to-all-done.3.late_ref
  121.4 4.0 %from_spectra.1 = (bf16[1,3,180,768]{3,2,1,0:T(8,128)(2,1)}, bf16[1,3,180,768]{3,2,1,0:T(8,128)(2,1)}) custom-call(bf16[32,72,128]{2,1,0:T(8,128)(2,1)S(1)} %all_to_all.20.early_ref.recv_ref, bf16[32,96,128]{2,1,0:T(8,128)(2,1)S(1)} %all-to-all-done.3.late_ref, bf16[1,3,180,768]{3,2,1,0:T(8,128)(2,1)S(1)} %copy-done, bf16[1,3,180,768]{3,2,1,0:T(8,128)(2,1)S(1)} %copy-done.1, ...), custom_call_target="tpu_custom_call" | custom-call | flops 212336640 | bytes 5000000 | tf_op jit(solution)/shard_map/from_spectra/pallas_call | solution.py:441
  (9 shorter events, 0.1 us)
Async XLA Ops:
  5.6 42.6 %copy-start.4 = (bf16[2,8,96,96]{3,2,1,0:T(8,128)(2,1)S(1)}, bf16[2,8,96,96]{3,2,1,0:T(8,128)(2,1)}, u32[]{:S(2)}) copy-start(bf16[2,8,96,96]{3,2,1,0:T(8,128)(2,1)} %first_ref.3) | copy-start | bytes 884740
  5.6 42.5 %copy-start.5 = (bf16[2,8,96,96]{3,2,1,0:T(8,128)(2,1)S(1)}, bf16[2,8,96,96]{3,2,1,0:T(8,128)(2,1)}, u32[]{:S(2)}) copy-start(bf16[2,8,96,96]{3,2,1,0:T(8,128)(2,1)} %second_ref.3) | copy-start | bytes 884740
  5.6 42.5 %copy-start.6 = (f32[2,768]{1,0:T(2,128)S(1)}, f32[2,768]{1,0:T(2,128)}, u32[]{:S(2)}) copy-start(f32[2,768]{1,0:T(2,128)} %bias_ref.2) | copy-start | bytes 18436
  5.6 42.5 %copy-start.8 = (bf16[192,192]{1,0:T(8,128)(2,1)S(1)}, bf16[192,192]{1,0:T(8,128)(2,1)}, u32[]{:S(2)}) copy-start(bf16[192,192]{1,0:T(8,128)(2,1)} %constant.34.clone.lat_ref) | copy-start | bytes 221188
  5.6 42.5 %all-to-all-start = ((bf16[32,144,128]{2,1,0:T(8,128)(2,1)}), bf16[32,144,128]{2,1,0:T(8,128)(2,1)S(1)}, u32[]{:S(2)}, u32[]{:S(2)}) async-start(bf16[32,144,128]{2,1,0:T(8,128)(2,1)} %to_spectra.1), calls=%async_computation | async-start | bytes 2359296 | tf_op jit(solution)/shard_map/all_to_all | solution.py:563
  48.1 15.5 %copy-start.7 = (f32[2,768]{1,0:T(2,128)S(1)}, f32[2,768]{1,0:T(2,128)}, u32[]{:S(2)}) copy-start(f32[2,768]{1,0:T(2,128)} %bias_ref.3) | copy-start | bytes 18436
  53.4 18.7 %all-to-all-start.1 = ((bf16[16,24,128]{2,1,0:T(8,128)(2,1)}), bf16[16,24,128]{2,1,0:T(8,128)(2,1)S(1)}, u32[]{:S(2)}, u32[]{:S(2)}) async-start(bf16[16,24,128]{2,1,0:T(8,128)(2,1)} %get-tuple-element.20), calls=%async_computation.1 | async-start | bytes 196608 | tf_op jit(solution)/shard_map/all_to_all | solution.py:589
  95.5 25.9 %all-to-all-start.3 = ((bf16[32,96,128]{2,1,0:T(8,128)(2,1)}), bf16[32,96,128]{2,1,0:T(8,128)(2,1)S(1)}, u32[]{:S(2)}, u32[]{:S(2)}) async-start(bf16[32,96,128]{2,1,0:T(8,128)(2,1)} %get-tuple-element.23), calls=%async_computation.3 | async-start | bytes 1572864 | tf_op jit(solution)/shard_map/all_to_all | solution.py:563
  100.6 20.8 %copy-start = (bf16[1,3,180,768]{3,2,1,0:T(8,128)(2,1)S(1)}, bf16[1,3,180,768]{3,2,1,0:T(8,128)(2,1)}, u32[]{:S(2)}) copy-start(bf16[1,3,180,768]{3,2,1,0:T(8,128)(2,1)} %x_ref.3) | copy-start | bytes 2488324
  100.6 20.8 %copy-start.1 = (bf16[1,3,180,768]{3,2,1,0:T(8,128)(2,1)S(1)}, bf16[1,3,180,768]{3,2,1,0:T(8,128)(2,1)}, u32[]{:S(2)}) copy-start(bf16[1,3,180,768]{3,2,1,0:T(8,128)(2,1)} %g_ref.3) | copy-start | bytes 2488324
  100.6 20.8 %copy-start.2 = (bf16[192,128]{1,0:T(8,128)(2,1)S(1)}, bf16[192,128]{1,0:T(8,128)(2,1)}, u32[]{:S(2)}) copy-start(bf16[192,128]{1,0:T(8,128)(2,1)} %constant.31.clone.inv_ref) | copy-start | bytes 147460
  100.6 20.8 %copy-start.3 = (bf16[192,128]{1,0:T(8,128)(2,1)S(1)}, bf16[192,128]{1,0:T(8,128)(2,1)}, u32[]{:S(2)}) copy-start(bf16[192,128]{1,0:T(8,128)(2,1)} %constant.30.clone.fwd_ref) | copy-start | bytes 147460

commit v5 on v4

--- a/solution.py
+++ b/solution.py
@@ -112,10 +112,10 @@
     centered = values - mean
     spread = jnp.sum(centered * centered, axis=-1, keepdims=True) * (1.0 / C)
     scale = 1.0 / jnp.sqrt(spread + EPSILON)
-    return centered * scale, scale
-
-
-def send_packed(acc_ref, out_ref, first):
+    return centered * scale, mean, scale
+
+
+def send_packed(acc_ref, out_ref):
     for block in range(NB):
         rows = [block_lanes(acc_ref[r], block) for r in range(ROWS)]
         for group in range(GROUPS):
@@ -123,14 +123,12 @@
                 [row[32 * group : 32 * group + 32] for row in rows], axis=0
             )
             pieces = pack_tile(tile)
-            out_ref[block * GROUPS + group, first : first + PACK] = jnp.concatenate(
-                pieces, axis=0
-            ).astype(BF)
+            out_ref[block * GROUPS + group] = jnp.concatenate(pieces, axis=0).astype(BF)
 
 
 def spectra_kernel(
-    x_ref, g_ref, fwd_ref, inv_ref, out_ref,
-    x_rows, g_rows, fwd_table, inv_table, padded_ref, acc_ref, sems,
+    x_ref, g_ref, fwd_ref, inv_ref, out_ref, moments_ref,
+    x_rows, g_rows, fwd_table, inv_table, padded_ref, acc_ref, send_ref, kept_ref, sems, out_sems,
 ):
     copies = [pltpu.make_async_copy(x_ref.at[0, 0], x_rows.at[0], sems.at[0])]
     copies += [pltpu.make_async_copy(fwd_ref, fwd_table, sems.at[1])]
@@ -150,17 +148,33 @@
         copies[0 if r == 0 else 1 + r].wait()
         for start, size in ROW_CHUNKS:
             values = x_rows[r, start : start + size].astype(F32)
-            padded_ref[start : start + size] = normalize(values)[0].astype(BF)
+            normed, mean, scale = normalize(values)
+            padded_ref[start : start + size] = normed.astype(BF)
+            kept_ref[r, start : start + size, 0:128] = jnp.broadcast_to(mean, (size, 128))
+            kept_ref[r, start : start + size, 128:256] = jnp.broadcast_to(scale, (size, 128))
         if r == 0:
             copies[1].wait()
         acc_ref[r] = jnp.dot(fwd_table[...], padded_ref[...], preferred_element_type=F32)
-    send_packed(acc_ref, out_ref, 0)
+    moments_out = pltpu.make_async_copy(kept_ref, moments_ref, out_sems.at[2])
+    moments_out.start()
+    send_packed(acc_ref, send_ref.at[0])
+    fields_out = pltpu.make_async_copy(
+        send_ref.at[0], out_ref.at[:, pl.ds(0, PACK), :], out_sems.at[0]
+    )
+    fields_out.start()
     copies[1 + ROWS].wait()
     for r in range(ROWS):
         copies[2 + ROWS + r].wait()
         padded_ref[0:W] = g_rows[r]
         acc_ref[r] = jnp.dot(inv_table[...], padded_ref[...], preferred_element_type=F32)
-    send_packed(acc_ref, out_ref, PACK)
+    send_packed(acc_ref, send_ref.at[1])
+    back_out = pltpu.make_async_copy(
+        send_ref.at[1], out_ref.at[:, pl.ds(PACK, PACK), :], out_sems.at[1]
+    )
+    back_out.start()
+    moments_out.wait()
+    fields_out.wait()
+    back_out.wait()
 
 
 def to_spectra(fields, cotangent, forward, inverse):
@@ -169,8 +183,11 @@
         spectra_kernel,
         name="to_spectra",
         in_specs=[held, held, held, held],
-        out_specs=pl.BlockSpec(memory_space=pltpu.VMEM),
-        out_shape=jax.ShapeDtypeStruct((BANDS, 2 * PACK, 128), BF),
+        out_specs=[held, held],
+        out_shape=[
+            pltpu.HBM((BANDS, 2 * PACK, 128), BF),
+            pltpu.HBM((ROWS, W, 256), F32),
+        ],
         scratch_shapes=[
             pltpu.VMEM((ROWS, W, C), BF),
             pltpu.VMEM((ROWS, W, C), BF),
@@ -178,7 +195,10 @@
             pltpu.VMEM((2 * KX, WPAD), BF),
             pltpu.VMEM((WPAD, C), BF),
             pltpu.VMEM((ROWS, 2 * KX, C), F32),
+            pltpu.VMEM((2, BANDS, PACK, 128), BF),
+            pltpu.VMEM((ROWS, W, 256), F32),
             pltpu.SemaphoreType.DMA((2 + 2 * ROWS,)),
+            pltpu.SemaphoreType.DMA((3,)),
         ],
         compiler_params=pltpu.CompilerParams(vmem_limit_bytes=VMEM_LIMIT),
         cost_estimate=pl.CostEstimate(
@@ -205,7 +225,7 @@
     lax.fori_loop(0, BANDS, one, 0, unroll=4)
 
 
-def pack_bands(rows_ref, back_rows_ref, early_ref, late_ref):
+def pack_bands(rows_ref, back_rows_ref, early_ref, late_ref, first):
     def one(s, carry):
         base = pl.multiple_of(s * TILE_ROWS, TILE_ROWS)
         pieces = pack_tile(rows_ref[pl.ds(base, TILE_ROWS), :])
@@ -214,7 +234,7 @@
         late_ref[s] = jnp.concatenate(pieces[2:] + back, axis=0).astype(BF)
         return carry
 
-    lax.fori_loop(0, BANDS, one, 0, unroll=4)
+    lax.fori_loop(first, first + BANDS // 4, one, 0, unroll=4)
 
 
 def mode_rows(rows_ref, lat, pair):
@@ -285,7 +305,7 @@
 def gradient_kernel(
     block_ref, recv_ref, lat_ref, first_ref, bias_ref, second_ref,
     saved_ref, grad_ref,
-    w1_ref, w2_ref, rows_ref, back_rows_ref, modes_ref, filtered_ref, sums_ref, kept_ref, sem,
+    w1_ref, w2_ref, rows_ref, back_rows_ref, modes_ref, filtered_ref, sums_ref, kept_ref, sems,
 ):
     fill_weight(first_ref, w1_ref)
     fill_weight(second_ref, w2_ref)
@@ -295,6 +315,7 @@
     lat = lat_ref[...]
     w1 = w1_ref[...]
     w2 = w2_ref[...]
+    saves = []
     for pair in range(PAIRS):
         span = slice(PAIR_ROWS * pair, PAIR_ROWS * pair + PAIR_ROWS)
         modes = mode_rows(rows_ref, lat, pair)
@@ -307,8 +328,12 @@
         filtered_ref[span] = back_filtered
         back_hidden = lax.dot_general(back_filtered, w2, NT, preferred_element_type=F32)
         kept_ref[1, span] = (back_hidden * slope).astype(BF)
-    save = pltpu.make_async_copy(kept_ref, saved_ref, sem)
-    save.start()
+        pair_rows = pl.ds(PAIR_ROWS * pair, PAIR_ROWS)
+        save = pltpu.make_async_copy(
+            kept_ref.at[:, pair_rows, :], saved_ref.at[:, pair_rows, :], sems.at[pair]
+        )
+        save.start()
+        saves.append(save)
     ones = jnp.ones((8, MODES * H), BF)
     row = 0
     bias_rows = []
@@ -331,14 +356,23 @@
         grad_ref[chunk] = sums_ref[CHUNK_ROWS * chunk : CHUNK_ROWS * chunk + CHUNK_ROWS].astype(
             BF
         )
-    save.wait()
+    for save in saves:
+        save.wait()
 
 
 def return_kernel(
-    block_ref, kept_ref, lat_ref, first_ref, second_ref, bias_ref,
-    early_ref, late_ref,
-    w1_ref, w2_ref, rows_ref, back_rows_ref,
+    block_ref, saved_ref, lat_ref, first_ref, second_ref, bias_ref,
+    early_ref, sent_ref,
+    w1_ref, w2_ref, rows_ref, back_rows_ref, kept_ref, late_ref, sems, out_sems,
 ):
+    fetches = []
+    for pair in range(PAIRS):
+        pair_rows = pl.ds(PAIR_ROWS * pair, PAIR_ROWS)
+        fetch = pltpu.make_async_copy(
+            saved_ref.at[:, pair_rows, :], kept_ref.at[:, pair_rows, :], sems.at[pair]
+        )
+        fetch.start()
+        fetches.append(fetch)
     fill_weight(first_ref, w1_ref)
     fill_weight(second_ref, w2_ref)
     bias = choose_bias(block_ref[0], bias_ref)
@@ -347,11 +381,22 @@
     w2 = w2_ref[...]
     for pair in range(PAIRS):
         span = slice(PAIR_ROWS * pair, PAIR_ROWS * pair + PAIR_ROWS)
+        fetches[pair].wait()
         filtered = jnp.dot(kept_ref[0, span], w2, preferred_element_type=F32) + bias
         store_rows(rows_ref, lat, pair, filtered.astype(BF))
         back_modes = lax.dot_general(kept_ref[1, span], w1, NT, preferred_element_type=F32)
         store_rows(back_rows_ref, lat, pair, back_modes.astype(BF))
-    pack_bands(rows_ref, back_rows_ref, early_ref, late_ref)
+    leaving = []
+    for part in range(4):
+        pack_bands(rows_ref, back_rows_ref, early_ref, late_ref, part * (BANDS // 4))
+        bands = pl.ds(part * (BANDS // 4), BANDS // 4)
+        copy = pltpu.make_async_copy(
+            late_ref.at[bands], sent_ref.at[bands], out_sems.at[part]
+        )
+        copy.start()
+        leaving.append(copy)
+    for copy in leaving:
+        copy.wait()
 
 
 PAIR_ROWS = 2 * H
@@ -361,7 +406,7 @@
 BAND_ROWS = pltpu.VMEM((2 * H * MODES, 128), F32)
 
 
-def block_call(kernel, name, block, operands, specs, outs, scratch):
+def block_call(kernel, name, block, operands, specs, outs, places, scratch):
     return pl.pallas_call(
         kernel,
         name=name,
@@ -371,19 +416,20 @@
             in_specs=[
                 pl.BlockSpec((2, 1, BS, BS), lambda i, n: (0, n[0], 0, 0))
                 if spec == "weight"
-                else pl.BlockSpec(operand.shape, lambda i, n, d=operand.ndim: (0,) * d)
+                else pl.BlockSpec(memory_space=pltpu.HBM)
+                if spec == "far"
+                else pl.BlockSpec(memory_space=pltpu.VMEM)
                 for operand, spec in zip(operands, specs)
             ],
             out_specs=[
-                pl.BlockSpec(memory_space=pltpu.HBM)
-                if out.shape == (2,) + WIDE
-                else pl.BlockSpec(out.shape, lambda i, n, d=len(out.shape): (0,) * d)
-                for out in outs
+                pl.BlockSpec(memory_space=pltpu.HBM if place == "far" else pltpu.VMEM)
+                for place in places
             ],
             scratch_shapes=scratch,
         ),
         out_shape=[
-            pltpu.HBM(out.shape, out.dtype) if out.shape == (2,) + WIDE else out for out in outs
+            pltpu.HBM(out.shape, out.dtype) if place == "far" else out
+            for out, place in zip(outs, places)
         ],
         compiler_params=pltpu.CompilerParams(vmem_limit_bytes=14 * 1024 * 1024),
         cost_estimate=pl.CostEstimate(
@@ -399,57 +445,57 @@
             for block in range(4):
                 band = (4 * quad + block) * GROUPS + group
                 pieces = [ref[band, at : at + 24, :].astype(F32) for ref, at in parts]
-                tiles.append(jnp.concatenate(pieces + [unpack_tail(pieces)], axis=0))
+                tiles.append(
+                    jnp.concatenate(pieces + [unpack_tail(pieces)], axis=0).astype(BF)
+                )
             for t, joined in enumerate(join_lanes(tiles)):
                 for r in range(ROWS):
                     rows_ref[
                         r,
                         32 * group : 32 * group + 32,
                         384 * quad + 128 * t : 384 * quad + 128 * t + 128,
-                    ] = joined[32 * r : 32 * r + 32].astype(BF)
+                    ] = joined[32 * r : 32 * r + 32]
 
 
 def output_kernel(
-    early_ref, late_ref, x_ref, g_ref, fwd_ref, inv_ref, out_ref, grad_ref,
-    rows_ref, back_rows_ref, mixed_ref, back_ref,
+    early_ref, late_ref, x_ref, moments_ref, g_ref, fwd_ref, inv_ref,
+    out_ref, grad_ref,
+    rows_ref, back_rows_ref, mixed_ref, back_ref, held_ref, sem,
 ):
     r = pl.program_id(0)
 
     @pl.when(r == 0)
     def _():
+        fetch = pltpu.make_async_copy(moments_ref, held_ref, sem)
+        fetch.start()
         receive(((early_ref, 0), (early_ref, 24), (late_ref, 0)), rows_ref)
         receive(((late_ref, 24), (late_ref, 48), (late_ref, 72)), back_rows_ref)
+        fetch.wait()
 
     mixed_ref[...] = jnp.dot(inv_ref[...], rows_ref[r], preferred_element_type=F32)
     back_ref[...] = jnp.dot(fwd_ref[...], back_rows_ref[r], preferred_element_type=F32)
     for start, size in ROW_CHUNKS:
         span = slice(start, start + size)
-        values = x_ref[0, 0, span].astype(F32)
-        normed, scale = normalize(values)
+        values = x_ref[0, r, span].astype(F32)
+        scale = held_ref[r, span, 128:256][:, 0:1]
+        normed = (values - held_ref[r, span, 0:128][:, 0:1]) * scale
         out_ref[0, 0, span] = (values + normed + mixed_ref[span]).astype(BF)
-        upstream = g_ref[0, 0, span].astype(F32)
+        upstream = g_ref[0, r, span].astype(F32)
         back = upstream + back_ref[span]
         mean = jnp.sum(back, axis=-1, keepdims=True) * (1.0 / C)
         along = jnp.sum(back * normed, axis=-1, keepdims=True) * (1.0 / C)
         grad_ref[0, 0, span] = (upstream + scale * (back - mean - normed * along)).astype(BF)
 
 
-def from_spectra(early, late, fields, cotangent, forward, inverse):
+def from_spectra(early, late, fields, moments, cotangent, forward, inverse):
     token_spec = pl.BlockSpec((1, 1, W, C), lambda r: (0, r, 0, 0))
-    table_spec = pl.BlockSpec((WPAD, 2 * KX), lambda r: (0, 0))
+    near = pl.BlockSpec(memory_space=pltpu.VMEM)
     token = jax.ShapeDtypeStruct((1, ROWS, W, C), BF)
     return pl.pallas_call(
         output_kernel,
         name="from_spectra",
         grid=(ROWS,),
-        in_specs=[
-            pl.BlockSpec((BANDS, PACK, 128), lambda r: (0, 0, 0)),
-            pl.BlockSpec((BANDS, 96, 128), lambda r: (0, 0, 0)),
-            token_spec,
-            token_spec,
-            table_spec,
-            table_spec,
-        ],
+        in_specs=[near] * 3 + [pl.BlockSpec(memory_space=pltpu.HBM)] + [near] * 3,
         out_specs=[token_spec, token_spec],
         out_shape=[token, token],
         scratch_shapes=[
@@ -457,12 +503,14 @@
             pltpu.VMEM((ROWS, 2 * KX, C), BF),
             pltpu.VMEM((WPAD, C), F32),
             pltpu.VMEM((WPAD, C), F32),
+            pltpu.VMEM((ROWS, W, 256), F32),
+            pltpu.SemaphoreType.DMA,
         ],
         compiler_params=pltpu.CompilerParams(vmem_limit_bytes=VMEM_LIMIT),
         cost_estimate=pl.CostEstimate(
             flops=4 * ROWS * W * 2 * KX * C, bytes_accessed=5000000, transcendentals=0
         ),
-    )(early, late, fields, cotangent, forward, inverse)
+    )(early, late, fields, moments, cotangent, forward, inverse)
 
 
 def whole(shape):
@@ -571,7 +619,9 @@
     lon_inv_t = jnp.asarray(LON_INV.T, BF)
     lat = jnp.asarray(LAT, BF)
 
-    spectra = exchange(to_spectra(fields, cotangent, lon_fwd_t, lon_inv_t))
+    spectra, moments = to_spectra(fields, cotangent, lon_fwd_t, lon_inv_t)
+    moments = pltpu.with_memory_space_constraint(moments, pltpu.HBM)
+    spectra = exchange(spectra)
     kept, grads = block_call(
         gradient_kernel,
         "spectral_grads",
@@ -579,9 +629,10 @@
         (spectra, lat, w_first, b_first, w_second),
         ("", "", "weight", "", "weight"),
         [jax.ShapeDtypeStruct((2,) + WIDE, BF), jax.ShapeDtypeStruct((CHUNKS, CHUNK_ROWS, 128), BF)],
+        ("far", "near"),
         [FORM, FORM, BAND_ROWS, BAND_ROWS, pltpu.VMEM(WIDE, BF), pltpu.VMEM(WIDE, BF)]
         + [pltpu.VMEM((CHUNKS * CHUNK_ROWS, 128), F32), pltpu.VMEM((2,) + WIDE, BF)]
-        + [pltpu.SemaphoreType.DMA],
+        + [pltpu.SemaphoreType.DMA((PAIRS,))],
     )
     kept = pltpu.with_memory_space_constraint(kept, pltpu.HBM)
     dp_size = lax.axis_size("dp")
@@ -594,12 +645,15 @@
         "spectral_return",
         block,
         (kept, lat, w_first, w_second, b_second),
-        ("", "", "weight", "weight", ""),
+        ("far", "", "weight", "weight", ""),
         [
             jax.ShapeDtypeStruct((BANDS, PACK, 128), BF),
             jax.ShapeDtypeStruct((BANDS, 96, 128), BF),
         ],
-        [FORM, FORM, BAND_ROWS, BAND_ROWS],
+        ("near", "far"),
+        [FORM, FORM, BAND_ROWS, BAND_ROWS, pltpu.VMEM((2,) + WIDE, BF)]
+        + [pltpu.VMEM((BANDS, 96, 128), BF)]
+        + [pltpu.SemaphoreType.DMA((PAIRS,)), pltpu.SemaphoreType.DMA((4,))],
     )
     early = exchange(add_share(shares, early))
     late, early = lax.optimization_barrier((late, early))
@@ -613,7 +667,9 @@
     g_w1, g_b1, g_w2, g_b2 = spectral_call(
         grads_kernel, "grad_out", (every,), [grad_w, grad_b, grad_w, grad_b], []
     )
-    result, back_fields = from_spectra(early, late, fields, cotangent, lon_fwd, lon_inv)
+    result, back_fields = from_spectra(
+        early, late, fields, moments, cotangent, lon_fwd, lon_inv
+    )
     return (result, back_fields, g_w1, g_b1, g_w2, g_b2)
 
 

time: 127 us -> 128 us (level)
  no operation moved by 1% of the time
where the time goes in v5:
time: 128 us; the launch traced here: 126 us
  blocking collectives  42.1 us (33%)
  waiting for transfers between devices  30.9 us (24%)
  starting transfers between devices  29.1 us (23%)
  Pallas kernels  22.8 us (18%)
    all_to_all x2, waiting for transfers between devices, exchange(): return lax.all_to_all(value, 'lat', split_axis=0, concat_axis=0, tiled=True)  29 us
    all_to_all x1, blocking collectives, exchange(): return lax.all_to_all(value, 'lat', split_axis=0, concat_axis=0, tiled=True)  23.3 us
    all_to_all x2, starting transfers between devices, exchange(): return lax.all_to_all(value, 'lat', split_axis=0, concat_axis=0, tiled=True)  18.9 us
    all_gather x1, blocking collectives, on_device(): every = lax.all_gather(blocks, 'dp', axis=0, tiled=False)  18.8 us
    pallas_call x2, Pallas kernels, block_call(): pl.pallas_call(kernel, name=name, grid_spec=pltpu.PrefetchScalarGridSpec(...  11.5 us
    all_to_all x1, starting transfers between devices, on_device(): shares = lax.all_to_all(grads, 'dp', 0, 0, tiled=True)  10.2 us
    pallas_call x1, Pallas kernels, from_spectra(): pl.pallas_call(output_kernel, name='from_spectra', grid=(ROWS,), in_specs...  4.98 us
    pallas_call x1, Pallas kernels, to_spectra(): pl.pallas_call(spectra_kernel, name='to_spectra', in_specs=[held, held, h...  4.75 us
  transfers between devices with their start and end apart: 3, of which 3 were waited for; matrix products, arithmetic and copies ran while one was open for 0% of the time, Pallas kernels for 6%

profile of v5, /device:TPU:1, one launch (start us, length us, event | category | flops | bytes accessed | tf_op | source)
XLA Modules:
  0.0 125.8 jit_solution(2007943822044899059)
XLA Ops:
  0.6 4.7 %to_spectra.1 = (bf16[32,144,128]{2,1,0:T(8,128)(2,1)}, f32[3,180,256]{2,1,0:T(8,128)}) custom-call(bf16[1,3,180,768]{3,2,1,0:T(8,128)(2,1)} %x_ref.3, bf16[1,3,180,768]{3,2,1,0:T(8,128)(2,1)} %g_ref.3, bf16[128,192]{1,0:T(8,128)(2,1)} %constant.32.clone.fwd_ref, bf16[128,192]{1,0:T(8,128)(2,1)} %constant.33.clone.inv_ref), custom_call_target="tpu_custom_call" | custom-call | flops 212336640 | bytes 3000000 | tf_op jit(solution)/shard_map/to_spectra/pallas_call | solution.py:182
  5.4 0.0 copy-start.4
  5.4 0.0 copy-start.5
  5.4 0.0 copy-start.6
  5.4 0.0 copy-start.8
  5.4 13.8 %all-to-all-start = ((bf16[32,144,128]{2,1,0:T(8,128)(2,1)}), bf16[32,144,128]{2,1,0:T(8,128)(2,1)S(1)}, u32[]{:S(2)}, u32[]{:S(2)}) async-start(bf16[32,144,128]{2,1,0:T(8,128)(2,1)} %get-tuple-element.20), calls=%async_computation | async-start | bytes 2359296 | tf_op jit(solution)/shard_map/all_to_all | solution.py:611
  19.3 28.7 %all-to-all-done.recv_ref = bf16[32,144,128]{2,1,0:T(8,128)(2,1)S(1)} async-done(((bf16[32,144,128]{2,1,0:T(8,128)(2,1)}), bf16[32,144,128]{2,1,0:T(8,128)(2,1)S(1)}, u32[]{:S(2)}, u32[]{:S(2)}) %all-to-all-start) | async-done | bytes 1179680 | tf_op jit(solution)/shard_map/all_to_all | solution.py:611
  48.0 0.0 copy-done.4
  48.0 0.0 copy-start.7
  48.0 4.9 %spectral_grads.1 = (bf16[2,1536,256]{2,1,0:T(8,128)(2,1)}, bf16[16,24,128]{2,1,0:T(8,128)(2,1)}) custom-call(s32[1]{0:T(128)} %bitcast.block_ref, bf16[32,144,128]{2,1,0:T(8,128)(2,1)S(1)} %all-to-all-done.recv_ref, bf16[192,192]{1,0:T(8,128)(2,1)S(1)} %copy-done.8, bf16[2,8,96,96]{3,2,1,0:T(8,128)(2,1)S(1)} %copy-done.4, f32[2,768]{1,0:T(2,128)S(1)} %copy-done.6, ...), custom_call_target="tpu_custom_call" | custom-call | flops 1000000000 | bytes 6000000 | tf_op jit(solution)/shard_map/spectral_grads/pallas_call | solution.py:410
  52.9 10.2 %all-to-all-start.1 = ((bf16[16,24,128]{2,1,0:T(8,128)(2,1)}), bf16[16,24,128]{2,1,0:T(8,128)(2,1)S(1)}, u32[]{:S(2)}, u32[]{:S(2)}) async-start(bf16[16,24,128]{2,1,0:T(8,128)(2,1)} %get-tuple-element.23), calls=%async_computation.1 | async-start | bytes 196608 | tf_op jit(solution)/shard_map/all_to_all | solution.py:640
  63.1 6.6 %spectral_return.1 = (bf16[32,72,128]{2,1,0:T(8,128)(2,1)S(1)}, bf16[32,96,128]{2,1,0:T(8,128)(2,1)}) custom-call(s32[1]{0:T(128)} %bitcast.block_ref, bf16[2,1536,256]{2,1,0:T(8,128)(2,1)} %get-tuple-element.21.saved_ref, bf16[192,192]{1,0:T(8,128)(2,1)S(1)} %copy-done.8, bf16[2,8,96,96]{3,2,1,0:T(8,128)(2,1)S(1)} %copy-done.4, ...), custom_call_target="tpu_custom_call" | custom-call | flops 1000000000 | bytes 6000000 | tf_op jit(solution)/shard_map/spectral_return/pallas_call | solution.py:410
  69.7 1.8 %all-to-all-done.1.recv_ref = bf16[16,24,128]{2,1,0:T(8,128)(2,1)S(1)} async-done(((bf16[16,24,128]{2,1,0:T(8,128)(2,1)}), bf16[16,24,128]{2,1,0:T(8,128)(2,1)S(1)}, u32[]{:S(2)}, u32[]{:S(2)}) %all-to-all-start.1) | async-done | bytes 98336 | tf_op jit(solution)/shard_map/all_to_all | solution.py:640
  71.6 0.1 grad_share.1
  71.6 23.3 %all_to_all.20.early_ref.recv_ref = bf16[32,72,128]{2,1,0:T(8,128)(2,1)S(1)} all-to-all(bf16[32,72,128]{2,1,0:T(8,128)(2,1)S(1)} %grad_share.1), channel_id=1, replica_groups=mesh['dp'=16,'lat'=32] {'lat'}, dimensions={0} | all-to-all | bytes 1179648 | tf_op jit(solution)/shard_map/all_to_all | solution.py:611
  94.9 5.1 %all-to-all-start.3 = ((bf16[32,96,128]{2,1,0:T(8,128)(2,1)}), bf16[32,96,128]{2,1,0:T(8,128)(2,1)S(1)}, u32[]{:S(2)}, u32[]{:S(2)}) async-start(bf16[32,96,128]{2,1,0:T(8,128)(2,1)} %get-tuple-element.26), calls=%async_computation.3 | async-start | bytes 1572864 | tf_op jit(solution)/shard_map/all_to_all | solution.py:611
  100.0 0.0 copy-start
  100.0 0.0 copy-start.1
  100.0 0.0 copy-start.2
  100.0 0.0 copy-start.3
  100.1 18.8 %all-gather = bf16[128,24,128]{2,1,0:T(8,128)(2,1)S(1)} all-gather(bf16[8,24,128]{2,1,0:T(8,128)(2,1)S(1)} %grad_groups.1), channel_id=2, replica_groups=mesh['dp'=16,'lat'=32] {'dp'}, dimensions={0}, use_global_device_ids=true | all-gather | bytes 835584 | tf_op jit(solution)/shard_map/all_gather | solution.py:662
  118.9 1.5 %grad_out.1 = (f32[2,8,96,96]{3,2,1,0:T(8,128)}, f32[2,768]{1,0:T(2,128)}, f32[2,8,96,96]{3,2,1,0:T(8,128)}, f32[2,768]{1,0:T(2,128)}) custom-call(bf16[16,8,24,128]{3,2,1,0:T(8,128)(2,1)S(1)} %bitcast.2), custom_call_target="tpu_custom_call" | custom-call | flops 1000000 | bytes 1000000 | tf_op jit(solution)/shard_map/grad_out/pallas_call | solution.py:521
  120.4 0.4 all-to-all-done.3.late_ref
  120.8 5.0 %from_spectra.1 = (bf16[1,3,180,768]{3,2,1,0:T(8,128)(2,1)}, bf16[1,3,180,768]{3,2,1,0:T(8,128)(2,1)}) custom-call(bf16[32,72,128]{2,1,0:T(8,128)(2,1)S(1)} %all_to_all.20.early_ref.recv_ref, bf16[32,96,128]{2,1,0:T(8,128)(2,1)S(1)} %all-to-all-done.3.late_ref, bf16[1,3,180,768]{3,2,1,0:T(8,128)(2,1)S(1)} %copy-done, ...), custom_call_target="tpu_custom_call" | custom-call | flops 212336640 | bytes 5000000 | tf_op jit(solution)/shard_map/from_spectra/pallas_call | solution.py:494
  (9 shorter events, 0.1 us)
Async XLA Ops:
  5.4 42.6 %copy-start.4 = (bf16[2,8,96,96]{3,2,1,0:T(8,128)(2,1)S(1)}, bf16[2,8,96,96]{3,2,1,0:T(8,128)(2,1)}, u32[]{:S(2)}) copy-start(bf16[2,8,96,96]{3,2,1,0:T(8,128)(2,1)} %first_ref.3) | copy-start | bytes 884740
  5.4 42.6 %copy-start.5 = (bf16[2,8,96,96]{3,2,1,0:T(8,128)(2,1)S(1)}, bf16[2,8,96,96]{3,2,1,0:T(8,128)(2,1)}, u32[]{:S(2)}) copy-start(bf16[2,8,96,96]{3,2,1,0:T(8,128)(2,1)} %second_ref.3) | copy-start | bytes 884740
  5.4 42.6 %copy-start.6 = (f32[2,768]{1,0:T(2,128)S(1)}, f32[2,768]{1,0:T(2,128)}, u32[]{:S(2)}) copy-start(f32[2,768]{1,0:T(2,128)} %bias_ref.2) | copy-start | bytes 18436
  5.4 42.6 %copy-start.8 = (bf16[192,192]{1,0:T(8,128)(2,1)S(1)}, bf16[192,192]{1,0:T(8,128)(2,1)}, u32[]{:S(2)}) copy-start(bf16[192,192]{1,0:T(8,128)(2,1)} %constant.34.clone.lat_ref) | copy-start | bytes 221188
  5.4 42.5 %all-to-all-start = ((bf16[32,144,128]{2,1,0:T(8,128)(2,1)}), bf16[32,144,128]{2,1,0:T(8,128)(2,1)S(1)}, u32[]{:S(2)}, u32[]{:S(2)}) async-start(bf16[32,144,128]{2,1,0:T(8,128)(2,1)} %get-tuple-element.20), calls=%async_computation | async-start | bytes 2359296 | tf_op jit(solution)/shard_map/all_to_all | solution.py:611
  48.0 15.1 %copy-start.7 = (f32[2,768]{1,0:T(2,128)S(1)}, f32[2,768]{1,0:T(2,128)}, u32[]{:S(2)}) copy-start(f32[2,768]{1,0:T(2,128)} %bias_ref.3) | copy-start | bytes 18436
  52.9 18.7 %all-to-all-start.1 = ((bf16[16,24,128]{2,1,0:T(8,128)(2,1)}), bf16[16,24,128]{2,1,0:T(8,128)(2,1)S(1)}, u32[]{:S(2)}, u32[]{:S(2)}) async-start(bf16[16,24,128]{2,1,0:T(8,128)(2,1)} %get-tuple-element.23), calls=%async_computation.1 | async-start | bytes 196608 | tf_op jit(solution)/shard_map/all_to_all | solution.py:640
  94.9 25.9 %all-to-all-start.3 = ((bf16[32,96,128]{2,1,0:T(8,128)(2,1)}), bf16[32,96,128]{2,1,0:T(8,128)(2,1)S(1)}, u32[]{:S(2)}, u32[]{:S(2)}) async-start(bf16[32,96,128]{2,1,0:T(8,128)(2,1)} %get-tuple-element.26), calls=%async_computation.3 | async-start | bytes 1572864 | tf_op jit(solution)/shard_map/all_to_all | solution.py:611
  100.0 20.8 %copy-start = (bf16[1,3,180,768]{3,2,1,0:T(8,128)(2,1)S(1)}, bf16[1,3,180,768]{3,2,1,0:T(8,128)(2,1)}, u32[]{:S(2)}) copy-start(bf16[1,3,180,768]{3,2,1,0:T(8,128)(2,1)} %x_ref.3) | copy-start | bytes 2488324
  100.0 20.8 %copy-start.1 = (bf16[1,3,180,768]{3,2,1,0:T(8,128)(2,1)S(1)}, bf16[1,3,180,768]{3,2,1,0:T(8,128)(2,1)}, u32[]{:S(2)}) copy-start(bf16[1,3,180,768]{3,2,1,0:T(8,128)(2,1)} %g_ref.3) | copy-start | bytes 2488324
  100.0 20.8 %copy-start.2 = (bf16[192,128]{1,0:T(8,128)(2,1)S(1)}, bf16[192,128]{1,0:T(8,128)(2,1)}, u32[]{:S(2)}) copy-start(bf16[192,128]{1,0:T(8,128)(2,1)} %constant.31.clone.inv_ref) | copy-start | bytes 147460
  100.0 20.8 %copy-start.3 = (bf16[192,128]{1,0:T(8,128)(2,1)S(1)}, bf16[192,128]{1,0:T(8,128)(2,1)}, u32[]{:S(2)}) copy-start(bf16[192,128]{1,0:T(8,128)(2,1)} %constant.30.clone.fwd_ref) | copy-start | bytes 147460

commit v6 on v5

--- a/solution.py
+++ b/solution.py
@@ -112,7 +112,7 @@
     centered = values - mean
     spread = jnp.sum(centered * centered, axis=-1, keepdims=True) * (1.0 / C)
     scale = 1.0 / jnp.sqrt(spread + EPSILON)
-    return centered * scale, mean, scale
+    return centered * scale, scale
 
 
 def send_packed(acc_ref, out_ref):
@@ -127,8 +127,8 @@
 
 
 def spectra_kernel(
-    x_ref, g_ref, fwd_ref, inv_ref, out_ref, moments_ref,
-    x_rows, g_rows, fwd_table, inv_table, padded_ref, acc_ref, send_ref, kept_ref, sems, out_sems,
+    x_ref, g_ref, fwd_ref, inv_ref, out_ref,
+    x_rows, g_rows, fwd_table, inv_table, padded_ref, acc_ref, send_ref, sems, out_sems,
 ):
     copies = [pltpu.make_async_copy(x_ref.at[0, 0], x_rows.at[0], sems.at[0])]
     copies += [pltpu.make_async_copy(fwd_ref, fwd_table, sems.at[1])]
@@ -148,15 +148,10 @@
         copies[0 if r == 0 else 1 + r].wait()
         for start, size in ROW_CHUNKS:
             values = x_rows[r, start : start + size].astype(F32)
-            normed, mean, scale = normalize(values)
-            padded_ref[start : start + size] = normed.astype(BF)
-            kept_ref[r, start : start + size, 0:128] = jnp.broadcast_to(mean, (size, 128))
-            kept_ref[r, start : start + size, 128:256] = jnp.broadcast_to(scale, (size, 128))
+            padded_ref[start : start + size] = normalize(values)[0].astype(BF)
         if r == 0:
             copies[1].wait()
         acc_ref[r] = jnp.dot(fwd_table[...], padded_ref[...], preferred_element_type=F32)
-    moments_out = pltpu.make_async_copy(kept_ref, moments_ref, out_sems.at[2])
-    moments_out.start()
     send_packed(acc_ref, send_ref.at[0])
     fields_out = pltpu.make_async_copy(
         send_ref.at[0], out_ref.at[:, pl.ds(0, PACK), :], out_sems.at[0]
@@ -172,7 +167,6 @@
         send_ref.at[1], out_ref.at[:, pl.ds(PACK, PACK), :], out_sems.at[1]
     )
     back_out.start()
-    moments_out.wait()
     fields_out.wait()
     back_out.wait()
 
@@ -183,11 +177,8 @@
         spectra_kernel,
         name="to_spectra",
         in_specs=[held, held, held, held],
-        out_specs=[held, held],
-        out_shape=[
-            pltpu.HBM((BANDS, 2 * PACK, 128), BF),
-            pltpu.HBM((ROWS, W, 256), F32),
-        ],
+        out_specs=held,
+        out_shape=pltpu.HBM((BANDS, 2 * PACK, 128), BF),
         scratch_shapes=[
             pltpu.VMEM((ROWS, W, C), BF),
             pltpu.VMEM((ROWS, W, C), BF),
@@ -196,9 +187,8 @@
             pltpu.VMEM((WPAD, C), BF),
             pltpu.VMEM((ROWS, 2 * KX, C), F32),
             pltpu.VMEM((2, BANDS, PACK, 128), BF),
-            pltpu.VMEM((ROWS, W, 256), F32),
             pltpu.SemaphoreType.DMA((2 + 2 * ROWS,)),
-            pltpu.SemaphoreType.DMA((3,)),
+            pltpu.SemaphoreType.DMA((2,)),
         ],
         compiler_params=pltpu.CompilerParams(vmem_limit_bytes=VMEM_LIMIT),
         cost_estimate=pl.CostEstimate(
@@ -207,7 +197,12 @@
     )(*[pltpu.with_memory_space_constraint(a, pltpu.HBM) for a in (fields, cotangent, forward, inverse)])
 
 
-TILE_ROWS = 2 * ROWS * MODES
+PITCH = 20
+BAND_PITCH = 2 * ROWS * PITCH
+
+
+def eight_rows(base, row):
+    return pl.ds(base + PITCH * (row // MODES) + row % MODES, 8)
 
 
 def unpack_bands(recv_ref, first, rows_ref):
@@ -216,10 +211,10 @@
             recv_ref[s, first + 24 * i : first + 24 * i + 24, :].astype(F32)
             for i in range(3)
         ]
-        base = pl.multiple_of(s * TILE_ROWS, TILE_ROWS)
-        for i in range(3):
-            rows_ref[pl.ds(base + 24 * i, 24), :] = pieces[i]
-        rows_ref[pl.ds(base + 72, 24), :] = unpack_tail(pieces)
+        base = pl.multiple_of(s * BAND_PITCH, 8)
+        for i, piece in enumerate(pieces + [unpack_tail(pieces)]):
+            for u in range(0, 24, 8):
+                rows_ref[eight_rows(base, 24 * i + u), :] = piece[u : u + 8]
         return carry
 
     lax.fori_loop(0, BANDS, one, 0, unroll=4)
@@ -227,10 +222,16 @@
 
 def pack_bands(rows_ref, back_rows_ref, early_ref, late_ref, first):
     def one(s, carry):
-        base = pl.multiple_of(s * TILE_ROWS, TILE_ROWS)
-        pieces = pack_tile(rows_ref[pl.ds(base, TILE_ROWS), :])
+        base = pl.multiple_of(s * BAND_PITCH, 8)
+
+        def tile(ref):
+            return jnp.concatenate(
+                [ref[eight_rows(base, row), :] for row in range(0, 96, 8)], axis=0
+            )
+
+        pieces = pack_tile(tile(rows_ref))
         early_ref[s, 0:48] = jnp.concatenate(pieces[:2], axis=0).astype(BF)
-        back = pack_tile(back_rows_ref[pl.ds(base, TILE_ROWS), :])
+        back = pack_tile(tile(back_rows_ref))
         late_ref[s] = jnp.concatenate(pieces[2:] + back, axis=0).astype(BF)
         return carry
 
@@ -240,7 +241,7 @@
 def mode_rows(rows_ref, lat, pair):
     columns = jnp.concatenate(
         [
-            rows_ref[pl.ds(2 * pair + j, 2 * H, stride=MODES), :].astype(BF)
+            rows_ref[pl.ds(2 * pair + j, 2 * H, stride=PITCH), :].astype(BF)
             for j in range(2)
         ],
         axis=1,
@@ -258,25 +259,21 @@
     )
 
 
-def store_rows(rows_ref, lat, pair, modes):
-    columns = jnp.concatenate(
-        [
-            jnp.concatenate(
-                [modes[H * j : H * j + H, 0:128], modes[H * j : H * j + H, 128:256]], axis=0
-            )
-            for j in range(2)
-        ],
-        axis=1,
-    )
-    done = lax.dot_general(
-        lat, columns, (((0,), (0,)), ((), ())), preferred_element_type=F32
-    )
+def spread(columns_ref, pair, modes):
     for j in range(2):
-        rows_ref[pl.ds(2 * pair + j, 2 * H, stride=MODES), :] = done[:, 128 * j : 128 * j + 128]
-
-
-PAIR_ROWS = 2 * H
-PAIRS = MODES // 2
+        lane = 128 * (2 * pair + j)
+        for part in range(2):
+            columns_ref[H * part : H * part + H, lane : lane + 128] = modes[
+                H * j : H * j + H, 128 * part : 128 * part + 128
+            ]
+
+
+def store_rows(rows_ref, lat_t, columns_ref, pair):
+    done = jnp.dot(
+        lat_t, columns_ref[:, 256 * pair : 256 * pair + 256], preferred_element_type=F32
+    )
+    for j in range(2):
+        rows_ref[pl.ds(2 * pair + j, 2 * H, stride=PITCH), :] = done[:, 128 * j : 128 * j + 128]
 
 
 def fill_weight(weight_ref, form_ref):
@@ -300,6 +297,17 @@
 
 NT = (((1,), (1,)), ((), ()))
 TN = (((0,), (0,)), ((), ()))
+
+
+def with_one(value):
+    return jnp.where(lanes(value.shape) == BS, jnp.ones_like(value), value)
+
+
+def half_copy(source_ref, target_ref, sems, half):
+    rows = pl.ds(HALF_PAIRS * PAIR_ROWS * half, HALF_PAIRS * PAIR_ROWS)
+    return pltpu.make_async_copy(
+        source_ref.at[:, rows, :], target_ref.at[:, rows, :], sems.at[half]
+    )
 
 
 def gradient_kernel(
@@ -319,22 +327,22 @@
     for pair in range(PAIRS):
         span = slice(PAIR_ROWS * pair, PAIR_ROWS * pair + PAIR_ROWS)
         modes = mode_rows(rows_ref, lat, pair)
+        modes = jnp.concatenate([with_one(modes[:, 0:128]), modes[:, 128:256]], axis=1)
         modes_ref[span] = modes
         pre = jnp.dot(modes, w1, preferred_element_type=F32) + bias
         cdf = 0.5 + 0.5 * lax.erf(pre * math.sqrt(0.5))
-        kept_ref[0, span] = (pre * cdf).astype(BF)
+        hidden = (pre * cdf).astype(BF)
+        hidden = jnp.concatenate([with_one(hidden[:, 0:128]), hidden[:, 128:256]], axis=1)
+        kept_ref[0, span] = hidden
         slope = cdf + pre * (jnp.exp(-0.5 * pre * pre) * (1.0 / math.sqrt(2.0 * math.pi)))
         back_filtered = mode_rows(back_rows_ref, lat, pair)
         filtered_ref[span] = back_filtered
         back_hidden = lax.dot_general(back_filtered, w2, NT, preferred_element_type=F32)
         kept_ref[1, span] = (back_hidden * slope).astype(BF)
-        pair_rows = pl.ds(PAIR_ROWS * pair, PAIR_ROWS)
-        save = pltpu.make_async_copy(
-            kept_ref.at[:, pair_rows, :], saved_ref.at[:, pair_rows, :], sems.at[pair]
-        )
-        save.start()
-        saves.append(save)
-    ones = jnp.ones((8, MODES * H), BF)
+        if (pair + 1) % HALF_PAIRS == 0:
+            save = half_copy(kept_ref, saved_ref, sems, pair // HALF_PAIRS)
+            save.start()
+            saves.append(save)
     row = 0
     bias_rows = []
     for left_ref, right_ref in ((modes_ref, kept_ref.at[1]), (kept_ref.at[0], filtered_ref)):
@@ -346,8 +354,7 @@
             for piece in pack_tile(part):
                 sums_ref[row : row + 24] = piece
                 row += 24
-        bias = jnp.dot(ones, right, preferred_element_type=F32)
-        bias_rows += [bias[:, 0:128], bias[:, 128:256]]
+        bias_rows += [gathered[BS : BS + 8, 0:128], gathered[BS : BS + 8, 128:256]]
     for value in bias_rows:
         sums_ref[row : row + 8] = value
         row += 8
@@ -363,29 +370,29 @@
 def return_kernel(
     block_ref, saved_ref, lat_ref, first_ref, second_ref, bias_ref,
     early_ref, sent_ref,
-    w1_ref, w2_ref, rows_ref, back_rows_ref, kept_ref, late_ref, sems, out_sems,
+    w1_ref, w2_ref, rows_ref, back_rows_ref, columns_ref, back_columns_ref,
+    kept_ref, late_ref, sems, out_sems,
 ):
-    fetches = []
-    for pair in range(PAIRS):
-        pair_rows = pl.ds(PAIR_ROWS * pair, PAIR_ROWS)
-        fetch = pltpu.make_async_copy(
-            saved_ref.at[:, pair_rows, :], kept_ref.at[:, pair_rows, :], sems.at[pair]
-        )
+    fetches = [half_copy(saved_ref, kept_ref, sems, half) for half in range(2)]
+    for fetch in fetches:
         fetch.start()
-        fetches.append(fetch)
     fill_weight(first_ref, w1_ref)
     fill_weight(second_ref, w2_ref)
     bias = choose_bias(block_ref[0], bias_ref)
-    lat = lat_ref[...]
+    lat_t = lat_ref[...]
     w1 = w1_ref[...]
     w2 = w2_ref[...]
     for pair in range(PAIRS):
         span = slice(PAIR_ROWS * pair, PAIR_ROWS * pair + PAIR_ROWS)
-        fetches[pair].wait()
+        if pair % HALF_PAIRS == 0:
+            fetches[pair // HALF_PAIRS].wait()
         filtered = jnp.dot(kept_ref[0, span], w2, preferred_element_type=F32) + bias
-        store_rows(rows_ref, lat, pair, filtered.astype(BF))
+        spread(columns_ref, pair, filtered.astype(BF))
         back_modes = lax.dot_general(kept_ref[1, span], w1, NT, preferred_element_type=F32)
-        store_rows(back_rows_ref, lat, pair, back_modes.astype(BF))
+        spread(back_columns_ref, pair, back_modes.astype(BF))
+    for pair in range(PAIRS):
+        store_rows(rows_ref, lat_t, columns_ref, pair)
+        store_rows(back_rows_ref, lat_t, back_columns_ref, pair)
     leaving = []
     for part in range(4):
         pack_bands(rows_ref, back_rows_ref, early_ref, late_ref, part * (BANDS // 4))
@@ -401,9 +408,11 @@
 
 PAIR_ROWS = 2 * H
 PAIRS = MODES // 2
+HALF_PAIRS = PAIRS // 2
 WIDE = (MODES * H, 256)
 FORM = pltpu.VMEM((256, 256), BF)
-BAND_ROWS = pltpu.VMEM((2 * H * MODES, 128), F32)
+COLUMNS = pltpu.VMEM((2 * H, MODES * 128), BF)
+BAND_ROWS = pltpu.VMEM((2 * H * PITCH, 128), F32)
 
 
 def block_call(kernel, name, block, operands, specs, outs, places, scratch):
@@ -458,27 +467,23 @@
 
 
 def output_kernel(
-    early_ref, late_ref, x_ref, moments_ref, g_ref, fwd_ref, inv_ref,
+    early_ref, late_ref, x_ref, g_ref, fwd_ref, inv_ref,
     out_ref, grad_ref,
-    rows_ref, back_rows_ref, mixed_ref, back_ref, held_ref, sem,
+    rows_ref, back_rows_ref, mixed_ref, back_ref,
 ):
     r = pl.program_id(0)
 
     @pl.when(r == 0)
     def _():
-        fetch = pltpu.make_async_copy(moments_ref, held_ref, sem)
-        fetch.start()
         receive(((early_ref, 0), (early_ref, 24), (late_ref, 0)), rows_ref)
         receive(((late_ref, 24), (late_ref, 48), (late_ref, 72)), back_rows_ref)
-        fetch.wait()
 
     mixed_ref[...] = jnp.dot(inv_ref[...], rows_ref[r], preferred_element_type=F32)
     back_ref[...] = jnp.dot(fwd_ref[...], back_rows_ref[r], preferred_element_type=F32)
     for start, size in ROW_CHUNKS:
         span = slice(start, start + size)
         values = x_ref[0, r, span].astype(F32)
-        scale = held_ref[r, span, 128:256][:, 0:1]
-        normed = (values - held_ref[r, span, 0:128][:, 0:1]) * scale
+        normed, scale = normalize(values)
         out_ref[0, 0, span] = (values + normed + mixed_ref[span]).astype(BF)
         upstream = g_ref[0, r, span].astype(F32)
         back = upstream + back_ref[span]
@@ -487,7 +492,7 @@
         grad_ref[0, 0, span] = (upstream + scale * (back - mean - normed * along)).astype(BF)
 
 
-def from_spectra(early, late, fields, moments, cotangent, forward, inverse):
+def from_spectra(early, late, fields, cotangent, forward, inverse):
     token_spec = pl.BlockSpec((1, 1, W, C), lambda r: (0, r, 0, 0))
     near = pl.BlockSpec(memory_space=pltpu.VMEM)
     token = jax.ShapeDtypeStruct((1, ROWS, W, C), BF)
@@ -495,7 +500,7 @@
         output_kernel,
         name="from_spectra",
         grid=(ROWS,),
-        in_specs=[near] * 3 + [pl.BlockSpec(memory_space=pltpu.HBM)] + [near] * 3,
+        in_specs=[near] * 6,
         out_specs=[token_spec, token_spec],
         out_shape=[token, token],
         scratch_shapes=[
@@ -503,14 +508,12 @@
             pltpu.VMEM((ROWS, 2 * KX, C), BF),
             pltpu.VMEM((WPAD, C), F32),
             pltpu.VMEM((WPAD, C), F32),
-            pltpu.VMEM((ROWS, W, 256), F32),
-            pltpu.SemaphoreType.DMA,
         ],
         compiler_params=pltpu.CompilerParams(vmem_limit_bytes=VMEM_LIMIT),
         cost_estimate=pl.CostEstimate(
             flops=4 * ROWS * W * 2 * KX * C, bytes_accessed=5000000, transcendentals=0
         ),
-    )(early, late, fields, moments, cotangent, forward, inverse)
+    )(early, late, fields, cotangent, forward, inverse)
 
 
 def whole(shape):
@@ -618,9 +621,9 @@
     lon_fwd_t = jnp.asarray(LON_FWD.T, BF)
     lon_inv_t = jnp.asarray(LON_INV.T, BF)
     lat = jnp.asarray(LAT, BF)
-
-    spectra, moments = to_spectra(fields, cotangent, lon_fwd_t, lon_inv_t)
-    moments = pltpu.with_memory_space_constraint(moments, pltpu.HBM)
+    lat_t = jnp.asarray(LAT.T, BF)
+
+    spectra = to_spectra(fields, cotangent, lon_fwd_t, lon_inv_t)
     spectra = exchange(spectra)
     kept, grads = block_call(
         gradient_kernel,
@@ -632,7 +635,7 @@
         ("far", "near"),
         [FORM, FORM, BAND_ROWS, BAND_ROWS, pltpu.VMEM(WIDE, BF), pltpu.VMEM(WIDE, BF)]
         + [pltpu.VMEM((CHUNKS * CHUNK_ROWS, 128), F32), pltpu.VMEM((2,) + WIDE, BF)]
-        + [pltpu.SemaphoreType.DMA((PAIRS,))],
+        + [pltpu.SemaphoreType.DMA((2,))],
     )
     kept = pltpu.with_memory_space_constraint(kept, pltpu.HBM)
     dp_size = lax.axis_size("dp")
@@ -644,16 +647,16 @@
         return_kernel,
         "spectral_return",
         block,
-        (kept, lat, w_first, w_second, b_second),
+        (kept, lat_t, w_first, w_second, b_second),
         ("far", "", "weight", "weight", ""),
         [
             jax.ShapeDtypeStruct((BANDS, PACK, 128), BF),
             jax.ShapeDtypeStruct((BANDS, 96, 128), BF),
         ],
         ("near", "far"),
-        [FORM, FORM, BAND_ROWS, BAND_ROWS, pltpu.VMEM((2,) + WIDE, BF)]
+        [FORM, FORM, BAND_ROWS, BAND_ROWS, COLUMNS, COLUMNS, pltpu.VMEM((2,) + WIDE, BF)]
         + [pltpu.VMEM((BANDS, 96, 128), BF)]
-        + [pltpu.SemaphoreType.DMA((PAIRS,)), pltpu.SemaphoreType.DMA((4,))],
+        + [pltpu.SemaphoreType.DMA((2,)), pltpu.SemaphoreType.DMA((4,))],
     )
     early = exchange(add_share(shares, early))
     late, early = lax.optimization_barrier((late, early))
@@ -667,9 +670,7 @@
     g_w1, g_b1, g_w2, g_b2 = spectral_call(
         grads_kernel, "grad_out", (every,), [grad_w, grad_b, grad_w, grad_b], []
     )
-    result, back_fields = from_spectra(
-        early, late, fields, moments, cotangent, lon_fwd, lon_inv
-    )
+    result, back_fields = from_spectra(early, late, fields, cotangent, lon_fwd, lon_inv)
     return (result, back_fields, g_w1, g_b1, g_w2, g_b2)
 
 

time: 128 us -> 127 us (level)
  Pallas kernels: 22.8 us -> 19.2 us
  waiting for transfers between devices: 30.9 us -> 34.1 us
    pallas_call x2, Pallas kernels: 11.5 us -> 8.88 us  [block_call(): pl.pallas_call(kernel, name=name, grid_spec=pltpu.PrefetchScalarGridSpec(...]
    all_to_all x1, waiting for transfers between devices: 1.82 us -> 4.35 us  [on_device(): shares = lax.all_to_all(grads, 'dp', 0, 0, tiled=True)]
  transfers between devices with their start and end apart: 3 -> 3, of which waited for: 3 -> 3; matrix products, arithmetic and copies ran while one was open for 0% -> 0% of each run, Pallas kernels for 6% -> 5%
where the time goes in v6:
time: 127 us; the launch traced here: 125 us
  blocking collectives  41.4 us (33%)
  waiting for transfers between devices  34.1 us (27%)
  starting transfers between devices  29.1 us (23%)
  Pallas kernels  19.2 us (15%)
    all_to_all x2, waiting for transfers between devices, exchange(): return lax.all_to_all(value, 'lat', split_axis=0, concat_axis=0, tiled=True)  29.7 us
    all_to_all x1, blocking collectives, exchange(): return lax.all_to_all(value, 'lat', split_axis=0, concat_axis=0, tiled=True)  23.3 us
    all_to_all x2, starting transfers between devices, exchange(): return lax.all_to_all(value, 'lat', split_axis=0, concat_axis=0, tiled=True)  18.9 us
    all_gather x1, blocking collectives, on_device(): every = lax.all_gather(blocks, 'dp', axis=0, tiled=False)  18.2 us
    all_to_all x1, starting transfers between devices, on_device(): shares = lax.all_to_all(grads, 'dp', 0, 0, tiled=True)  10.2 us
    pallas_call x2, Pallas kernels, block_call(): pl.pallas_call(kernel, name=name, grid_spec=pltpu.PrefetchScalarGridSpec(...  8.88 us
    pallas_call x1, Pallas kernels, to_spectra(): pl.pallas_call(spectra_kernel, name='to_spectra', in_specs=[held, held, h...  4.73 us
    all_to_all x1, waiting for transfers between devices, on_device(): shares = lax.all_to_all(grads, 'dp', 0, 0, tiled=True)  4.35 us
  transfers between devices with their start and end apart: 3, of which 3 were waited for; matrix products, arithmetic and copies ran while one was open for 0% of the time, Pallas kernels for 5%

profile of v6, /device:TPU:1, one launch (start us, length us, event | category | flops | bytes accessed | tf_op | source)
XLA Modules:
  0.0 124.7 jit_solution(18418816496222057354)
XLA Ops:
  0.6 4.7 %to_spectra.1 = bf16[32,144,128]{2,1,0:T(8,128)(2,1)} custom-call(bf16[1,3,180,768]{3,2,1,0:T(8,128)(2,1)} %x_ref.3, bf16[1,3,180,768]{3,2,1,0:T(8,128)(2,1)} %g_ref.3, bf16[128,192]{1,0:T(8,128)(2,1)} %constant.34.clone.fwd_ref, bf16[128,192]{1,0:T(8,128)(2,1)} %constant.35.clone.inv_ref), custom_call_target="tpu_custom_call" | custom-call | flops 212336640 | bytes 3000000 | tf_op jit(solution)/shard_map/to_spectra/pallas_call | solution.py:176
  5.4 0.0 copy-start.4
  5.4 0.0 copy-start.5
  5.4 0.0 copy-start.6
  5.4 0.0 copy-start.9
  5.4 13.8 %all-to-all-start = ((bf16[32,144,128]{2,1,0:T(8,128)(2,1)}), bf16[32,144,128]{2,1,0:T(8,128)(2,1)S(1)}, u32[]{:S(2)}, u32[]{:S(2)}) async-start(bf16[32,144,128]{2,1,0:T(8,128)(2,1)} %to_spectra.1), calls=%async_computation | async-start | bytes 2359296 | tf_op jit(solution)/shard_map/all_to_all | solution.py:614
  19.3 28.7 %all-to-all-done.recv_ref = bf16[32,144,128]{2,1,0:T(8,128)(2,1)S(1)} async-done(((bf16[32,144,128]{2,1,0:T(8,128)(2,1)}), bf16[32,144,128]{2,1,0:T(8,128)(2,1)S(1)}, u32[]{:S(2)}, u32[]{:S(2)}) %all-to-all-start) | async-done | bytes 1179680 | tf_op jit(solution)/shard_map/all_to_all | solution.py:614
  48.0 0.0 copy-start.7
  48.0 0.0 copy-start.8
  48.0 4.8 %spectral_grads.1 = (bf16[2,1536,256]{2,1,0:T(8,128)(2,1)}, bf16[16,24,128]{2,1,0:T(8,128)(2,1)}) custom-call(s32[1]{0:T(128)} %bitcast.block_ref, bf16[32,144,128]{2,1,0:T(8,128)(2,1)S(1)} %all-to-all-done.recv_ref, bf16[192,192]{1,0:T(8,128)(2,1)S(1)} %copy-done.9, bf16[2,8,96,96]{3,2,1,0:T(8,128)(2,1)S(1)} %copy-done.4, f32[2,768]{1,0:T(2,128)S(1)} %copy-done.6, ...), custom_call_target="tpu_custom_call" | custom-call | flops 1000000000 | bytes 6000000 | tf_op jit(solution)/shard_map/spectral_grads/pallas_call | solution.py:419
  52.8 10.2 %all-to-all-start.1 = ((bf16[16,24,128]{2,1,0:T(8,128)(2,1)}), bf16[16,24,128]{2,1,0:T(8,128)(2,1)S(1)}, u32[]{:S(2)}, u32[]{:S(2)}) async-start(bf16[16,24,128]{2,1,0:T(8,128)(2,1)} %get-tuple-element.20), calls=%async_computation.1 | async-start | bytes 196608 | tf_op jit(solution)/shard_map/all_to_all | solution.py:643
  63.0 4.1 %spectral_return.1 = (bf16[32,72,128]{2,1,0:T(8,128)(2,1)S(1)}, bf16[32,96,128]{2,1,0:T(8,128)(2,1)}) custom-call(s32[1]{0:T(128)} %bitcast.block_ref, bf16[2,1536,256]{2,1,0:T(8,128)(2,1)} %get-tuple-element.18.saved_ref, bf16[192,192]{1,0:T(8,128)(2,1)S(1)} %copy-done.8, bf16[2,8,96,96]{3,2,1,0:T(8,128)(2,1)S(1)} %copy-done.4, ...), custom_call_target="tpu_custom_call" | custom-call | flops 1000000000 | bytes 6000000 | tf_op jit(solution)/shard_map/spectral_return/pallas_call | solution.py:419
  67.1 4.3 %all-to-all-done.1.recv_ref = bf16[16,24,128]{2,1,0:T(8,128)(2,1)S(1)} async-done(((bf16[16,24,128]{2,1,0:T(8,128)(2,1)}), bf16[16,24,128]{2,1,0:T(8,128)(2,1)S(1)}, u32[]{:S(2)}, u32[]{:S(2)}) %all-to-all-start.1) | async-done | bytes 98336 | tf_op jit(solution)/shard_map/all_to_all | solution.py:643
  71.5 0.1 grad_share.1
  71.5 23.3 %all_to_all.20.early_ref.recv_ref = bf16[32,72,128]{2,1,0:T(8,128)(2,1)S(1)} all-to-all(bf16[32,72,128]{2,1,0:T(8,128)(2,1)S(1)} %grad_share.1), channel_id=1, replica_groups=mesh['dp'=16,'lat'=32] {'lat'}, dimensions={0} | all-to-all | bytes 1179648 | tf_op jit(solution)/shard_map/all_to_all | solution.py:614
  94.8 5.1 %all-to-all-start.3 = ((bf16[32,96,128]{2,1,0:T(8,128)(2,1)}), bf16[32,96,128]{2,1,0:T(8,128)(2,1)S(1)}, u32[]{:S(2)}, u32[]{:S(2)}) async-start(bf16[32,96,128]{2,1,0:T(8,128)(2,1)} %get-tuple-element.23), calls=%async_computation.3 | async-start | bytes 1572864 | tf_op jit(solution)/shard_map/all_to_all | solution.py:614
  99.9 0.0 copy-start
  99.9 0.0 copy-start.1
  99.9 0.0 copy-start.2
  99.9 0.0 copy-start.3
  100.0 18.2 %all-gather = bf16[128,24,128]{2,1,0:T(8,128)(2,1)S(1)} all-gather(bf16[8,24,128]{2,1,0:T(8,128)(2,1)S(1)} %grad_groups.1), channel_id=2, replica_groups=mesh['dp'=16,'lat'=32] {'dp'}, dimensions={0}, use_global_device_ids=true | all-gather | bytes 835584 | tf_op jit(solution)/shard_map/all_gather | solution.py:665
  118.1 1.5 %grad_out.1 = (f32[2,8,96,96]{3,2,1,0:T(8,128)}, f32[2,768]{1,0:T(2,128)}, f32[2,8,96,96]{3,2,1,0:T(8,128)}, f32[2,768]{1,0:T(2,128)}) custom-call(bf16[16,8,24,128]{3,2,1,0:T(8,128)(2,1)S(1)} %bitcast.2), custom_call_target="tpu_custom_call" | custom-call | flops 1000000 | bytes 1000000 | tf_op jit(solution)/shard_map/grad_out/pallas_call | solution.py:524
  119.6 1.1 all-to-all-done.3.late_ref
  120.7 4.0 %from_spectra.1 = (bf16[1,3,180,768]{3,2,1,0:T(8,128)(2,1)}, bf16[1,3,180,768]{3,2,1,0:T(8,128)(2,1)}) custom-call(bf16[32,72,128]{2,1,0:T(8,128)(2,1)S(1)} %all_to_all.20.early_ref.recv_ref, bf16[32,96,128]{2,1,0:T(8,128)(2,1)S(1)} %all-to-all-done.3.late_ref, bf16[1,3,180,768]{3,2,1,0:T(8,128)(2,1)S(1)} %copy-done, bf16[1,3,180,768]{3,2,1,0:T(8,128)(2,1)S(1)} %copy-done.1, ...), custom_call_target="tpu_custom_call" | custom-call | flops 212336640 | bytes 5000000 | tf_op jit(solution)/shard_map/from_spectra/pallas_call | solution.py:499
  (11 shorter events, 0.1 us)
Async XLA Ops:
  5.4 42.6 %copy-start.4 = (bf16[2,8,96,96]{3,2,1,0:T(8,128)(2,1)S(1)}, bf16[2,8,96,96]{3,2,1,0:T(8,128)(2,1)}, u32[]{:S(2)}) copy-start(bf16[2,8,96,96]{3,2,1,0:T(8,128)(2,1)} %first_ref.3) | copy-start | bytes 884740
  5.4 42.6 %copy-start.5 = (bf16[2,8,96,96]{3,2,1,0:T(8,128)(2,1)S(1)}, bf16[2,8,96,96]{3,2,1,0:T(8,128)(2,1)}, u32[]{:S(2)}) copy-start(bf16[2,8,96,96]{3,2,1,0:T(8,128)(2,1)} %second_ref.3) | copy-start | bytes 884740
  5.4 42.5 %copy-start.6 = (f32[2,768]{1,0:T(2,128)S(1)}, f32[2,768]{1,0:T(2,128)}, u32[]{:S(2)}) copy-start(f32[2,768]{1,0:T(2,128)} %bias_ref.2) | copy-start | bytes 18436
  5.4 42.5 %copy-start.9 = (bf16[192,192]{1,0:T(8,128)(2,1)S(1)}, bf16[192,192]{1,0:T(8,128)(2,1)}, u32[]{:S(2)}) copy-start(bf16[192,192]{1,0:T(8,128)(2,1)} %constant.36.clone.lat_ref) | copy-start | bytes 221188
  5.4 42.5 %all-to-all-start = ((bf16[32,144,128]{2,1,0:T(8,128)(2,1)}), bf16[32,144,128]{2,1,0:T(8,128)(2,1)S(1)}, u32[]{:S(2)}, u32[]{:S(2)}) async-start(bf16[32,144,128]{2,1,0:T(8,128)(2,1)} %to_spectra.1), calls=%async_computation | async-start | bytes 2359296 | tf_op jit(solution)/shard_map/all_to_all | solution.py:614
  48.0 15.1 %copy-start.7 = (f32[2,768]{1,0:T(2,128)S(1)}, f32[2,768]{1,0:T(2,128)}, u32[]{:S(2)}) copy-start(f32[2,768]{1,0:T(2,128)} %bias_ref.3) | copy-start | bytes 18436
  48.0 15.1 %copy-start.8 = (bf16[192,192]{1,0:T(8,128)(2,1)S(1)}, bf16[192,192]{1,0:T(8,128)(2,1)}, u32[]{:S(2)}) copy-start(bf16[192,192]{1,0:T(8,128)(2,1)} %constant.37.clone.lat_ref) | copy-start | bytes 221188
  52.8 18.7 %all-to-all-start.1 = ((bf16[16,24,128]{2,1,0:T(8,128)(2,1)}), bf16[16,24,128]{2,1,0:T(8,128)(2,1)S(1)}, u32[]{:S(2)}, u32[]{:S(2)}) async-start(bf16[16,24,128]{2,1,0:T(8,128)(2,1)} %get-tuple-element.20), calls=%async_computation.1 | async-start | bytes 196608 | tf_op jit(solution)/shard_map/all_to_all | solution.py:643
  94.8 25.9 %all-to-all-start.3 = ((bf16[32,96,128]{2,1,0:T(8,128)(2,1)}), bf16[32,96,128]{2,1,0:T(8,128)(2,1)S(1)}, u32[]{:S(2)}, u32[]{:S(2)}) async-start(bf16[32,96,128]{2,1,0:T(8,128)(2,1)} %get-tuple-element.23), calls=%async_computation.3 | async-start | bytes 1572864 | tf_op jit(solution)/shard_map/all_to_all | solution.py:614
  99.9 20.8 %copy-start = (bf16[1,3,180,768]{3,2,1,0:T(8,128)(2,1)S(1)}, bf16[1,3,180,768]{3,2,1,0:T(8,128)(2,1)}, u32[]{:S(2)}) copy-start(bf16[1,3,180,768]{3,2,1,0:T(8,128)(2,1)} %x_ref.3) | copy-start | bytes 2488324
  99.9 20.8 %copy-start.1 = (bf16[1,3,180,768]{3,2,1,0:T(8,128)(2,1)S(1)}, bf16[1,3,180,768]{3,2,1,0:T(8,128)(2,1)}, u32[]{:S(2)}) copy-start(bf16[1,3,180,768]{3,2,1,0:T(8,128)(2,1)} %g_ref.3) | copy-start | bytes 2488324
  99.9 20.8 %copy-start.2 = (bf16[192,128]{1,0:T(8,128)(2,1)S(1)}, bf16[192,128]{1,0:T(8,128)(2,1)}, u32[]{:S(2)}) copy-start(bf16[192,128]{1,0:T(8,128)(2,1)} %constant.33.clone.inv_ref) | copy-start | bytes 147460
  99.9 20.8 %copy-start.3 = (bf16[192,128]{1,0:T(8,128)(2,1)S(1)}, bf16[192,128]{1,0:T(8,128)(2,1)}, u32[]{:S(2)}) copy-start(bf16[192,128]{1,0:T(8,128)(2,1)} %constant.32.clone.fwd_ref) | copy-start | bytes 147460

commit v7 on v6

--- a/solution.py
+++ b/solution.py
@@ -115,7 +115,7 @@
     return centered * scale, scale
 
 
-def send_packed(acc_ref, out_ref):
+def send_packed(acc_ref, out_ref, first):
     for block in range(NB):
         rows = [block_lanes(acc_ref[r], block) for r in range(ROWS)]
         for group in range(GROUPS):
@@ -123,12 +123,14 @@
                 [row[32 * group : 32 * group + 32] for row in rows], axis=0
             )
             pieces = pack_tile(tile)
-            out_ref[block * GROUPS + group] = jnp.concatenate(pieces, axis=0).astype(BF)
+            out_ref[block * GROUPS + group, first : first + PACK] = jnp.concatenate(
+                pieces, axis=0
+            ).astype(BF)
 
 
 def spectra_kernel(
     x_ref, g_ref, fwd_ref, inv_ref, out_ref,
-    x_rows, g_rows, fwd_table, inv_table, padded_ref, acc_ref, send_ref, sems, out_sems,
+    x_rows, g_rows, fwd_table, inv_table, padded_ref, acc_ref, sems,
 ):
     copies = [pltpu.make_async_copy(x_ref.at[0, 0], x_rows.at[0], sems.at[0])]
     copies += [pltpu.make_async_copy(fwd_ref, fwd_table, sems.at[1])]
@@ -152,23 +154,13 @@
         if r == 0:
             copies[1].wait()
         acc_ref[r] = jnp.dot(fwd_table[...], padded_ref[...], preferred_element_type=F32)
-    send_packed(acc_ref, send_ref.at[0])
-    fields_out = pltpu.make_async_copy(
-        send_ref.at[0], out_ref.at[:, pl.ds(0, PACK), :], out_sems.at[0]
-    )
-    fields_out.start()
-    copies[1 + ROWS].wait()
+    for copy in copies[1 + ROWS :]:
+        copy.wait()
+    send_packed(acc_ref, out_ref, 0)
     for r in range(ROWS):
-        copies[2 + ROWS + r].wait()
         padded_ref[0:W] = g_rows[r]
         acc_ref[r] = jnp.dot(inv_table[...], padded_ref[...], preferred_element_type=F32)
-    send_packed(acc_ref, send_ref.at[1])
-    back_out = pltpu.make_async_copy(
-        send_ref.at[1], out_ref.at[:, pl.ds(PACK, PACK), :], out_sems.at[1]
-    )
-    back_out.start()
-    fields_out.wait()
-    back_out.wait()
+    send_packed(acc_ref, out_ref, PACK)
 
 
 def to_spectra(fields, cotangent, forward, inverse):
@@ -177,8 +169,8 @@
         spectra_kernel,
         name="to_spectra",
         in_specs=[held, held, held, held],
-        out_specs=held,
-        out_shape=pltpu.HBM((BANDS, 2 * PACK, 128), BF),
+        out_specs=pl.BlockSpec(memory_space=pltpu.VMEM),
+        out_shape=jax.ShapeDtypeStruct((BANDS, 2 * PACK, 128), BF),
         scratch_shapes=[
             pltpu.VMEM((ROWS, W, C), BF),
             pltpu.VMEM((ROWS, W, C), BF),
@@ -186,9 +178,7 @@
             pltpu.VMEM((2 * KX, WPAD), BF),
             pltpu.VMEM((WPAD, C), BF),
             pltpu.VMEM((ROWS, 2 * KX, C), F32),
-            pltpu.VMEM((2, BANDS, PACK, 128), BF),
             pltpu.SemaphoreType.DMA((2 + 2 * ROWS,)),
-            pltpu.SemaphoreType.DMA((2,)),
         ],
         compiler_params=pltpu.CompilerParams(vmem_limit_bytes=VMEM_LIMIT),
         cost_estimate=pl.CostEstimate(
@@ -205,16 +195,17 @@
     return pl.ds(base + PITCH * (row // MODES) + row % MODES, 8)
 
 
-def unpack_bands(recv_ref, first, rows_ref):
+def unpack_bands(recv_ref, rows_ref, back_rows_ref):
     def one(s, carry):
-        pieces = [
-            recv_ref[s, first + 24 * i : first + 24 * i + 24, :].astype(F32)
-            for i in range(3)
-        ]
         base = pl.multiple_of(s * BAND_PITCH, 8)
-        for i, piece in enumerate(pieces + [unpack_tail(pieces)]):
-            for u in range(0, 24, 8):
-                rows_ref[eight_rows(base, 24 * i + u), :] = piece[u : u + 8]
+        for first, target_ref in ((0, rows_ref), (PACK, back_rows_ref)):
+            pieces = [
+                recv_ref[s, first + 24 * i : first + 24 * i + 24, :].astype(F32)
+                for i in range(3)
+            ]
+            for i, piece in enumerate(pieces + [unpack_tail(pieces)]):
+                for u in range(0, 24, 8):
+                    target_ref[eight_rows(base, 24 * i + u), :] = piece[u : u + 8]
         return carry
 
     lax.fori_loop(0, BANDS, one, 0, unroll=4)
@@ -276,10 +267,10 @@
         rows_ref[pl.ds(2 * pair + j, 2 * H, stride=PITCH), :] = done[:, 128 * j : 128 * j + 128]
 
 
-def fill_weight(weight_ref, form_ref):
+def fill_weight(weight_ref, block, form_ref):
     form_ref[...] = jnp.zeros_like(form_ref)
-    real = weight_ref[0, 0]
-    imag = weight_ref[1, 0]
+    real = weight_ref[0, block]
+    imag = weight_ref[1, block]
     form_ref[0:BS, 0:BS] = real
     form_ref[0:BS, 128 : 128 + BS] = imag
     form_ref[128 : 128 + BS, 0:BS] = -imag
@@ -315,11 +306,11 @@
     saved_ref, grad_ref,
     w1_ref, w2_ref, rows_ref, back_rows_ref, modes_ref, filtered_ref, sums_ref, kept_ref, sems,
 ):
-    fill_weight(first_ref, w1_ref)
-    fill_weight(second_ref, w2_ref)
-    bias = choose_bias(block_ref[0], bias_ref)
-    unpack_bands(recv_ref, 0, rows_ref)
-    unpack_bands(recv_ref, PACK, back_rows_ref)
+    block = block_ref[0]
+    fill_weight(first_ref, block, w1_ref)
+    fill_weight(second_ref, block, w2_ref)
+    bias = choose_bias(block, bias_ref)
+    unpack_bands(recv_ref, rows_ref, back_rows_ref)
     lat = lat_ref[...]
     w1 = w1_ref[...]
     w2 = w2_ref[...]
@@ -376,9 +367,10 @@
     fetches = [half_copy(saved_ref, kept_ref, sems, half) for half in range(2)]
     for fetch in fetches:
         fetch.start()
-    fill_weight(first_ref, w1_ref)
-    fill_weight(second_ref, w2_ref)
-    bias = choose_bias(block_ref[0], bias_ref)
+    block = block_ref[0]
+    fill_weight(first_ref, block, w1_ref)
+    fill_weight(second_ref, block, w2_ref)
+    bias = choose_bias(block, bias_ref)
     lat_t = lat_ref[...]
     w1 = w1_ref[...]
     w2 = w2_ref[...]
@@ -415,7 +407,7 @@
 BAND_ROWS = pltpu.VMEM((2 * H * PITCH, 128), F32)
 
 
-def block_call(kernel, name, block, operands, specs, outs, places, scratch):
+def block_call(kernel, name, block, operands, operand_places, outs, places, scratch):
     return pl.pallas_call(
         kernel,
         name=name,
@@ -423,12 +415,8 @@
             num_scalar_prefetch=1,
             grid=(1,),
             in_specs=[
-                pl.BlockSpec((2, 1, BS, BS), lambda i, n: (0, n[0], 0, 0))
-                if spec == "weight"
-                else pl.BlockSpec(memory_space=pltpu.HBM)
-                if spec == "far"
-                else pl.BlockSpec(memory_space=pltpu.VMEM)
-                for operand, spec in zip(operands, specs)
+                pl.BlockSpec(memory_space=pltpu.HBM if place == "far" else pltpu.VMEM)
+                for place in operand_places
             ],
             out_specs=[
                 pl.BlockSpec(memory_space=pltpu.HBM if place == "far" else pltpu.VMEM)
@@ -624,13 +612,14 @@
     lat_t = jnp.asarray(LAT.T, BF)
 
     spectra = to_spectra(fields, cotangent, lon_fwd_t, lon_inv_t)
+    spectra, block = lax.optimization_barrier((spectra, block))
     spectra = exchange(spectra)
     kept, grads = block_call(
         gradient_kernel,
         "spectral_grads",
         block,
         (spectra, lat, w_first, b_first, w_second),
-        ("", "", "weight", "", "weight"),
+        ("near",) * 5,
         [jax.ShapeDtypeStruct((2,) + WIDE, BF), jax.ShapeDtypeStruct((CHUNKS, CHUNK_ROWS, 128), BF)],
         ("far", "near"),
         [FORM, FORM, BAND_ROWS, BAND_ROWS, pltpu.VMEM(WIDE, BF), pltpu.VMEM(WIDE, BF)]
@@ -648,7 +637,7 @@
         "spectral_return",
         block,
         (kept, lat_t, w_first, w_second, b_second),
-        ("far", "", "weight", "weight", ""),
+        ("far",) + ("near",) * 4,
         [
             jax.ShapeDtypeStruct((BANDS, PACK, 128), BF),
             jax.ShapeDtypeStruct((BANDS, 96, 128), BF),

time: 127 us -> 125 us (0.984)
  blocking collectives: 41.4 us -> 84.2 us
  waiting for transfers between devices: 34.1 us -> 5.4 us
  starting transfers between devices: 29.1 us -> 14.9 us
    all_to_all x1 -> x2, blocking collectives: 23.3 us -> 66 us  [exchange(): return lax.all_to_all(value, 'lat', split_axis=0, concat_axis=0, tiled=True)]
    all_to_all x2 -> x1, waiting for transfers between devices: 29.7 us -> 1.08 us  [exchange(): return lax.all_to_all(value, 'lat', split_axis=0, concat_axis=0, tiled=True)]
    all_to_all x2 -> x1, starting transfers between devices: 18.9 us -> 5.06 us  [exchange(): return lax.all_to_all(value, 'lat', split_axis=0, concat_axis=0, tiled=True)]
  transfers between devices with their start and end apart: 3 -> 2, of which waited for: 3 -> 2; matrix products, arithmetic and copies ran while one was open for 0% -> 0% of each run, Pallas kernels for 5% -> 5%
where the time goes in v7:
time: 125 us; the launch traced here: 123 us
  blocking collectives  84.2 us (67%)
  Pallas kernels  18 us (14%)
  starting transfers between devices  14.9 us (12%)
  waiting for transfers between devices  5.4 us (4%)
    all_to_all x2, blocking collectives, exchange(): return lax.all_to_all(value, 'lat', split_axis=0, concat_axis=0, tiled=True)  66 us
    all_gather x1, blocking collectives, on_device(): every = lax.all_gather(blocks, 'dp', axis=0, tiled=False)  18.2 us
    all_to_all x1, starting transfers between devices, on_device(): shares = lax.all_to_all(grads, 'dp', 0, 0, tiled=True)  9.82 us
    pallas_call x2, Pallas kernels, block_call(): pl.pallas_call(kernel, name=name, grid_spec=pltpu.PrefetchScalarGridSpec(...  8.36 us
    all_to_all x1, starting transfers between devices, exchange(): return lax.all_to_all(value, 'lat', split_axis=0, concat_axis=0, tiled=True)  5.06 us
    all_to_all x1, waiting for transfers between devices, on_device(): shares = lax.all_to_all(grads, 'dp', 0, 0, tiled=True)  4.33 us
    pallas_call x1, Pallas kernels, to_spectra(): pl.pallas_call(spectra_kernel, name='to_spectra', in_specs=[held, held, h...  4.06 us
    pallas_call x1, Pallas kernels, from_spectra(): pl.pallas_call(output_kernel, name='from_spectra', grid=(ROWS,), in_specs...  4 us
  transfers between devices with their start and end apart: 2, of which 2 were waited for; matrix products, arithmetic and copies ran while one was open for 0% of the time, Pallas kernels for 5%

profile of v7, /device:TPU:1, one launch (start us, length us, event | category | flops | bytes accessed | tf_op | source)
XLA Modules:
  0.0 123.3 jit_solution(8166488046586615295)
XLA Ops:
  0.6 4.1 %to_spectra.1 = bf16[32,144,128]{2,1,0:T(8,128)(2,1)S(1)} custom-call(bf16[1,3,180,768]{3,2,1,0:T(8,128)(2,1)} %x_ref.3, bf16[1,3,180,768]{3,2,1,0:T(8,128)(2,1)} %g_ref.3, bf16[128,192]{1,0:T(8,128)(2,1)} %constant.34.clone.fwd_ref, bf16[128,192]{1,0:T(8,128)(2,1)} %constant.35.clone.inv_ref), custom_call_target="tpu_custom_call" | custom-call | flops 212336640 | bytes 3000000 | tf_op jit(solution)/shard_map/to_spectra/pallas_call | solution.py:168
  4.7 0.0 copy-start.4
  4.7 0.0 copy-start.5
  4.7 0.0 copy-start.6
  4.8 0.0 copy-start.9
  4.8 44.8 %all_to_all.20.recv_ref = bf16[32,144,128]{2,1,0:T(8,128)(2,1)S(1)} all-to-all(bf16[32,144,128]{2,1,0:T(8,128)(2,1)S(1)} %to_spectra.1), channel_id=1, replica_groups=mesh['dp'=16,'lat'=32] {'lat'}, dimensions={0} | all-to-all | bytes 2359296 | tf_op jit(solution)/shard_map/all_to_all | solution.py:602
  49.6 0.0 copy-start.7
  49.6 0.0 copy-start.8
  49.7 4.3 %spectral_grads.1 = (bf16[2,1536,256]{2,1,0:T(8,128)(2,1)}, bf16[16,24,128]{2,1,0:T(8,128)(2,1)}) custom-call(s32[1]{0:T(128)} %bitcast.block_ref, bf16[32,144,128]{2,1,0:T(8,128)(2,1)S(1)} %all_to_all.20.recv_ref, bf16[192,192]{1,0:T(8,128)(2,1)S(1)} %copy-done.9, bf16[2,8,96,96]{3,2,1,0:T(8,128)(2,1)S(1)} %copy-done.4, f32[2,768]{1,0:T(2,128)S(1)} %copy-done.6, ...), custom_call_target="tpu_custom_call" | custom-call | flops 1000000000 | bytes 6000000 | tf_op jit(solution)/shard_map/spectral_grads/pallas_call | solution.py:411
  53.9 9.8 %all-to-all-start.1 = ((bf16[16,24,128]{2,1,0:T(8,128)(2,1)}), bf16[16,24,128]{2,1,0:T(8,128)(2,1)S(1)}, u32[]{:S(2)}, u32[]{:S(2)}) async-start(bf16[16,24,128]{2,1,0:T(8,128)(2,1)} %get-tuple-element.24), calls=%async_computation.1 | async-start | bytes 196608 | tf_op jit(solution)/shard_map/all_to_all | solution.py:632
  63.7 0.0 copy-done.7
  63.8 4.1 %spectral_return.1 = (bf16[32,72,128]{2,1,0:T(8,128)(2,1)S(1)}, bf16[32,96,128]{2,1,0:T(8,128)(2,1)}) custom-call(s32[1]{0:T(128)} %bitcast.block_ref, bf16[2,1536,256]{2,1,0:T(8,128)(2,1)} %get-tuple-element.22.saved_ref, bf16[192,192]{1,0:T(8,128)(2,1)S(1)} %copy-done.8, bf16[2,8,96,96]{3,2,1,0:T(8,128)(2,1)S(1)} %copy-done.4, ...), custom_call_target="tpu_custom_call" | custom-call | flops 1000000000 | bytes 6000000 | tf_op jit(solution)/shard_map/spectral_return/pallas_call | solution.py:411
  67.9 4.3 %all-to-all-done.1.recv_ref = bf16[16,24,128]{2,1,0:T(8,128)(2,1)S(1)} async-done(((bf16[16,24,128]{2,1,0:T(8,128)(2,1)}), bf16[16,24,128]{2,1,0:T(8,128)(2,1)S(1)}, u32[]{:S(2)}, u32[]{:S(2)}) %all-to-all-start.1) | async-done | bytes 98336 | tf_op jit(solution)/shard_map/all_to_all | solution.py:632
  72.2 0.1 grad_share.1
  72.3 21.2 %all_to_all.21.early_ref.recv_ref = bf16[32,72,128]{2,1,0:T(8,128)(2,1)S(1)} all-to-all(bf16[32,72,128]{2,1,0:T(8,128)(2,1)S(1)} %grad_share.1), channel_id=1, replica_groups=mesh['dp'=16,'lat'=32] {'lat'}, dimensions={0} | all-to-all | bytes 1179648 | tf_op jit(solution)/shard_map/all_to_all | solution.py:602
  93.4 5.1 %all-to-all-start.3 = ((bf16[32,96,128]{2,1,0:T(8,128)(2,1)}), bf16[32,96,128]{2,1,0:T(8,128)(2,1)S(1)}, u32[]{:S(2)}, u32[]{:S(2)}) async-start(bf16[32,96,128]{2,1,0:T(8,128)(2,1)} %get-tuple-element.27), calls=%async_computation.3 | async-start | bytes 1572864 | tf_op jit(solution)/shard_map/all_to_all | solution.py:602
  98.5 0.0 copy-start
  98.5 0.0 copy-start.1
  98.5 0.0 copy-start.2
  98.5 0.0 copy-start.3
  98.6 18.2 %all-gather = bf16[128,24,128]{2,1,0:T(8,128)(2,1)S(1)} all-gather(bf16[8,24,128]{2,1,0:T(8,128)(2,1)S(1)} %grad_groups.1), channel_id=2, replica_groups=mesh['dp'=16,'lat'=32] {'dp'}, dimensions={0}, use_global_device_ids=true | all-gather | bytes 835584 | tf_op jit(solution)/shard_map/all_gather | solution.py:654
  116.7 1.5 %grad_out.1 = (f32[2,8,96,96]{3,2,1,0:T(8,128)}, f32[2,768]{1,0:T(2,128)}, f32[2,8,96,96]{3,2,1,0:T(8,128)}, f32[2,768]{1,0:T(2,128)}) custom-call(bf16[16,8,24,128]{3,2,1,0:T(8,128)(2,1)S(1)} %bitcast.2), custom_call_target="tpu_custom_call" | custom-call | flops 1000000 | bytes 1000000 | tf_op jit(solution)/shard_map/grad_out/pallas_call | solution.py:512
  118.2 1.1 all-to-all-done.3.late_ref
  119.3 4.0 %from_spectra.1 = (bf16[1,3,180,768]{3,2,1,0:T(8,128)(2,1)}, bf16[1,3,180,768]{3,2,1,0:T(8,128)(2,1)}) custom-call(bf16[32,72,128]{2,1,0:T(8,128)(2,1)S(1)} %all_to_all.21.early_ref.recv_ref, bf16[32,96,128]{2,1,0:T(8,128)(2,1)S(1)} %all-to-all-done.3.late_ref, bf16[1,3,180,768]{3,2,1,0:T(8,128)(2,1)S(1)} %copy-done, bf16[1,3,180,768]{3,2,1,0:T(8,128)(2,1)S(1)} %copy-done.1, ...), custom_call_target="tpu_custom_call" | custom-call | flops 212336640 | bytes 5000000 | tf_op jit(solution)/shard_map/from_spectra/pallas_call | solution.py:487
  (10 shorter events, 0.1 us)
Async XLA Ops:
  4.7 44.9 %copy-start.4 = (bf16[2,8,96,96]{3,2,1,0:T(8,128)(2,1)S(1)}, bf16[2,8,96,96]{3,2,1,0:T(8,128)(2,1)}, u32[]{:S(2)}) copy-start(bf16[2,8,96,96]{3,2,1,0:T(8,128)(2,1)} %first_ref.3) | copy-start | bytes 884740
  4.7 44.9 %copy-start.5 = (bf16[2,8,96,96]{3,2,1,0:T(8,128)(2,1)S(1)}, bf16[2,8,96,96]{3,2,1,0:T(8,128)(2,1)}, u32[]{:S(2)}) copy-start(bf16[2,8,96,96]{3,2,1,0:T(8,128)(2,1)} %second_ref.3) | copy-start | bytes 884740
  4.7 44.9 %copy-start.6 = (f32[2,768]{1,0:T(2,128)S(1)}, f32[2,768]{1,0:T(2,128)}, u32[]{:S(2)}) copy-start(f32[2,768]{1,0:T(2,128)} %bias_ref.2) | copy-start | bytes 18436
  4.8 44.9 %copy-start.9 = (bf16[192,192]{1,0:T(8,128)(2,1)S(1)}, bf16[192,192]{1,0:T(8,128)(2,1)}, u32[]{:S(2)}) copy-start(bf16[192,192]{1,0:T(8,128)(2,1)} %constant.36.clone.lat_ref) | copy-start | bytes 221188
  49.6 14.1 %copy-start.7 = (f32[2,768]{1,0:T(2,128)S(1)}, f32[2,768]{1,0:T(2,128)}, u32[]{:S(2)}) copy-start(f32[2,768]{1,0:T(2,128)} %bias_ref.3) | copy-start | bytes 18436
  49.6 14.1 %copy-start.8 = (bf16[192,192]{1,0:T(8,128)(2,1)S(1)}, bf16[192,192]{1,0:T(8,128)(2,1)}, u32[]{:S(2)}) copy-start(bf16[192,192]{1,0:T(8,128)(2,1)} %constant.37.clone.lat_ref) | copy-start | bytes 221188
  53.9 18.3 %all-to-all-start.1 = ((bf16[16,24,128]{2,1,0:T(8,128)(2,1)}), bf16[16,24,128]{2,1,0:T(8,128)(2,1)S(1)}, u32[]{:S(2)}, u32[]{:S(2)}) async-start(bf16[16,24,128]{2,1,0:T(8,128)(2,1)} %get-tuple-element.24), calls=%async_computation.1 | async-start | bytes 196608 | tf_op jit(solution)/shard_map/all_to_all | solution.py:632
  93.4 25.9 %all-to-all-start.3 = ((bf16[32,96,128]{2,1,0:T(8,128)(2,1)}), bf16[32,96,128]{2,1,0:T(8,128)(2,1)S(1)}, u32[]{:S(2)}, u32[]{:S(2)}) async-start(bf16[32,96,128]{2,1,0:T(8,128)(2,1)} %get-tuple-element.27), calls=%async_computation.3 | async-start | bytes 1572864 | tf_op jit(solution)/shard_map/all_to_all | solution.py:602
  98.5 20.8 %copy-start = (bf16[1,3,180,768]{3,2,1,0:T(8,128)(2,1)S(1)}, bf16[1,3,180,768]{3,2,1,0:T(8,128)(2,1)}, u32[]{:S(2)}) copy-start(bf16[1,3,180,768]{3,2,1,0:T(8,128)(2,1)} %x_ref.3) | copy-start | bytes 2488324
  98.5 20.8 %copy-start.1 = (bf16[1,3,180,768]{3,2,1,0:T(8,128)(2,1)S(1)}, bf16[1,3,180,768]{3,2,1,0:T(8,128)(2,1)}, u32[]{:S(2)}) copy-start(bf16[1,3,180,768]{3,2,1,0:T(8,128)(2,1)} %g_ref.3) | copy-start | bytes 2488324
  98.5 20.8 %copy-start.2 = (bf16[192,128]{1,0:T(8,128)(2,1)S(1)}, bf16[192,128]{1,0:T(8,128)(2,1)}, u32[]{:S(2)}) copy-start(bf16[192,128]{1,0:T(8,128)(2,1)} %constant.33.clone.inv_ref) | copy-start | bytes 147460
  98.5 20.8 %copy-start.3 = (bf16[192,128]{1,0:T(8,128)(2,1)S(1)}, bf16[192,128]{1,0:T(8,128)(2,1)}, u32[]{:S(2)}) copy-start(bf16[192,128]{1,0:T(8,128)(2,1)} %constant.32.clone.fwd_ref) | copy-start | bytes 147460
